TPU v7x, 1024 devices: a whole 4x8x16 slice. The times are simulated.
1024 devices in a mesh: coarse: 16 (over y, x_hi), fine: 64 (over x_lo, z, core).
Axes of the slice: x: 4 (x_hi: 2, x_lo: 2; x = x_hi * 2 + x_lo), y: 8, z: 16, core: 2. Of those that a mesh axis runs over, the one named last changes fastest.
Arguments:
- embeddings: bfloat16 [524288, 512], P(('coarse', 'fine')), may hold values from -64 to 64
- labels: int32 [524288, 1], P(('coarse', 'fine')), may hold values from 0 to 63; in each aligned block of 512 rows (0 to 511, 512 to 1023, ...) at most 16 rows name the same one
Outputs:
- max_similarity: float32 [524288], P(('coarse', 'fine'))
Inputs may be any that keep to these rules, and one draw needn't show every extreme that they name: `labels`: among the rows of one device no label appears more than 16 times; on some device one label appears exactly 16 times.
All inputs are finite; a program needn't handle non-finite values. Where the computation divides by a largest or mean magnitude, that divisor is 1e-20 or more.
Results may differ from a plain program's by a relative error of at most 0.00035.
The roundings to bfloat16 on the way count: a program that leaves them out, or rounds other values in their place, can miss the bound.
Values may be sent and summed in bfloat16 or wider, within the bound.
No kernel may reach another device: no remote copies, remote signals or barrier semaphores. Data moves between devices by JAX's collectives and lax.ppermute only.
A program may use at most 32 MiB of HBM per device.

v0:
```python
import math

import jax
import jax.numpy as jnp
from jax import lax
from jax.sharding import PartitionSpec as P

ITERS = 2


EPS = 1e-06
RIDGE = 0.001


def matmul_high(left, right):
    return jnp.dot(left, right, precision=lax.Precision.HIGHEST, preferred_element_type=jnp.float32)


def inverse_root(second):
    identity = jnp.eye(second.shape[0], dtype=jnp.float32)
    norm_scale = jnp.max(jnp.sum(jnp.abs(second), axis=1))
    root_est = second / norm_scale
    inverse_est = identity
    for sweep in range(ITERS):
        product = root_est if sweep == 0 else matmul_high(inverse_est, root_est)
        newton_step = 0.5 * (3.0 * identity - product)
        if sweep + 1 < ITERS:
            root_est = matmul_high(root_est, newton_step)
        inverse_est = newton_step if sweep == 0 else matmul_high(newton_step, inverse_est)
    return (inverse_est / jnp.sqrt(norm_scale)).astype(jnp.bfloat16)


def unit_rows(values, whiten_b):
    whitened = jnp.dot(values, whiten_b, preferred_element_type=jnp.float32)
    width_value = whitened.shape[-1]
    meansq = jnp.mean(whitened * whitened, axis=-1, keepdims=True)
    return (whitened * lax.rsqrt(width_value * (meansq + EPS))).astype(jnp.bfloat16)


def per_device(embeddings, labels):
    rows_here, feature_count = embeddings.shape
    fine_count = lax.axis_size("fine")
    slot_count = 2 * rows_here // fine_count
    row_total = rows_here * fine_count * lax.axis_size("coarse")
    partial_value = lax.dot_general(
        embeddings, embeddings, (((0,), (0,)), ((), ())), preferred_element_type=jnp.float32
    )
    second = lax.psum(partial_value, ("coarse", "fine"))
    second = second / row_total + RIDGE * jnp.eye(feature_count, dtype=jnp.float32)
    whiten_b = inverse_root(second)
    owner_label = labels[:, 0]
    onehot = (owner_label[:, None] == jnp.arange(fine_count, dtype=jnp.int32)).astype(jnp.int32)
    rank_before = jnp.cumsum(onehot, axis=0, dtype=jnp.int32) - onehot
    slot_index = jnp.sum(rank_before * onehot, axis=1)
    payload = unit_rows(embeddings, whiten_b)
    outgoing = (
        jnp.zeros((fine_count, slot_count, feature_count), jnp.bfloat16)
        .at[owner_label, slot_index]
        .set(payload)
    )
    slot_flags = (
        jnp.zeros((fine_count, slot_count), jnp.bfloat16).at[owner_label, slot_index].set(1.0)
    )
    received, received_flags = (
        lax.all_to_all(outgoing, "fine", split_axis=0, concat_axis=0, tiled=True),
        lax.all_to_all(slot_flags, "fine", split_axis=0, concat_axis=0, tiled=True),
    )
    slot_total = fine_count * slot_count
    received = received.reshape(slot_total, feature_count)
    unit_values = received
    valid_slots = received_flags.reshape(slot_total) > 0
    block_rows = math.gcd(slot_total, 512)

    def block_best(offset):
        queries = lax.dynamic_slice_in_dim(unit_values, offset, block_rows, 0)
        similar = lax.dot_general(
            queries, unit_values, (((1,), (1,)), ((), ())), preferred_element_type=jnp.float32
        )
        row_ids = offset + jnp.arange(block_rows, dtype=jnp.int32)[:, None]
        column_ids = jnp.arange(slot_total, dtype=jnp.int32)[None, :]
        keep_mask = valid_slots[None, :] & (row_ids != column_ids)
        return jnp.max(jnp.where(keep_mask, similar, -1.0), axis=1)

    offsets = jnp.arange(slot_total // block_rows, dtype=jnp.int32) * block_rows
    best_match = lax.map(block_best, offsets).reshape(fine_count, slot_count)
    returned = lax.all_to_all(best_match, "fine", split_axis=0, concat_axis=0, tiled=True)
    return returned[owner_label, slot_index]


def solution(mesh):
    in_specs = (P(("coarse", "fine"), None), P(("coarse", "fine"), None))
    out_specs = P(("coarse", "fine"))
    return jax.shard_map(
        per_device, mesh=mesh, in_specs=in_specs, out_specs=out_specs, check_vma=False
    )
```

profile of v0, /device:TPU:1, one launch (start us, length us, event | category | flops | bytes accessed | tf_op | source)
XLA Modules:
  0.0 687.8 jit_solution(9081461279622706136)
XLA Ops:
  6.5 0.0 copy-start
  6.5 0.0 all-reduce.2.cloned.1.call-start
  6.5 1.0 copy-done
  7.6 1.5 fusion.39
  9.1 0.0 copy-start.2
  9.1 0.0 all-reduce.2.cloned.1.call-update
  9.1 0.7 copy-done.2
  9.8 1.2 reduce-window.6
  11.0 0.2 slice_reduce_fusion
  11.3 0.1 fusion.23
  11.4 25.4 %scatter_fusion = bf16[64,16]{0,1:T(8,128)(2,1)S(1)} fusion(bf16[64,16]{0,1:T(8,128)(2,1)S(1)} %broadcast_in_dim.20, s32[512]{0:T(512)S(1)} %bitcast.47, bf16[512]{0:T(512)(128)(2,1)S(1)} %broadcast.139), kind=kCustom, calls=%fused_computation.1 | custom fusion | bytes 7168 | tf_op jit(solution)/shard_map/scatter | solution.py:62
  36.8 0.7 copy.8
  37.5 21.7 %all-to-all-start = ((bf16[64,1,16]{2,1,0:T(2,128)(2,1)}), bf16[64,1,16]{2,1,0:T(2,128)(2,1)S(1)}, u32[]{:S(2)}, u32[]{:S(2)}) async-start(bf16[64,1,16]{2,1,0:T(2,128)(2,1)} %copy.8), calls=%async_computation | async-start | bytes 65536 | tf_op jit(solution)/shard_map/all_to_all | solution.py:66
  59.3 445.8 %all-reduce.2.cloned.1.call-done = f32[512,512]{1,0:T(8,128)} async-done(((f32[512,512]{1,0:T(8,128)}), f32[512,512]{1,0:T(8,128)}) %all-reduce.2.cloned.1.call-update) | async-done | bytes 1048592 | tf_op jit(solution)/shard_map/psum | solution.py:48
  505.1 0.0 copy-start.1
  505.1 1.5 abs_reduce_fusion
  506.6 0.6 reduce_max.18
  507.9 0.0 copy-done.1
  507.9 2.7 fusion.8
  510.6 2.7 fusion.3
  513.3 2.6 fusion.4
  515.9 0.5 multiply_reduce_fusion
  516.4 0.1 fusion.11
  516.6 0.2 copy.9
  516.8 1.1 broadcast_in_dim.34
  517.9 64.3 %scatter_fusion.1 = bf16[64,16,512]{2,1,0:T(8,128)(2,1)} fusion(bf16[64,16,512]{2,1,0:T(8,128)(2,1)} %broadcast_in_dim.34, s32[512]{0:T(512)S(1)} %bitcast.48, bf16[512,512]{1,0:T(8,128)(2,1)S(1)} %copy.9), kind=kCustom, calls=%fused_computation.2 | custom fusion | bytes 1576960 | tf_op jit(solution)/shard_map/scatter | solution.py:59
  582.2 0.0 all-to-all-done
  582.2 10.7 %all-to-all-start.1 = ((bf16[64,16,512]{2,1,0:T(8,128)(2,1)}), bf16[64,16,512]{2,1,0:T(8,128)(2,1)S(1)}, u32[]{:S(2)}, u32[]{:S(2)}) async-start(bf16[64,16,512]{2,1,0:T(8,128)(2,1)} %scatter_fusion.1), calls=%async_computation.1 | async-start | bytes 2097152 | tf_op jit(solution)/shard_map/all_to_all | solution.py:65
  592.9 0.1 compare_reduce_fusion
  593.1 0.1 gt.11
  593.1 50.1 %all-to-all-done.1 = bf16[64,16,512]{2,1,0:T(8,128)(2,1)S(1)} async-done(((bf16[64,16,512]{2,1,0:T(8,128)(2,1)}), bf16[64,16,512]{2,1,0:T(8,128)(2,1)S(1)}, u32[]{:S(2)}, u32[]{:S(2)}) %all-to-all-start.1) | async-done | bytes 1048608 | tf_op jit(solution)/shard_map/all_to_all | solution.py:65
  643.3 8.9 %while.10 = (s32[]{:T(128)}, f32[2,512]{1,0:T(2,128)S(1)}, pred[1024]{0:T(1024)(128)(4,1)S(1)}, s32[2]{0:T(128)S(1)}, bf16[1024,512]{1,0:T(8,128)(2,1)S(1)}, /*index=5*/s32[]{:T(128)}, s32[]{:T(128)}, s32[]{:T(128)}) while((s32[]{:T(128)}, f32[2,512]{1,0:T(2,128)S(1)}, pred[1024]{0:T(1024)(128)(4,1)S(1)}, s32[2]{0:T(128)S(1)}, ...), condition=%wide.region_11.12_spmd, body=%wide.region_9.11_spmd.sunk | while | flops 538968064 | bytes 1584271 | solution.py:85
  643.3 0.7 dynamic_slice.12
  646.0 0.7 iota_add_fusion.2
  646.7 1.0 select_reduce_fusion.2
  647.7 0.7 dynamic_slice.12
  650.5 0.7 iota_add_fusion.2
  651.2 1.0 select_reduce_fusion.2
  652.2 0.1 all_to_all.20
  652.3 22.7 %all_to_all.26 = f32[64,1,16]{2,1,0:T(1,128)S(1)} all-to-all(f32[64,1,16]{2,1,0:T(1,128)S(1)} %bitcast.51), channel_id=1, replica_groups=mesh['coarse'=16,'fine'=64] {'fine'}, dimensions={0} | all-to-all | bytes 8192 | tf_op jit(solution)/shard_map/all_to_all | solution.py:86
  675.0 6.0 gather_fusion
  (11 shorter events, 0.2 us)
Async XLA Ops:
  6.5 1.0 copy-start
  6.5 498.5 %all-reduce.2.cloned.1.call-start = ((), (), s32[]{:S(2)}) async-start(), calls=%async_computation.3 | async-start | bytes 2097152 | tf_op jit(solution)/shard_map/psum | solution.py:48
  9.1 0.7 copy-start.2
  37.5 544.7 %all-to-all-start = ((bf16[64,1,16]{2,1,0:T(2,128)(2,1)}), bf16[64,1,16]{2,1,0:T(2,128)(2,1)S(1)}, u32[]{:S(2)}, u32[]{:S(2)}) async-start(bf16[64,1,16]{2,1,0:T(2,128)(2,1)} %copy.8), calls=%async_computation | async-start | bytes 65536 | tf_op jit(solution)/shard_map/all_to_all | solution.py:66
  505.1 2.8 copy-start.1
  582.2 61.1 %all-to-all-start.1 = ((bf16[64,16,512]{2,1,0:T(8,128)(2,1)}), bf16[64,16,512]{2,1,0:T(8,128)(2,1)S(1)}, u32[]{:S(2)}, u32[]{:S(2)}) async-start(bf16[64,16,512]{2,1,0:T(8,128)(2,1)} %scatter_fusion.1), calls=%async_computation.1 | async-start | bytes 2097152 | tf_op jit(solution)/shard_map/all_to_all | solution.py:65
Sparse Core Ops, SparseCore 0:
  12.8 492.1 all-reduce.1
where the time goes:
time: 690 us; the launch traced here: 688 us
  waiting for transfers between devices  496 us (72%)
  local copies, waits for them, and re-layouts  101 us (15%)
  starting transfers between devices  32.5 us (5%)
  blocking collectives  22.7 us (3%)
  between operations  14.2 us (2%)
  matrix products  12 us (2%)
    psum x1, waiting for transfers between devices, per_device(): second = lax.psum(partial_value, ('coarse', 'fine'))  446 us
    scatter x1, local copies, waits for them, and re-layouts, per_device(): outgoing = jnp.zeros((fine_count, slot_count, feature_count), jnp.bfloat1...  64.3 us
    all_to_all x1, waiting for transfers between devices, per_device(): lax.all_to_all(outgoing, 'fine', split_axis=0, concat_axis=0, tiled=True)  50.1 us
    scatter x1, local copies, waits for them, and re-layouts, per_device(): jnp.zeros((fine_count, slot_count), jnp.bfloat16)  25.4 us
    all_to_all x1, blocking collectives, per_device(): lax.all_to_all(best_match, 'fine', split_axis=0, concat_axis=0, tiled=True)  22.7 us
    all_to_all x1, starting transfers between devices, per_device(): lax.all_to_all(slot_flags, 'fine', split_axis=0, concat_axis=0, tiled=True)  21.7 us
  transfers between devices with their start and end apart: 3, of which 2 were waited for; matrix products, arithmetic and copies ran while one was open for 15% of the time, Pallas kernels for 0%

commit v1 on v0

v1 whole, which is shorter than its diff:
```python
import functools

import jax
import jax.numpy as jnp
from jax import lax
from jax.experimental import pallas as pl
from jax.experimental.pallas import tpu as pltpu
from jax.sharding import Mesh, PartitionSpec as P

ITERS = 2
EPS = 1e-06
RIDGE = 0.001

AXES = ("y", "xh", "xl", "z", "c")
SIZES = (8, 2, 2, 16, 2)
FINE = ("xl", "z", "c")
PLANE = ("y", "xh", "xl", "c")

D = 512
ROW_DEV = 512
ROWS = 524288
N_FINE = 64
N_PLANE = 64
N_Z = 16
CAP = 16
SLOTS = N_FINE * CAP
BLOCK = 128
BLOCKS = D // BLOCK
STRIP = 3 * BLOCK
STRIP_ROWS = D // N_PLANE

F32 = jnp.float32
BF16 = jnp.bfloat16


def iota(shape, dim):
    return lax.broadcasted_iota(jnp.int32, shape, dim)


def call(body, outs, flops, moved, scratch=(), name=None):
    return pl.pallas_call(
        body,
        out_shape=outs,
        scratch_shapes=scratch,
        name=name,
        compiler_params=pltpu.CompilerParams(vmem_limit_bytes=48 << 20),
        cost_estimate=pl.CostEstimate(flops=flops, bytes_accessed=moved, transcendentals=0),
    )


def gram_body(rows_ref, out_ref):
    rows = rows_ref[...]
    gram = lax.dot_general(rows, rows, (((0,), (0,)), ((), ())), preferred_element_type=F32)
    for b in range(BLOCKS):
        for k in range(3):
            c = (b + k) % BLOCKS
            out_ref[b * BLOCK:(b + 1) * BLOCK, k * BLOCK:(k + 1) * BLOCK] = gram[
                b * BLOCK:(b + 1) * BLOCK, c * BLOCK:(c + 1) * BLOCK
            ].astype(out_ref.dtype)


def pack_body(label_ref, rows_ref, out_ref, slot_ref):
    label = label_ref[...]
    onehot = (iota((N_FINE, ROW_DEV), 0) == label).astype(F32)
    earlier = (iota((ROW_DEV, ROW_DEV), 0) < iota((ROW_DEV, ROW_DEV), 1)).astype(BF16)
    rank = jnp.dot(onehot.astype(BF16), earlier, preferred_element_type=F32)
    slot = jnp.sum(onehot * rank, axis=0, keepdims=True).astype(jnp.int32)
    slot_ref[...] = slot
    place = label * CAP + slot
    chosen = (iota((SLOTS, ROW_DEV), 0) == place).astype(F32).astype(BF16)
    packed = jnp.dot(chosen, rows_ref[...], preferred_element_type=F32)
    filled = jnp.dot(chosen, jnp.ones((ROW_DEV, BLOCK), BF16), preferred_element_type=F32) > 0.5
    for k in range(D // BLOCK):
        part = packed[:, k * BLOCK:(k + 1) * BLOCK]
        out_ref[:, k * BLOCK:(k + 1) * BLOCK] = jnp.where(filled, part, jnp.nan).astype(BF16)


def high(left, right):
    return jnp.dot(left, right, precision=lax.Precision.HIGHEST, preferred_element_type=F32)


def root_body(strip_ref, out_ref, full_ref):
    for b in range(BLOCKS):
        for k in range(BLOCKS):
            c = (b + k) % BLOCKS
            if k < 3:
                piece = strip_ref[b * BLOCK:(b + 1) * BLOCK, k * BLOCK:(k + 1) * BLOCK]
            else:
                piece = strip_ref[c * BLOCK:(c + 1) * BLOCK, BLOCK:2 * BLOCK].T
            full_ref[b * BLOCK:(b + 1) * BLOCK, c * BLOCK:(c + 1) * BLOCK] = piece
    identity = (iota((D, D), 0) == iota((D, D), 1)).astype(F32)
    second = full_ref[...] / ROWS + RIDGE * identity
    norm_scale = jnp.max(jnp.sum(jnp.abs(second), axis=0, keepdims=True), axis=1, keepdims=True)
    root_est = second / norm_scale
    inverse_est = 0.5 * (3.0 * identity - root_est)
    root_est = high(root_est, inverse_est)
    newton_step = 0.5 * (3.0 * identity - high(inverse_est, root_est))
    inverse_est = high(newton_step, inverse_est)
    out_ref[...] = (inverse_est / jnp.sqrt(norm_scale)).astype(BF16)


def best_body(rows_ref, whiten_ref, out_ref):
    rows = rows_ref[...].astype(F32)
    present = rows == rows
    clean = jnp.where(present, rows, 0.0).astype(BF16)
    whitened = jnp.dot(clean, whiten_ref[...], preferred_element_type=F32)
    meansq = jnp.mean(whitened * whitened, axis=-1, keepdims=True)
    unit = (whitened * lax.rsqrt(D * (meansq + EPS))).astype(BF16)
    bias = jnp.where(present[:, :1], 0.0, -4.0)
    tile = 256
    best = jnp.full((1, SLOTS), -1.0, F32)
    for b in range(SLOTS // tile):
        lo = b * tile
        similar = lax.dot_general(
            unit[lo:lo + tile], unit, (((1,), (1,)), ((), ())), preferred_element_type=F32
        )
        similar = similar + bias[lo:lo + tile]
        similar = jnp.where(
            iota((tile, SLOTS), 0) + lo == iota((tile, SLOTS), 1), -1.0, similar
        )
        best = jnp.maximum(best, jnp.max(similar, axis=0, keepdims=True))
    spread = jnp.where(iota((N_FINE, SLOTS), 1) // CAP == iota((N_FINE, SLOTS), 0), best, 0.0)
    fold = (iota((SLOTS, CAP), 0) % CAP == iota((SLOTS, CAP), 1)).astype(F32)
    out_ref[...] = high(spread, fold)


def pick_body(label_ref, slot_ref, best_ref, out_ref):
    onehot = (iota((N_FINE, ROW_DEV), 0) == label_ref[...]).astype(F32)
    mine = lax.dot_general(
        best_ref[...], onehot, (((0,), (0,)), ((), ())),
        precision=lax.Precision.HIGHEST, preferred_element_type=F32,
    )
    chosen = iota((CAP, ROW_DEV), 0) == slot_ref[...]
    out_ref[...] = jnp.sum(jnp.where(chosen, mine, 0.0), axis=0, keepdims=True)


def swap(value, axes):
    return lax.all_to_all(value, axes, split_axis=0, concat_axis=0, tiled=True)


def per_device(embeddings, labels):
    label = labels.reshape(1, ROW_DEV)
    strips = call(
        gram_body, jax.ShapeDtypeStruct((D, STRIP), BF16), 2 * ROW_DEV * D * D, 1 << 20, name="gram"
    )(embeddings)
    parts = swap(strips.reshape(N_PLANE, STRIP_ROWS, STRIP), PLANE)

    outgoing, slot = call(
        pack_body,
        (
            jax.ShapeDtypeStruct((SLOTS, D), BF16),
            jax.ShapeDtypeStruct((1, ROW_DEV), jnp.int32),
        ),
        2 * SLOTS * ROW_DEV * D, 2 << 20, name="pack",
    )(label, embeddings)
    received = swap(outgoing.reshape(N_FINE, CAP, D), FINE).reshape(SLOTS, D)

    strip = jnp.sum(parts.astype(F32), axis=0)
    layers = swap(jnp.broadcast_to(strip, (N_Z, STRIP_ROWS, STRIP)), "z")
    strip = jnp.sum(layers, axis=0)
    whole = swap(jnp.broadcast_to(strip, (N_PLANE, STRIP_ROWS, STRIP)), PLANE).reshape(D, STRIP)
    whiten_b = call(
        root_body, jax.ShapeDtypeStruct((D, D), BF16), 36 * D * D * D, 2 << 20,
        (pltpu.VMEM((D, D), F32),), name="root",
    )(whole)

    best = call(
        best_body, jax.ShapeDtypeStruct((N_FINE, CAP), F32),
        2 * SLOTS * D * (D + SLOTS), 2 << 20, name="best",
    )(received, whiten_b)
    returned = swap(best.reshape(N_FINE, 1, CAP), FINE).reshape(N_FINE, CAP)
    picked = call(
        pick_body, jax.ShapeDtypeStruct((1, ROW_DEV), F32), 1 << 20, 1 << 16, name="pick"
    )(label, slot, returned)
    return picked.reshape(ROW_DEV)


def solution(mesh):
    fine = Mesh(mesh.devices.reshape(SIZES), AXES)
    return jax.shard_map(
        per_device,
        mesh=fine,
        in_specs=(P(AXES, None), P(AXES, None)),
        out_specs=P(AXES),
        check_vma=False,
    )
```

time: 690 us -> 176 us (0.26)
  waiting for transfers between devices: 496 us -> 65.2 us
  local copies, waits for them, and re-layouts: 101 us -> 2.03 us
  blocking collectives: 22.7 us -> 80.6 us
  starting transfers between devices: 32.5 us -> 16.6 us
  between operations: 14.2 us -> 0.07 us
  matrix products: 12 us -> 0 us
  Pallas kernels: 0 us -> 11.5 us
    psum x1 -> x0, waiting for transfers between devices: 446 us -> none  [per_device(): second = lax.psum(partial_value, ('coarse', 'fine'))]
    scatter x2 -> x0, local copies, waits for them, and re-layouts: 89.6 us -> none  [the longest x1 64.3 us: per_device(): outgoing = jnp.zeros((fine_count, slot_count, feature_count), jnp.bfloat1...]
    all_to_all x1 -> x3, blocking collectives: 22.7 us -> 80.6 us  [swap(): return lax.all_to_all(value, axes, split_axis=0, concat_axis=0, tiled=True)]
    all_to_all x2, starting transfers between devices: 32.5 us -> 16.6 us  [swap(): return lax.all_to_all(value, axes, split_axis=0, concat_axis=0, tiled=True)]
    all_to_all x2, waiting for transfers between devices: 50.1 us -> 65.2 us  [swap(): return lax.all_to_all(value, axes, split_axis=0, concat_axis=0, tiled=True)]
    dot_general x7 -> x0, matrix products: 12 us -> none  [the longest x3 7.99 us: matmul_high(): jnp.dot(left, right, precision=lax.Precision.HIGHEST, preferred_element_t...]
    pallas_call x0 -> x5, Pallas kernels: none -> 11.5 us  [the longest x1 5.72 us: per_device(): call(root_body, jax.ShapeDtypeStruct((D, D), BF16), 36 * D * D * D, 2 <<...]
  transfers between devices with their start and end apart: 3 -> 2, of which waited for: 2 -> 2; matrix products, arithmetic and copies ran while one was open for 15% -> 0% of each run, Pallas kernels for 0% -> 4%
where the time goes in v1:
time: 176 us
  blocking collectives  80.6 us (46%)
  waiting for transfers between devices  65.2 us (37%)
  starting transfers between devices  16.6 us (9%)
  Pallas kernels  11.5 us (7%)
  local copies, waits for them, and re-layouts  2.03 us (1%)
    all_to_all x3, blocking collectives, swap(): return lax.all_to_all(value, axes, split_axis=0, concat_axis=0, tiled=True)  80.6 us
    all_to_all x2, waiting for transfers between devices, swap(): return lax.all_to_all(value, axes, split_axis=0, concat_axis=0, tiled=True)  65.2 us
    all_to_all x2, starting transfers between devices, swap(): return lax.all_to_all(value, axes, split_axis=0, concat_axis=0, tiled=True)  16.6 us
    pallas_call x1, Pallas kernels, per_device(): call(root_body, jax.ShapeDtypeStruct((D, D), BF16), 36 * D * D * D, 2 <<...  5.72 us
  transfers between devices with their start and end apart: 2, of which 2 were waited for; matrix products, arithmetic and copies ran while one was open for 0% of the time, Pallas kernels for 4%

profile of v1, /device:TPU:1, one launch (start us, length us, event | category | flops | bytes accessed | tf_op | source)
XLA Modules:
  0.0 176.0 jit_solution(13931070952161903548)
XLA Ops:
  0.0 0.0 copy-start.1
  0.0 1.0 copy-done.1
  1.0 0.5 gram.1
  1.5 32.6 %all_to_all.25 = bf16[64,8,384]{2,1,0:T(8,128)(2,1)S(1)} all-to-all(bf16[64,8,384]{2,1,0:T(8,128)(2,1)S(1)} %bitcast.12), channel_id=1, replica_groups=mesh['y'=8,'xh'=2,'xl'=2,'z'=16,'c'=2] {'y','xh','xl','c'}, dimensions={0} | all-to-all | bytes 786432 | tf_op jit(solution)/shard_map/all_to_all | solution.py:138
  34.1 0.1 convert_reduce_fusion
  34.2 25.3 %all_to_all.26 = f32[16,8,384]{2,1,0:T(8,128)S(1)} all-to-all(f32[16,8,384]{2,1,0:T(8,128)S(1)} %broadcast_in_dim.6), channel_id=1, replica_groups=mesh['y'=8,'xh'=2,'xl'=2,'z'=16,'c'=2] {'z'}, dimensions={0} | all-to-all | bytes 393216 | tf_op jit(solution)/shard_map/all_to_all | solution.py:138
  59.5 1.0 broadcast_in_dim.7
  60.5 0.0 copy-start
  60.5 0.0 copy-start.2
  60.5 9.2 %all-to-all-start.3 = ((f32[64,8,384]{2,1,0:T(8,128)}), f32[64,8,384]{2,1,0:T(8,128)S(1)}, u32[]{:S(2)}, u32[]{:S(2)}) async-start(f32[64,8,384]{2,1,0:T(8,128)} %broadcast_in_dim.7), calls=%async_computation.3 | async-start | bytes 1572864 | tf_op jit(solution)/shard_map/all_to_all | solution.py:138
  69.7 0.0 copy-done
  69.7 0.0 copy-done.2
  69.7 2.2 %pack.1 = (bf16[1024,512]{1,0:T(8,128)(2,1)}, s32[1,512]{1,0:T(1,128)S(1)}) custom-call(s32[1,512]{1,0:T(1,128)S(1)} %bitcast.15, bf16[512,512]{1,0:T(8,128)(2,1)S(1)} %copy-done.2), custom_call_target="tpu_custom_call" | custom-call | flops 536870912 | bytes 2097152 | tf_op jit(solution)/shard_map/pack/pallas_call | solution.py:148
  71.9 20.6 %all-to-all-done.3 = f32[64,8,384]{2,1,0:T(8,128)S(1)} async-done(((f32[64,8,384]{2,1,0:T(8,128)}), f32[64,8,384]{2,1,0:T(8,128)S(1)}, u32[]{:S(2)}, u32[]{:S(2)}) %all-to-all-start.3) | async-done | bytes 786464 | tf_op jit(solution)/shard_map/all_to_all | solution.py:138
  92.4 7.4 %all-to-all-start = ((bf16[64,16,512]{2,1,0:T(8,128)(2,1)}), bf16[64,16,512]{2,1,0:T(8,128)(2,1)S(1)}, u32[]{:S(2)}, u32[]{:S(2)}) async-start(bf16[64,16,512]{2,1,0:T(8,128)(2,1)} %bitcast.1), calls=%async_computation | async-start | bytes 2097152 | tf_op jit(solution)/shard_map/all_to_all | solution.py:138
  99.9 5.7 %root.1.whiten_ref = bf16[512,512]{1,0:T(8,128)(2,1)S(1)} custom-call(f32[512,384]{1,0:T(8,128)S(1)} %bitcast.11), custom_call_target="tpu_custom_call" | custom-call | flops 4831838208 | bytes 2097152 | tf_op jit(solution)/shard_map/root/pallas_call | solution.py:162
  105.6 44.6 %all-to-all-done = bf16[64,16,512]{2,1,0:T(8,128)(2,1)S(1)} async-done(((bf16[64,16,512]{2,1,0:T(8,128)(2,1)}), bf16[64,16,512]{2,1,0:T(8,128)(2,1)S(1)}, u32[]{:S(2)}, u32[]{:S(2)}) %all-to-all-start) | async-done | bytes 1048608 | tf_op jit(solution)/shard_map/all_to_all | solution.py:138
  150.2 2.3 %best.1 = f32[64,16]{1,0:T(8,128)S(1)} custom-call(bf16[1024,512]{1,0:T(8,128)(2,1)S(1)} %bitcast.10, bf16[512,512]{1,0:T(8,128)(2,1)S(1)} %root.1.whiten_ref), custom_call_target="tpu_custom_call" | custom-call | flops 1610612736 | bytes 2097152 | tf_op jit(solution)/shard_map/best/pallas_call | solution.py:167
  152.5 22.7 %all_to_all.27 = f32[64,1,16]{2,1,0:T(1,128)S(1)} all-to-all(f32[64,1,16]{2,1,0:T(1,128)S(1)} %bitcast.14), channel_id=1, replica_groups=mesh['y'=8,'xh'=2,'xl'=2,'z'=16,'c'=2] {'xl','z','c'}, dimensions={0} | all-to-all | bytes 8192 | tf_op jit(solution)/shard_map/all_to_all | solution.py:138
  175.2 0.8 pick.1
  (2 shorter events, 0.0 us)
Async XLA Ops:
  0.0 1.0 copy-start.1
  60.5 9.2 %copy-start = (s32[512,1]{0,1:T(1,128)S(1)}, s32[512,1]{0,1:T(1,128)}, u32[]{:S(2)}) copy-start(s32[512,1]{0,1:T(1,128)} %param.3) | copy-start | bytes 6148
  60.5 9.2 %copy-start.2 = (bf16[512,512]{1,0:T(8,128)(2,1)S(1)}, bf16[512,512]{1,0:T(8,128)(2,1)}, u32[]{:S(2)}) copy-start(bf16[512,512]{1,0:T(8,128)(2,1)} %rows_ref.3) | copy-start | bytes 1572868
  60.5 31.9 %all-to-all-start.3 = ((f32[64,8,384]{2,1,0:T(8,128)}), f32[64,8,384]{2,1,0:T(8,128)S(1)}, u32[]{:S(2)}, u32[]{:S(2)}) async-start(f32[64,8,384]{2,1,0:T(8,128)} %broadcast_in_dim.7), calls=%async_computation.3 | async-start | bytes 1572864 | tf_op jit(solution)/shard_map/all_to_all | solution.py:138
  92.4 57.8 %all-to-all-start = ((bf16[64,16,512]{2,1,0:T(8,128)(2,1)}), bf16[64,16,512]{2,1,0:T(8,128)(2,1)S(1)}, u32[]{:S(2)}, u32[]{:S(2)}) async-start(bf16[64,16,512]{2,1,0:T(8,128)(2,1)} %bitcast.1), calls=%async_computation | async-start | bytes 2097152 | tf_op jit(solution)/shard_map/all_to_all | solution.py:138

commit v2 on v1

--- a/solution.py
+++ b/solution.py
@@ -28,6 +28,8 @@
 BLOCKS = D // BLOCK
 STRIP = 3 * BLOCK
 STRIP_ROWS = D // N_PLANE
+FIRST = (8, 7, 9, 1, 15, 2, 14)
+SECOND = (6, 10, 5, 11, 4, 12, 3, 13)
 
 F32 = jnp.float32
 BF16 = jnp.bfloat16
@@ -37,9 +39,14 @@
     return lax.broadcasted_iota(jnp.int32, shape, dim)
 
 
-def call(body, outs, flops, moved, scratch=(), name=None):
+VMEM = pl.BlockSpec(memory_space=pltpu.VMEM)
+SMEM = pl.BlockSpec(memory_space=pltpu.SMEM)
+
+
+def call(body, outs, flops, moved, scratch=(), name=None, specs=None):
     return pl.pallas_call(
         body,
+        **({} if specs is None else dict(in_specs=specs)),
         out_shape=outs,
         scratch_shapes=scratch,
         name=name,
@@ -59,20 +66,36 @@
             ].astype(out_ref.dtype)
 
 
-def pack_body(label_ref, rows_ref, out_ref, slot_ref):
+def split(index):
+    return index // (2 * N_Z), (index // 2) % N_Z, index % 2
+
+
+def pack_body(me_ref, label_ref, rows_ref, *refs):
+    outs, slot_ref = refs[:4], refs[4]
     label = label_ref[...]
     onehot = (iota((N_FINE, ROW_DEV), 0) == label).astype(F32)
     earlier = (iota((ROW_DEV, ROW_DEV), 0) < iota((ROW_DEV, ROW_DEV), 1)).astype(BF16)
     rank = jnp.dot(onehot.astype(BF16), earlier, preferred_element_type=F32)
     slot = jnp.sum(onehot * rank, axis=0, keepdims=True).astype(jnp.int32)
     slot_ref[...] = slot
-    place = label * CAP + slot
+    xl, z, c = split(me_ref[0])
+    to_xl, to_z, to_c = split(label)
+    block = (to_xl ^ xl) * 2 + (to_c ^ c)
+    place = (block * N_Z + ((to_z - z + N_Z) % N_Z)) * CAP + slot
     chosen = (iota((SLOTS, ROW_DEV), 0) == place).astype(F32).astype(BF16)
     packed = jnp.dot(chosen, rows_ref[...], preferred_element_type=F32)
     filled = jnp.dot(chosen, jnp.ones((ROW_DEV, BLOCK), BF16), preferred_element_type=F32) > 0.5
     for k in range(D // BLOCK):
         part = packed[:, k * BLOCK:(k + 1) * BLOCK]
-        out_ref[:, k * BLOCK:(k + 1) * BLOCK] = jnp.where(filled, part, jnp.nan).astype(BF16)
+        part = jnp.where(filled, part, jnp.nan).astype(BF16)
+        for e in range(4):
+            outs[e][:, k * BLOCK:(k + 1) * BLOCK] = part[e * N_Z * CAP:(e + 1) * N_Z * CAP]
+
+
+def turn_body(*refs):
+    for d in range(N_Z):
+        for e in range(4):
+            refs[4 + d][e * CAP:(e + 1) * CAP, :] = refs[e][d * CAP:(d + 1) * CAP, :]
 
 
 def high(left, right):
@@ -99,8 +122,9 @@
     out_ref[...] = (inverse_est / jnp.sqrt(norm_scale)).astype(BF16)
 
 
-def best_body(rows_ref, whiten_ref, out_ref):
-    rows = rows_ref[...].astype(F32)
+def best_body(me_ref, whiten_ref, *refs):
+    out_ref = refs[N_Z]
+    rows = jnp.concatenate([ref[...] for ref in refs[:N_Z]], axis=0).astype(F32)
     present = rows == rows
     clean = jnp.where(present, rows, 0.0).astype(BF16)
     whitened = jnp.dot(clean, whiten_ref[...], preferred_element_type=F32)
@@ -119,7 +143,11 @@
             iota((tile, SLOTS), 0) + lo == iota((tile, SLOTS), 1), -1.0, similar
         )
         best = jnp.maximum(best, jnp.max(similar, axis=0, keepdims=True))
-    spread = jnp.where(iota((N_FINE, SLOTS), 1) // CAP == iota((N_FINE, SLOTS), 0), best, 0.0)
+    xl, z, c = split(me_ref[0])
+    column = iota((1, SLOTS), 1) // CAP
+    block, step = column % 4, column // 4
+    source = ((xl ^ (block // 2)) * N_Z + ((z - step + N_Z) % N_Z)) * 2 + (c ^ (block % 2))
+    spread = jnp.where(source == iota((N_FINE, SLOTS), 0), best, 0.0)
     fold = (iota((SLOTS, CAP), 0) % CAP == iota((SLOTS, CAP), 1)).astype(F32)
     out_ref[...] = high(spread, fold)
 
@@ -145,20 +173,35 @@
     )(embeddings)
     parts = swap(strips.reshape(N_PLANE, STRIP_ROWS, STRIP), PLANE)
 
-    outgoing, slot = call(
+    me = lax.axis_index(FINE).reshape(1)
+    *blocks, slot = call(
         pack_body,
-        (
-            jax.ShapeDtypeStruct((SLOTS, D), BF16),
-            jax.ShapeDtypeStruct((1, ROW_DEV), jnp.int32),
-        ),
-        2 * SLOTS * ROW_DEV * D, 2 << 20, name="pack",
-    )(label, embeddings)
-    received = swap(outgoing.reshape(N_FINE, CAP, D), FINE).reshape(SLOTS, D)
+        (jax.ShapeDtypeStruct((N_Z * CAP, D), BF16),) * 4
+        + (jax.ShapeDtypeStruct((1, ROW_DEV), jnp.int32),),
+        2 * SLOTS * ROW_DEV * D, 2 << 20, name="pack", specs=(SMEM, VMEM, VMEM),
+    )(me, label, embeddings)
+    blocks = [
+        block if e == 0 else lax.ppermute(block, ("xl", "c"), [(i, i ^ e) for i in range(4)])
+        for e, block in enumerate(blocks)
+    ]
+    parts, *blocks = lax.optimization_barrier((parts, *blocks))
+    received = list(call(
+        turn_body, (jax.ShapeDtypeStruct((4 * CAP, D), BF16),) * N_Z, 0, 2 << 20, name="turn"
+    )(*blocks))
+
+    def send(steps):
+        for d in steps:
+            received[d] = lax.ppermute(received[d], "z", [(i, (i + d) % N_Z) for i in range(N_Z)])
 
     strip = jnp.sum(parts.astype(F32), axis=0)
     layers = swap(jnp.broadcast_to(strip, (N_Z, STRIP_ROWS, STRIP)), "z")
+    send(FIRST)
+    layers, *received = lax.optimization_barrier((layers, *received))
     strip = jnp.sum(layers, axis=0)
-    whole = swap(jnp.broadcast_to(strip, (N_PLANE, STRIP_ROWS, STRIP)), PLANE).reshape(D, STRIP)
+    whole = swap(jnp.broadcast_to(strip, (N_PLANE, STRIP_ROWS, STRIP)), PLANE)
+    send(SECOND)
+    whole, *received = lax.optimization_barrier((whole, *received))
+    whole = whole.reshape(D, STRIP)
     whiten_b = call(
         root_body, jax.ShapeDtypeStruct((D, D), BF16), 36 * D * D * D, 2 << 20,
         (pltpu.VMEM((D, D), F32),), name="root",
@@ -167,7 +210,8 @@
     best = call(
         best_body, jax.ShapeDtypeStruct((N_FINE, CAP), F32),
         2 * SLOTS * D * (D + SLOTS), 2 << 20, name="best",
-    )(received, whiten_b)
+        specs=(SMEM,) + (VMEM,) * (N_Z + 1),
+    )(me, whiten_b, *received)
     returned = swap(best.reshape(N_FINE, 1, CAP), FINE).reshape(N_FINE, CAP)
     picked = call(
         pick_body, jax.ShapeDtypeStruct((1, ROW_DEV), F32), 1 << 20, 1 << 16, name="pick"

time: 176 us -> 197 us (1.12)
  starting transfers between devices: 16.6 us -> 125 us
  blocking collectives: 80.6 us -> 24.7 us
  waiting for transfers between devices: 65.2 us -> 30.9 us
    ppermute x0 -> x18, starting transfers between devices: none -> 85.5 us  [the longest x15 77.5 us: send(): lax.ppermute(received[d], 'z', [(i, (i + d) % N_Z) for i in range(N_Z)])]
    all_to_all x2 -> x3, waiting for transfers between devices: 65.2 us -> 0.01 us  [swap(): return lax.all_to_all(value, axes, split_axis=0, concat_axis=0, tiled=True)]
    all_to_all x3 -> x1, blocking collectives: 80.6 us -> 24.7 us  [swap(): return lax.all_to_all(value, axes, split_axis=0, concat_axis=0, tiled=True)]
    ppermute x0 -> x18, waiting for transfers between devices: none -> 30.9 us  [the longest x15 19 us: send(): lax.ppermute(received[d], 'z', [(i, (i + d) % N_Z) for i in range(N_Z)])]
    all_to_all x2 -> x3, starting transfers between devices: 16.6 us -> 39.7 us  [swap(): return lax.all_to_all(value, axes, split_axis=0, concat_axis=0, tiled=True)]
  transfers between devices with their start and end apart: 2 -> 21, of which waited for: 2 -> 7; matrix products, arithmetic and copies ran while one was open for 0% -> 0% of each run, Pallas kernels for 4% -> 1%
where the time goes in v2:
time: 197 us; the launch traced here: 196 us
  starting transfers between devices  125 us (63%)
  waiting for transfers between devices  30.9 us (16%)
  blocking collectives  24.7 us (13%)
  Pallas kernels  11.4 us (6%)
  local copies, waits for them, and re-layouts  3.33 us (2%)
    ppermute x15, starting transfers between devices, send(): lax.ppermute(received[d], 'z', [(i, (i + d) % N_Z) for i in range(N_Z)])  77.5 us
    all_to_all x3, starting transfers between devices, swap(): return lax.all_to_all(value, axes, split_axis=0, concat_axis=0, tiled=True)  39.7 us
    all_to_all x1, blocking collectives, swap(): return lax.all_to_all(value, axes, split_axis=0, concat_axis=0, tiled=True)  24.7 us
    ppermute x15, waiting for transfers between devices, send(): lax.ppermute(received[d], 'z', [(i, (i + d) % N_Z) for i in range(N_Z)])  19 us
    ppermute x3, waiting for transfers between devices, per_device(): lax.ppermute(block, ('xl', 'c'), [(i, i ^ e) for i in range(4)])  11.9 us
    ppermute x3, starting transfers between devices, per_device(): lax.ppermute(block, ('xl', 'c'), [(i, i ^ e) for i in range(4)])  7.93 us
    pallas_call x1, Pallas kernels, per_device(): call(root_body, jax.ShapeDtypeStruct((D, D), BF16), 36 * D * D * D, 2 <<...  5.72 us
  transfers between devices with their start and end apart: 21, of which 7 were waited for; matrix products, arithmetic and copies ran while one was open for 0% of the time, Pallas kernels for 1%

profile of v2, /device:TPU:1, one launch (start us, length us, event | category | flops | bytes accessed | tf_op | source)
XLA Modules:
  0.0 195.9 jit_solution(17149744424300471330)
XLA Ops:
  0.0 1.0 copy-done.1
  1.0 1.2 gram.1
  2.3 18.3 %all-to-all-start = ((bf16[64,8,384]{2,1,0:T(8,128)(2,1)}), bf16[64,8,384]{2,1,0:T(8,128)(2,1)S(1)}, u32[]{:S(2)}, u32[]{:S(2)}) async-start(bf16[64,8,384]{2,1,0:T(8,128)(2,1)} %bitcast.2), calls=%async_computation | async-start | bytes 786432 | tf_op jit(solution)/shard_map/all_to_all | solution.py:166
  20.6 0.0 copy-start
  20.6 0.7 copy-done
  21.3 1.2 pack.1
  22.5 2.5 %collective-permute-start = (bf16[256,512]{1,0:T(8,128)(2,1)S(1)}, bf16[256,512]{1,0:T(8,128)(2,1)S(1)}, u32[]{:S(2)}, u32[]{:S(2)}) collective-permute-start(bf16[256,512]{1,0:T(8,128)(2,1)S(1)} %get-tuple-element.67), channel_id=1, source_target_pairs={{0,1},{1,0},{32,33},{33,32},{2,3},{3,2},{34,35},{35,34},{4,5},{5,4... | collective-permute-start | bytes 786440 | tf_op jit(solution)/shard_map/ppermute | solution.py:184
  25.0 3.1 %collective-permute-start.1 = (bf16[256,512]{1,0:T(8,128)(2,1)S(1)}, bf16[256,512]{1,0:T(8,128)(2,1)S(1)}, u32[]{:S(2)}, u32[]{:S(2)}) collective-permute-start(bf16[256,512]{1,0:T(8,128)(2,1)S(1)} %get-tuple-element.68), channel_id=1, source_target_pairs={{0,32},{1,33},{32,0},{33,1},{2,34},{3,35},{34,2},{35,3},{4,36},{5,... | collective-permute-start | bytes 786440 | tf_op jit(solution)/shard_map/ppermute | solution.py:184
  28.1 2.4 %collective-permute-start.2 = (bf16[256,512]{1,0:T(8,128)(2,1)S(1)}, bf16[256,512]{1,0:T(8,128)(2,1)S(1)}, u32[]{:S(2)}, u32[]{:S(2)}) collective-permute-start(bf16[256,512]{1,0:T(8,128)(2,1)S(1)} %get-tuple-element.69), channel_id=1, source_target_pairs={{0,33},{1,32},{32,1},{33,0},{2,35},{3,34},{34,3},{35,2},{4,37},{5,... | collective-permute-start | bytes 786440 | tf_op jit(solution)/shard_map/ppermute | solution.py:184
  30.5 0.0 collective-permute-done.refs_1_
  30.5 6.3 %collective-permute-done.1.refs_2_ = bf16[256,512]{1,0:T(8,128)(2,1)S(1)} collective-permute-done((bf16[256,512]{1,0:T(8,128)(2,1)S(1)}, bf16[256,512]{1,0:T(8,128)(2,1)S(1)}, u32[]{:S(2)}, u32[]{:S(2)}) %collective-permute-start.1) | collective-permute-done | bytes 262176 | tf_op jit(solution)/shard_map/ppermute | solution.py:184
  36.7 5.6 %collective-permute-done.2.refs_3_ = bf16[256,512]{1,0:T(8,128)(2,1)S(1)} collective-permute-done((bf16[256,512]{1,0:T(8,128)(2,1)S(1)}, bf16[256,512]{1,0:T(8,128)(2,1)S(1)}, u32[]{:S(2)}, u32[]{:S(2)}) %collective-permute-start.2) | collective-permute-done | bytes 262176 | tf_op jit(solution)/shard_map/ppermute | solution.py:184
  42.4 0.1 convert_reduce_fusion
  42.4 0.7 broadcast_in_dim.6
  43.1 11.8 %all-to-all-start.1 = ((f32[16,8,384]{2,1,0:T(8,128)}), f32[16,8,384]{2,1,0:T(8,128)S(1)}, u32[]{:S(2)}, u32[]{:S(2)}) async-start(f32[16,8,384]{2,1,0:T(8,128)} %broadcast_in_dim.6), calls=%async_computation.1 | async-start | bytes 393216 | tf_op jit(solution)/shard_map/all_to_all | solution.py:166
  55.0 0.1 turn.1
  55.0 3.3 %collective-permute-start.3 = (bf16[64,512]{1,0:T(8,128)(2,1)S(1)}, bf16[64,512]{1,0:T(8,128)(2,1)S(1)}, u32[]{:S(2)}, u32[]{:S(2)}) collective-permute-start(bf16[64,512]{1,0:T(8,128)(2,1)S(1)} %get-tuple-element.76), channel_id=1, source_target_pairs={{0,2},{2,4},{4,6},{6,8},{8,10},{10,12},{12,14},{14,16},{16,18},{18... | collective-permute-start | bytes 196616 | tf_op jit(solution)/shard_map/ppermute | solution.py:194
  58.3 4.0 %collective-permute-start.4 = (bf16[64,512]{1,0:T(8,128)(2,1)S(1)}, bf16[64,512]{1,0:T(8,128)(2,1)S(1)}, u32[]{:S(2)}, u32[]{:S(2)}) collective-permute-start(bf16[64,512]{1,0:T(8,128)(2,1)S(1)} %get-tuple-element.77), channel_id=1, source_target_pairs={{0,4},{2,6},{4,8},{6,10},{8,12},{10,14},{12,16},{14,18},{16,20},{1... | collective-permute-start | bytes 196616 | tf_op jit(solution)/shard_map/ppermute | solution.py:194
  62.3 9.1 %collective-permute-start.5 = (bf16[64,512]{1,0:T(8,128)(2,1)S(1)}, bf16[64,512]{1,0:T(8,128)(2,1)S(1)}, u32[]{:S(2)}, u32[]{:S(2)}) collective-permute-start(bf16[64,512]{1,0:T(8,128)(2,1)S(1)} %get-tuple-element.82), channel_id=1, source_target_pairs={{0,14},{2,16},{4,18},{6,20},{8,22},{10,24},{12,26},{14,28},{16,30}... | collective-permute-start | bytes 196616 | tf_op jit(solution)/shard_map/ppermute | solution.py:194
  71.4 4.0 %collective-permute-start.6 = (bf16[64,512]{1,0:T(8,128)(2,1)S(1)}, bf16[64,512]{1,0:T(8,128)(2,1)S(1)}, u32[]{:S(2)}, u32[]{:S(2)}) collective-permute-start(bf16[64,512]{1,0:T(8,128)(2,1)S(1)} %get-tuple-element.83), channel_id=1, source_target_pairs={{0,16},{2,18},{4,20},{6,22},{8,24},{10,26},{12,28},{14,30},{16,0},... | collective-permute-start | bytes 196616 | tf_op jit(solution)/shard_map/ppermute | solution.py:194
  75.4 9.1 %collective-permute-start.7 = (bf16[64,512]{1,0:T(8,128)(2,1)S(1)}, bf16[64,512]{1,0:T(8,128)(2,1)S(1)}, u32[]{:S(2)}, u32[]{:S(2)}) collective-permute-start(bf16[64,512]{1,0:T(8,128)(2,1)S(1)} %get-tuple-element.84), channel_id=1, source_target_pairs={{0,18},{2,20},{4,22},{6,24},{8,26},{10,28},{12,30},{14,0},{16,2},{... | collective-permute-start | bytes 196616 | tf_op jit(solution)/shard_map/ppermute | solution.py:194
  84.6 0.0 collective-permute-done.3.refs_1_
  84.6 5.2 %collective-permute-start.8 = (bf16[64,512]{1,0:T(8,128)(2,1)S(1)}, bf16[64,512]{1,0:T(8,128)(2,1)S(1)}, u32[]{:S(2)}, u32[]{:S(2)}) collective-permute-start(bf16[64,512]{1,0:T(8,128)(2,1)S(1)} %get-tuple-element.89), channel_id=1, source_target_pairs={{0,28},{2,30},{4,0},{6,2},{8,4},{10,6},{12,8},{14,10},{16,12},{18,... | collective-permute-start | bytes 196616 | tf_op jit(solution)/shard_map/ppermute | solution.py:194
  89.8 3.1 %collective-permute-start.9 = (bf16[64,512]{1,0:T(8,128)(2,1)S(1)}, bf16[64,512]{1,0:T(8,128)(2,1)S(1)}, u32[]{:S(2)}, u32[]{:S(2)}) collective-permute-start(bf16[64,512]{1,0:T(8,128)(2,1)S(1)} %get-tuple-element.90), channel_id=1, source_target_pairs={{0,30},{2,0},{4,2},{6,4},{8,6},{10,8},{12,10},{14,12},{16,14},{18,... | collective-permute-start | bytes 196616 | tf_op jit(solution)/shard_map/ppermute | solution.py:194
  92.9 1.6 collective-permute-done.6.refs_8_
  94.5 0.5 collective-permute-done.7.refs_9_
  95.0 5.7 %collective-permute-done.8.refs_14_ = bf16[64,512]{1,0:T(8,128)(2,1)S(1)} collective-permute-done((bf16[64,512]{1,0:T(8,128)(2,1)S(1)}, bf16[64,512]{1,0:T(8,128)(2,1)S(1)}, u32[]{:S(2)}, u32[]{:S(2)}) %collective-permute-start.8) | collective-permute-done | bytes 65568 | tf_op jit(solution)/shard_map/ppermute | solution.py:194
  100.7 0.0 collective-permute-done.9.refs_15_
  100.7 0.0 all-to-all-done.1
  100.7 0.9 broadcast_in_dim.7
  101.7 9.5 %all-to-all-start.2 = ((f32[64,8,384]{2,1,0:T(8,128)}), f32[64,8,384]{2,1,0:T(8,128)S(1)}, u32[]{:S(2)}, u32[]{:S(2)}) async-start(f32[64,8,384]{2,1,0:T(8,128)} %broadcast_in_dim.7), calls=%async_computation.2 | async-start | bytes 1572864 | tf_op jit(solution)/shard_map/all_to_all | solution.py:166
  111.2 4.6 %collective-permute-start.10 = (bf16[64,512]{1,0:T(8,128)(2,1)S(1)}, bf16[64,512]{1,0:T(8,128)(2,1)S(1)}, u32[]{:S(2)}, u32[]{:S(2)}) collective-permute-start(bf16[64,512]{1,0:T(8,128)(2,1)S(1)} %get-tuple-element.95), channel_id=1, source_target_pairs={{0,6},{2,8},{4,10},{6,12},{8,14},{10,16},{12,18},{14,20},{16,22},{... | collective-permute-start | bytes 196616 | tf_op jit(solution)/shard_map/ppermute | solution.py:194
  115.8 5.3 %collective-permute-start.11 = (bf16[64,512]{1,0:T(8,128)(2,1)S(1)}, bf16[64,512]{1,0:T(8,128)(2,1)S(1)}, u32[]{:S(2)}, u32[]{:S(2)}) collective-permute-start(bf16[64,512]{1,0:T(8,128)(2,1)S(1)} %get-tuple-element.96), channel_id=1, source_target_pairs={{0,8},{2,10},{4,12},{6,14},{8,16},{10,18},{12,20},{14,22},{16,24},... | collective-permute-start | bytes 196616 | tf_op jit(solution)/shard_map/ppermute | solution.py:194
  121.2 4.5 %collective-permute-start.12 = (bf16[64,512]{1,0:T(8,128)(2,1)S(1)}, bf16[64,512]{1,0:T(8,128)(2,1)S(1)}, u32[]{:S(2)}, u32[]{:S(2)}) collective-permute-start(bf16[64,512]{1,0:T(8,128)(2,1)S(1)} %get-tuple-element.97), channel_id=1, source_target_pairs={{0,10},{2,12},{4,14},{6,16},{8,18},{10,20},{12,22},{14,24},{16,26}... | collective-permute-start | bytes 196616 | tf_op jit(solution)/shard_map/ppermute | solution.py:194
  125.7 5.0 %collective-permute-start.13 = (bf16[64,512]{1,0:T(8,128)(2,1)S(1)}, bf16[64,512]{1,0:T(8,128)(2,1)S(1)}, u32[]{:S(2)}, u32[]{:S(2)}) collective-permute-start(bf16[64,512]{1,0:T(8,128)(2,1)S(1)} %get-tuple-element.98), channel_id=1, source_target_pairs={{0,12},{2,14},{4,16},{6,18},{8,20},{10,22},{12,24},{14,26},{16,28}... | collective-permute-start | bytes 196616 | tf_op jit(solution)/shard_map/ppermute | solution.py:194
  130.8 7.2 %collective-permute-start.14 = (bf16[64,512]{1,0:T(8,128)(2,1)S(1)}, bf16[64,512]{1,0:T(8,128)(2,1)S(1)}, u32[]{:S(2)}, u32[]{:S(2)}) collective-permute-start(bf16[64,512]{1,0:T(8,128)(2,1)S(1)} %get-tuple-element.102), channel_id=1, source_target_pairs={{0,20},{2,22},{4,24},{6,26},{8,28},{10,30},{12,0},{14,2},{16,4},{1... | collective-permute-start | bytes 196616 | tf_op jit(solution)/shard_map/ppermute | solution.py:194
  138.0 5.5 %collective-permute-start.15 = (bf16[64,512]{1,0:T(8,128)(2,1)S(1)}, bf16[64,512]{1,0:T(8,128)(2,1)S(1)}, u32[]{:S(2)}, u32[]{:S(2)}) collective-permute-start(bf16[64,512]{1,0:T(8,128)(2,1)S(1)} %get-tuple-element.103), channel_id=1, source_target_pairs={{0,22},{2,24},{4,26},{6,28},{8,30},{10,0},{12,2},{14,4},{16,6},{18... | collective-permute-start | bytes 196616 | tf_op jit(solution)/shard_map/ppermute | solution.py:194
  143.5 3.8 %collective-permute-start.16 = (bf16[64,512]{1,0:T(8,128)(2,1)S(1)}, bf16[64,512]{1,0:T(8,128)(2,1)S(1)}, u32[]{:S(2)}, u32[]{:S(2)}) collective-permute-start(bf16[64,512]{1,0:T(8,128)(2,1)S(1)} %get-tuple-element.104), channel_id=1, source_target_pairs={{0,24},{2,26},{4,28},{6,30},{8,0},{10,2},{12,4},{14,6},{16,8},{18,... | collective-permute-start | bytes 196616 | tf_op jit(solution)/shard_map/ppermute | solution.py:194
  147.4 0.0 collective-permute-done.12.refs_5_
  147.4 3.6 %collective-permute-start.17 = (bf16[64,512]{1,0:T(8,128)(2,1)S(1)}, bf16[64,512]{1,0:T(8,128)(2,1)S(1)}, u32[]{:S(2)}, u32[]{:S(2)}) collective-permute-start(bf16[64,512]{1,0:T(8,128)(2,1)S(1)} %get-tuple-element.105), channel_id=1, source_target_pairs={{0,26},{2,28},{4,30},{6,0},{8,2},{10,4},{12,6},{14,8},{16,10},{18,... | collective-permute-start | bytes 196616 | tf_op jit(solution)/shard_map/ppermute | solution.py:194
  151.0 0.0 collective-permute-done.13.refs_6_
  151.1 4.0 %collective-permute-done.15.refs_11_ = bf16[64,512]{1,0:T(8,128)(2,1)S(1)} collective-permute-done((bf16[64,512]{1,0:T(8,128)(2,1)S(1)}, bf16[64,512]{1,0:T(8,128)(2,1)S(1)}, u32[]{:S(2)}, u32[]{:S(2)}) %collective-permute-start.15) | collective-permute-done | bytes 65568 | tf_op jit(solution)/shard_map/ppermute | solution.py:194
  155.1 7.2 %collective-permute-done.16.refs_12_ = bf16[64,512]{1,0:T(8,128)(2,1)S(1)} collective-permute-done((bf16[64,512]{1,0:T(8,128)(2,1)S(1)}, bf16[64,512]{1,0:T(8,128)(2,1)S(1)}, u32[]{:S(2)}, u32[]{:S(2)}) %collective-permute-start.16) | collective-permute-done | bytes 65568 | tf_op jit(solution)/shard_map/ppermute | solution.py:194
  162.2 0.0 collective-permute-done.17.refs_13_
  162.3 5.7 %root.1.whiten_ref = bf16[512,512]{1,0:T(8,128)(2,1)S(1)} custom-call(f32[512,384]{1,0:T(8,128)S(1)} %bitcast.9), custom_call_target="tpu_custom_call" | custom-call | flops 4831838208 | bytes 2097152 | tf_op jit(solution)/shard_map/root/pallas_call | solution.py:205
  168.0 2.4 %best.1 = f32[64,16]{1,0:T(8,128)S(1)} custom-call(s32[1]{0:T(128)} %bitcast.1.me_ref, bf16[512,512]{1,0:T(8,128)(2,1)S(1)} %root.1.whiten_ref, bf16[64,512]{1,0:T(8,128)(2,1)S(1)} %get-tuple-element.109.refs_0_, bf16[64,512]{1,0:T(8,128)(2,1)S(1)} %collective-permute-done.3.refs_1_, bf16[64,512]{1,0:T(8,128)(2,1)S(1)} %collective-permute-done.4.refs_2_, ...), custom_call_target="tpu_custom_call" | custom-call | flops 1610612736 | bytes 2097152 | tf_op jit(solution)/shard_map/best/pallas_call | solution.py:210
  170.4 24.7 %all_to_all.20 = f32[64,1,16]{2,1,0:T(1,128)S(1)} all-to-all(f32[64,1,16]{2,1,0:T(1,128)S(1)} %bitcast.11), channel_id=1, replica_groups=mesh['y'=8,'xh'=2,'xl'=2,'z'=16,'c'=2] {'xl','z','c'}, dimensions={0} | all-to-all | bytes 8192 | tf_op jit(solution)/shard_map/all_to_all | solution.py:166
  195.1 0.8 pick.1
  (11 shorter events, 0.0 us)
Async XLA Ops:
  0.0 1.0 copy-start.1
  2.3 18.4 %copy-start.2 = (bf16[512,512]{1,0:T(8,128)(2,1)S(1)}, bf16[512,512]{1,0:T(8,128)(2,1)}, u32[]{:S(2)}) copy-start(bf16[512,512]{1,0:T(8,128)(2,1)} %rows_ref.3) | copy-start | bytes 1572868
  2.3 40.1 %all-to-all-start = ((bf16[64,8,384]{2,1,0:T(8,128)(2,1)}), bf16[64,8,384]{2,1,0:T(8,128)(2,1)S(1)}, u32[]{:S(2)}, u32[]{:S(2)}) async-start(bf16[64,8,384]{2,1,0:T(8,128)(2,1)} %bitcast.2), calls=%async_computation | async-start | bytes 786432 | tf_op jit(solution)/shard_map/all_to_all | solution.py:166
  20.6 0.7 copy-start
  22.5 8.0 %collective-permute-start = (bf16[256,512]{1,0:T(8,128)(2,1)S(1)}, bf16[256,512]{1,0:T(8,128)(2,1)S(1)}, u32[]{:S(2)}, u32[]{:S(2)}) collective-permute-start(bf16[256,512]{1,0:T(8,128)(2,1)S(1)} %get-tuple-element.67), channel_id=1, source_target_pairs={{0,1},{1,0},{32,33},{33,32},{2,3},{3,2},{34,35},{35,34},{4,5},{5,4... | collective-permute-start | bytes 786440 | tf_op jit(solution)/shard_map/ppermute | solution.py:184
  25.0 11.7 %collective-permute-start.1 = (bf16[256,512]{1,0:T(8,128)(2,1)S(1)}, bf16[256,512]{1,0:T(8,128)(2,1)S(1)}, u32[]{:S(2)}, u32[]{:S(2)}) collective-permute-start(bf16[256,512]{1,0:T(8,128)(2,1)S(1)} %get-tuple-element.68), channel_id=1, source_target_pairs={{0,32},{1,33},{32,0},{33,1},{2,34},{3,35},{34,2},{35,3},{4,36},{5,... | collective-permute-start | bytes 786440 | tf_op jit(solution)/shard_map/ppermute | solution.py:184
  28.1 14.3 %collective-permute-start.2 = (bf16[256,512]{1,0:T(8,128)(2,1)S(1)}, bf16[256,512]{1,0:T(8,128)(2,1)S(1)}, u32[]{:S(2)}, u32[]{:S(2)}) collective-permute-start(bf16[256,512]{1,0:T(8,128)(2,1)S(1)} %get-tuple-element.69), channel_id=1, source_target_pairs={{0,33},{1,32},{32,1},{33,0},{2,35},{3,34},{34,3},{35,2},{4,37},{5,... | collective-permute-start | bytes 786440 | tf_op jit(solution)/shard_map/ppermute | solution.py:184
  43.1 57.6 %all-to-all-start.1 = ((f32[16,8,384]{2,1,0:T(8,128)}), f32[16,8,384]{2,1,0:T(8,128)S(1)}, u32[]{:S(2)}, u32[]{:S(2)}) async-start(f32[16,8,384]{2,1,0:T(8,128)} %broadcast_in_dim.6), calls=%async_computation.1 | async-start | bytes 393216 | tf_op jit(solution)/shard_map/all_to_all | solution.py:166
  55.0 29.5 %collective-permute-start.3 = (bf16[64,512]{1,0:T(8,128)(2,1)S(1)}, bf16[64,512]{1,0:T(8,128)(2,1)S(1)}, u32[]{:S(2)}, u32[]{:S(2)}) collective-permute-start(bf16[64,512]{1,0:T(8,128)(2,1)S(1)} %get-tuple-element.76), channel_id=1, source_target_pairs={{0,2},{2,4},{4,6},{6,8},{8,10},{10,12},{12,14},{14,16},{16,18},{18... | collective-permute-start | bytes 196616 | tf_op jit(solution)/shard_map/ppermute | solution.py:194
  58.3 31.5 %collective-permute-start.4 = (bf16[64,512]{1,0:T(8,128)(2,1)S(1)}, bf16[64,512]{1,0:T(8,128)(2,1)S(1)}, u32[]{:S(2)}, u32[]{:S(2)}) collective-permute-start(bf16[64,512]{1,0:T(8,128)(2,1)S(1)} %get-tuple-element.77), channel_id=1, source_target_pairs={{0,4},{2,6},{4,8},{6,10},{8,12},{10,14},{12,16},{14,18},{16,20},{1... | collective-permute-start | bytes 196616 | tf_op jit(solution)/shard_map/ppermute | solution.py:194
  62.3 30.6 %collective-permute-start.5 = (bf16[64,512]{1,0:T(8,128)(2,1)S(1)}, bf16[64,512]{1,0:T(8,128)(2,1)S(1)}, u32[]{:S(2)}, u32[]{:S(2)}) collective-permute-start(bf16[64,512]{1,0:T(8,128)(2,1)S(1)} %get-tuple-element.82), channel_id=1, source_target_pairs={{0,14},{2,16},{4,18},{6,20},{8,22},{10,24},{12,26},{14,28},{16,30}... | collective-permute-start | bytes 196616 | tf_op jit(solution)/shard_map/ppermute | solution.py:194
  71.4 23.1 %collective-permute-start.6 = (bf16[64,512]{1,0:T(8,128)(2,1)S(1)}, bf16[64,512]{1,0:T(8,128)(2,1)S(1)}, u32[]{:S(2)}, u32[]{:S(2)}) collective-permute-start(bf16[64,512]{1,0:T(8,128)(2,1)S(1)} %get-tuple-element.83), channel_id=1, source_target_pairs={{0,16},{2,18},{4,20},{6,22},{8,24},{10,26},{12,28},{14,30},{16,0},... | collective-permute-start | bytes 196616 | tf_op jit(solution)/shard_map/ppermute | solution.py:194
  75.4 19.6 %collective-permute-start.7 = (bf16[64,512]{1,0:T(8,128)(2,1)S(1)}, bf16[64,512]{1,0:T(8,128)(2,1)S(1)}, u32[]{:S(2)}, u32[]{:S(2)}) collective-permute-start(bf16[64,512]{1,0:T(8,128)(2,1)S(1)} %get-tuple-element.84), channel_id=1, source_target_pairs={{0,18},{2,20},{4,22},{6,24},{8,26},{10,28},{12,30},{14,0},{16,2},{... | collective-permute-start | bytes 196616 | tf_op jit(solution)/shard_map/ppermute | solution.py:194
  84.6 16.1 %collective-permute-start.8 = (bf16[64,512]{1,0:T(8,128)(2,1)S(1)}, bf16[64,512]{1,0:T(8,128)(2,1)S(1)}, u32[]{:S(2)}, u32[]{:S(2)}) collective-permute-start(bf16[64,512]{1,0:T(8,128)(2,1)S(1)} %get-tuple-element.89), channel_id=1, source_target_pairs={{0,28},{2,30},{4,0},{6,2},{8,4},{10,6},{12,8},{14,10},{16,12},{18,... | collective-permute-start | bytes 196616 | tf_op jit(solution)/shard_map/ppermute | solution.py:194
  89.8 10.9 %collective-permute-start.9 = (bf16[64,512]{1,0:T(8,128)(2,1)S(1)}, bf16[64,512]{1,0:T(8,128)(2,1)S(1)}, u32[]{:S(2)}, u32[]{:S(2)}) collective-permute-start(bf16[64,512]{1,0:T(8,128)(2,1)S(1)} %get-tuple-element.90), channel_id=1, source_target_pairs={{0,30},{2,0},{4,2},{6,4},{8,6},{10,8},{12,10},{14,12},{16,14},{18,... | collective-permute-start | bytes 196616 | tf_op jit(solution)/shard_map/ppermute | solution.py:194
  101.7 60.6 %all-to-all-start.2 = ((f32[64,8,384]{2,1,0:T(8,128)}), f32[64,8,384]{2,1,0:T(8,128)S(1)}, u32[]{:S(2)}, u32[]{:S(2)}) async-start(f32[64,8,384]{2,1,0:T(8,128)} %broadcast_in_dim.7), calls=%async_computation.2 | async-start | bytes 1572864 | tf_op jit(solution)/shard_map/all_to_all | solution.py:166
  111.2 26.8 %collective-permute-start.10 = (bf16[64,512]{1,0:T(8,128)(2,1)S(1)}, bf16[64,512]{1,0:T(8,128)(2,1)S(1)}, u32[]{:S(2)}, u32[]{:S(2)}) collective-permute-start(bf16[64,512]{1,0:T(8,128)(2,1)S(1)} %get-tuple-element.95), channel_id=1, source_target_pairs={{0,6},{2,8},{4,10},{6,12},{8,14},{10,16},{12,18},{14,20},{16,22},{... | collective-permute-start | bytes 196616 | tf_op jit(solution)/shard_map/ppermute | solution.py:194
  115.8 27.7 %collective-permute-start.11 = (bf16[64,512]{1,0:T(8,128)(2,1)S(1)}, bf16[64,512]{1,0:T(8,128)(2,1)S(1)}, u32[]{:S(2)}, u32[]{:S(2)}) collective-permute-start(bf16[64,512]{1,0:T(8,128)(2,1)S(1)} %get-tuple-element.96), channel_id=1, source_target_pairs={{0,8},{2,10},{4,12},{6,14},{8,16},{10,18},{12,20},{14,22},{16,24},... | collective-permute-start | bytes 196616 | tf_op jit(solution)/shard_map/ppermute | solution.py:194
  121.2 26.2 %collective-permute-start.12 = (bf16[64,512]{1,0:T(8,128)(2,1)S(1)}, bf16[64,512]{1,0:T(8,128)(2,1)S(1)}, u32[]{:S(2)}, u32[]{:S(2)}) collective-permute-start(bf16[64,512]{1,0:T(8,128)(2,1)S(1)} %get-tuple-element.97), channel_id=1, source_target_pairs={{0,10},{2,12},{4,14},{6,16},{8,18},{10,20},{12,22},{14,24},{16,26}... | collective-permute-start | bytes 196616 | tf_op jit(solution)/shard_map/ppermute | solution.py:194
  125.7 25.3 %collective-permute-start.13 = (bf16[64,512]{1,0:T(8,128)(2,1)S(1)}, bf16[64,512]{1,0:T(8,128)(2,1)S(1)}, u32[]{:S(2)}, u32[]{:S(2)}) collective-permute-start(bf16[64,512]{1,0:T(8,128)(2,1)S(1)} %get-tuple-element.98), channel_id=1, source_target_pairs={{0,12},{2,14},{4,16},{6,18},{8,20},{10,22},{12,24},{14,26},{16,28}... | collective-permute-start | bytes 196616 | tf_op jit(solution)/shard_map/ppermute | solution.py:194
  130.8 20.3 %collective-permute-start.14 = (bf16[64,512]{1,0:T(8,128)(2,1)S(1)}, bf16[64,512]{1,0:T(8,128)(2,1)S(1)}, u32[]{:S(2)}, u32[]{:S(2)}) collective-permute-start(bf16[64,512]{1,0:T(8,128)(2,1)S(1)} %get-tuple-element.102), channel_id=1, source_target_pairs={{0,20},{2,22},{4,24},{6,26},{8,28},{10,30},{12,0},{14,2},{16,4},{1... | collective-permute-start | bytes 196616 | tf_op jit(solution)/shard_map/ppermute | solution.py:194
  138.0 17.1 %collective-permute-start.15 = (bf16[64,512]{1,0:T(8,128)(2,1)S(1)}, bf16[64,512]{1,0:T(8,128)(2,1)S(1)}, u32[]{:S(2)}, u32[]{:S(2)}) collective-permute-start(bf16[64,512]{1,0:T(8,128)(2,1)S(1)} %get-tuple-element.103), channel_id=1, source_target_pairs={{0,22},{2,24},{4,26},{6,28},{8,30},{10,0},{12,2},{14,4},{16,6},{18... | collective-permute-start | bytes 196616 | tf_op jit(solution)/shard_map/ppermute | solution.py:194
  143.5 18.7 %collective-permute-start.16 = (bf16[64,512]{1,0:T(8,128)(2,1)S(1)}, bf16[64,512]{1,0:T(8,128)(2,1)S(1)}, u32[]{:S(2)}, u32[]{:S(2)}) collective-permute-start(bf16[64,512]{1,0:T(8,128)(2,1)S(1)} %get-tuple-element.104), channel_id=1, source_target_pairs={{0,24},{2,26},{4,28},{6,30},{8,0},{10,2},{12,4},{14,6},{16,8},{18,... | collective-permute-start | bytes 196616 | tf_op jit(solution)/shard_map/ppermute | solution.py:194
  147.4 14.9 %collective-permute-start.17 = (bf16[64,512]{1,0:T(8,128)(2,1)S(1)}, bf16[64,512]{1,0:T(8,128)(2,1)S(1)}, u32[]{:S(2)}, u32[]{:S(2)}) collective-permute-start(bf16[64,512]{1,0:T(8,128)(2,1)S(1)} %get-tuple-element.105), channel_id=1, source_target_pairs={{0,26},{2,28},{4,30},{6,0},{8,2},{10,4},{12,6},{14,8},{16,10},{18,... | collective-permute-start | bytes 196616 | tf_op jit(solution)/shard_map/ppermute | solution.py:194

commit v3 on v1

--- a/solution.py
+++ b/solution.py
@@ -156,8 +156,9 @@
     received = swap(outgoing.reshape(N_FINE, CAP, D), FINE).reshape(SLOTS, D)
 
     strip = jnp.sum(parts.astype(F32), axis=0)
-    layers = swap(jnp.broadcast_to(strip, (N_Z, STRIP_ROWS, STRIP)), "z")
-    strip = jnp.sum(layers, axis=0)
+    for step in (1, 2, 4, 8):
+        strip = strip + lax.ppermute(strip, "z", [(i, i ^ step) for i in range(N_Z)])
+    strip, received = lax.optimization_barrier((strip, received))
     whole = swap(jnp.broadcast_to(strip, (N_PLANE, STRIP_ROWS, STRIP)), PLANE).reshape(D, STRIP)
     whiten_b = call(
         root_body, jax.ShapeDtypeStruct((D, D), BF16), 36 * D * D * D, 2 << 20,

time: 176 us -> 191 us (1.085)
  starting transfers between devices: 16.6 us -> 57.5 us
  blocking collectives: 80.6 us -> 59.3 us
  waiting for transfers between devices: 65.2 us -> 60.7 us
    all_to_all x2, waiting for transfers between devices: 65.2 us -> 13 us  [swap(): return lax.all_to_all(value, axes, split_axis=0, concat_axis=0, tiled=True)]
    ppermute x0 -> x4, waiting for transfers between devices: none -> 47.7 us  [per_device(): lax.ppermute(strip, 'z', [(i, i ^ step) for i in range(N_Z)])]
    ppermute x0 -> x4, starting transfers between devices: none -> 25.4 us  [per_device(): lax.ppermute(strip, 'z', [(i, i ^ step) for i in range(N_Z)])]
    all_to_all x3 -> x2, blocking collectives: 80.6 us -> 59.3 us  [swap(): return lax.all_to_all(value, axes, split_axis=0, concat_axis=0, tiled=True)]
    all_to_all x2, starting transfers between devices: 16.6 us -> 32.1 us  [swap(): return lax.all_to_all(value, axes, split_axis=0, concat_axis=0, tiled=True)]
  transfers between devices with their start and end apart: 2 -> 6, of which waited for: 2 -> 5; matrix products, arithmetic and copies ran while one was open for 0% -> 0% of each run, Pallas kernels for 4% -> 1%
where the time goes in v3:
time: 191 us
  waiting for transfers between devices  60.7 us (32%)
  blocking collectives  59.3 us (31%)
  starting transfers between devices  57.5 us (30%)
  Pallas kernels  12.2 us (6%)
    all_to_all x2, blocking collectives, swap(): return lax.all_to_all(value, axes, split_axis=0, concat_axis=0, tiled=True)  59.3 us
    ppermute x4, waiting for transfers between devices, per_device(): lax.ppermute(strip, 'z', [(i, i ^ step) for i in range(N_Z)])  47.7 us
    all_to_all x2, starting transfers between devices, swap(): return lax.all_to_all(value, axes, split_axis=0, concat_axis=0, tiled=True)  32.1 us
    ppermute x4, starting transfers between devices, per_device(): lax.ppermute(strip, 'z', [(i, i ^ step) for i in range(N_Z)])  25.4 us
    all_to_all x2, waiting for transfers between devices, swap(): return lax.all_to_all(value, axes, split_axis=0, concat_axis=0, tiled=True)  13 us
    pallas_call x1, Pallas kernels, per_device(): call(root_body, jax.ShapeDtypeStruct((D, D), BF16), 36 * D * D * D, 2 <<...  5.72 us
  transfers between devices with their start and end apart: 6, of which 5 were waited for; matrix products, arithmetic and copies ran while one was open for 0% of the time, Pallas kernels for 1%

profile of v3, /device:TPU:1, one launch (start us, length us, event | category | flops | bytes accessed | tf_op | source)
XLA Modules:
  0.0 191.0 jit_solution(3466701612639642327)
XLA Ops:
  0.0 0.0 copy-start.1
  0.0 1.0 copy-done.1
  1.0 1.2 gram.1
  2.3 0.0 copy-start.2
  2.3 0.0 copy-start
  2.3 18.3 %all-to-all-start = ((bf16[64,8,384]{2,1,0:T(8,128)(2,1)}), bf16[64,8,384]{2,1,0:T(8,128)(2,1)S(1)}, u32[]{:S(2)}, u32[]{:S(2)}) async-start(bf16[64,8,384]{2,1,0:T(8,128)(2,1)} %bitcast.1), calls=%async_computation | async-start | bytes 786432 | tf_op jit(solution)/shard_map/all_to_all | solution.py:138
  20.6 0.0 copy-done.2
  20.6 0.0 copy-done
  20.7 2.2 %pack.1 = (bf16[1024,512]{1,0:T(8,128)(2,1)}, s32[1,512]{1,0:T(1,128)S(1)}) custom-call(s32[1,512]{1,0:T(1,128)S(1)} %bitcast.14, bf16[512,512]{1,0:T(8,128)(2,1)S(1)} %copy-done.2), custom_call_target="tpu_custom_call" | custom-call | flops 536870912 | bytes 2097152 | tf_op jit(solution)/shard_map/pack/pallas_call | solution.py:148
  22.8 13.0 %all-to-all-done = bf16[64,8,384]{2,1,0:T(8,128)(2,1)S(1)} async-done(((bf16[64,8,384]{2,1,0:T(8,128)(2,1)}), bf16[64,8,384]{2,1,0:T(8,128)(2,1)S(1)}, u32[]{:S(2)}, u32[]{:S(2)}) %all-to-all-start) | async-done | bytes 393248 | tf_op jit(solution)/shard_map/all_to_all | solution.py:138
  35.8 13.8 %all-to-all-start.1 = ((bf16[64,16,512]{2,1,0:T(8,128)(2,1)}), bf16[64,16,512]{2,1,0:T(8,128)(2,1)S(1)}, u32[]{:S(2)}, u32[]{:S(2)}) async-start(bf16[64,16,512]{2,1,0:T(8,128)(2,1)} %bitcast.2), calls=%async_computation.1 | async-start | bytes 2097152 | tf_op jit(solution)/shard_map/all_to_all | solution.py:138
  49.6 0.1 convert_reduce_fusion
  49.7 3.3 %collective-permute-start = (f32[8,384]{1,0:T(8,128)S(1)}, f32[8,384]{1,0:T(8,128)S(1)}, u32[]{:S(2)}, u32[]{:S(2)}) collective-permute-start(f32[8,384]{1,0:T(8,128)S(1)} %convert_reduce_fusion), channel_id=1, source_target_pairs={{0,2},{2,0},{4,6},{6,4},{8,10},{10,8},{12,14},{14,12},{16,18},{18,... | collective-permute-start | bytes 36872 | tf_op jit(solution)/shard_map/ppermute | solution.py:160
  53.0 42.4 %collective-permute-done = f32[8,384]{1,0:T(8,128)S(1)} collective-permute-done((f32[8,384]{1,0:T(8,128)S(1)}, f32[8,384]{1,0:T(8,128)S(1)}, u32[]{:S(2)}, u32[]{:S(2)}) %collective-permute-start) | collective-permute-done | bytes 12320 | tf_op jit(solution)/shard_map/ppermute | solution.py:160
  95.4 2.8 %collective-permute-start.1 = (f32[8,384]{1,0:T(8,128)S(1)}, f32[8,384]{1,0:T(8,128)S(1)}, u32[]{:S(2)}, u32[]{:S(2)}) collective-permute-start(f32[8,384]{1,0:T(8,128)S(1)} %add.12), channel_id=1, source_target_pairs={{0,4},{2,6},{4,0},{6,2},{8,12},{10,14},{12,8},{14,10},{16,20},{18,... | collective-permute-start | bytes 36872 | tf_op jit(solution)/shard_map/ppermute | solution.py:160
  98.2 2.8 %collective-permute-done.1 = f32[8,384]{1,0:T(8,128)S(1)} collective-permute-done((f32[8,384]{1,0:T(8,128)S(1)}, f32[8,384]{1,0:T(8,128)S(1)}, u32[]{:S(2)}, u32[]{:S(2)}) %collective-permute-start.1) | collective-permute-done | bytes 12320 | tf_op jit(solution)/shard_map/ppermute | solution.py:160
  101.0 6.9 %collective-permute-start.2 = (f32[8,384]{1,0:T(8,128)S(1)}, f32[8,384]{1,0:T(8,128)S(1)}, u32[]{:S(2)}, u32[]{:S(2)}) collective-permute-start(f32[8,384]{1,0:T(8,128)S(1)} %add.13), channel_id=1, source_target_pairs={{0,8},{2,10},{4,12},{6,14},{8,0},{10,2},{12,4},{14,6},{16,24},{18,... | collective-permute-start | bytes 36872 | tf_op jit(solution)/shard_map/ppermute | solution.py:160
  107.9 1.4 collective-permute-done.2
  109.4 12.4 %collective-permute-start.3 = (f32[8,384]{1,0:T(8,128)S(1)}, f32[8,384]{1,0:T(8,128)S(1)}, u32[]{:S(2)}, u32[]{:S(2)}) collective-permute-start(f32[8,384]{1,0:T(8,128)S(1)} %add.14), channel_id=1, source_target_pairs={{0,16},{2,18},{4,20},{6,22},{8,24},{10,26},{12,28},{14,30},{16,0},... | collective-permute-start | bytes 36872 | tf_op jit(solution)/shard_map/ppermute | solution.py:160
  121.7 1.1 collective-permute-done.3
  122.8 0.0 all-to-all-done.1
  122.8 0.1 broadcast_in_dim.3
  122.9 32.1 %all_to_all.20 = f32[64,8,384]{2,1,0:T(8,128)S(1)} all-to-all(f32[64,8,384]{2,1,0:T(8,128)S(1)} %broadcast_in_dim.3), channel_id=1, replica_groups=mesh['y'=8,'xh'=2,'xl'=2,'z'=16,'c'=2] {'y','xh','xl','c'}, dimensions={0} | all-to-all | bytes 1572864 | tf_op jit(solution)/shard_map/all_to_all | solution.py:138
  155.0 5.7 %root.1.whiten_ref = bf16[512,512]{1,0:T(8,128)(2,1)S(1)} custom-call(f32[512,384]{1,0:T(8,128)S(1)} %bitcast.11), custom_call_target="tpu_custom_call" | custom-call | flops 4831838208 | bytes 2097152 | tf_op jit(solution)/shard_map/root/pallas_call | solution.py:163
  160.7 2.3 %best.1 = f32[64,16]{1,0:T(8,128)S(1)} custom-call(bf16[1024,512]{1,0:T(8,128)(2,1)S(1)} %bitcast.10, bf16[512,512]{1,0:T(8,128)(2,1)S(1)} %root.1.whiten_ref), custom_call_target="tpu_custom_call" | custom-call | flops 1610612736 | bytes 2097152 | tf_op jit(solution)/shard_map/best/pallas_call | solution.py:168
  163.0 27.2 %all_to_all.21 = f32[64,1,16]{2,1,0:T(1,128)S(1)} all-to-all(f32[64,1,16]{2,1,0:T(1,128)S(1)} %bitcast.13), channel_id=1, replica_groups=mesh['y'=8,'xh'=2,'xl'=2,'z'=16,'c'=2] {'xl','z','c'}, dimensions={0} | all-to-all | bytes 8192 | tf_op jit(solution)/shard_map/all_to_all | solution.py:138
  190.1 0.8 pick.1
  (4 shorter events, 0.0 us)
Async XLA Ops:
  0.0 1.0 copy-start.1
  2.3 18.4 %copy-start.2 = (bf16[512,512]{1,0:T(8,128)(2,1)S(1)}, bf16[512,512]{1,0:T(8,128)(2,1)}, u32[]{:S(2)}) copy-start(bf16[512,512]{1,0:T(8,128)(2,1)} %rows_ref.3) | copy-start | bytes 1572868
  2.3 18.4 %copy-start = (s32[512,1]{0,1:T(1,128)S(1)}, s32[512,1]{0,1:T(1,128)}, u32[]{:S(2)}) copy-start(s32[512,1]{0,1:T(1,128)} %param.3) | copy-start | bytes 6148
  2.3 33.5 %all-to-all-start = ((bf16[64,8,384]{2,1,0:T(8,128)(2,1)}), bf16[64,8,384]{2,1,0:T(8,128)(2,1)S(1)}, u32[]{:S(2)}, u32[]{:S(2)}) async-start(bf16[64,8,384]{2,1,0:T(8,128)(2,1)} %bitcast.1), calls=%async_computation | async-start | bytes 786432 | tf_op jit(solution)/shard_map/all_to_all | solution.py:138
  35.8 87.0 %all-to-all-start.1 = ((bf16[64,16,512]{2,1,0:T(8,128)(2,1)}), bf16[64,16,512]{2,1,0:T(8,128)(2,1)S(1)}, u32[]{:S(2)}, u32[]{:S(2)}) async-start(bf16[64,16,512]{2,1,0:T(8,128)(2,1)} %bitcast.2), calls=%async_computation.1 | async-start | bytes 2097152 | tf_op jit(solution)/shard_map/all_to_all | solution.py:138
  49.7 45.7 %collective-permute-start = (f32[8,384]{1,0:T(8,128)S(1)}, f32[8,384]{1,0:T(8,128)S(1)}, u32[]{:S(2)}, u32[]{:S(2)}) collective-permute-start(f32[8,384]{1,0:T(8,128)S(1)} %convert_reduce_fusion), channel_id=1, source_target_pairs={{0,2},{2,0},{4,6},{6,4},{8,10},{10,8},{12,14},{14,12},{16,18},{18,... | collective-permute-start | bytes 36872 | tf_op jit(solution)/shard_map/ppermute | solution.py:160
  95.4 5.6 %collective-permute-start.1 = (f32[8,384]{1,0:T(8,128)S(1)}, f32[8,384]{1,0:T(8,128)S(1)}, u32[]{:S(2)}, u32[]{:S(2)}) collective-permute-start(f32[8,384]{1,0:T(8,128)S(1)} %add.12), channel_id=1, source_target_pairs={{0,4},{2,6},{4,0},{6,2},{8,12},{10,14},{12,8},{14,10},{16,20},{18,... | collective-permute-start | bytes 36872 | tf_op jit(solution)/shard_map/ppermute | solution.py:160
  101.0 8.3 %collective-permute-start.2 = (f32[8,384]{1,0:T(8,128)S(1)}, f32[8,384]{1,0:T(8,128)S(1)}, u32[]{:S(2)}, u32[]{:S(2)}) collective-permute-start(f32[8,384]{1,0:T(8,128)S(1)} %add.13), channel_id=1, source_target_pairs={{0,8},{2,10},{4,12},{6,14},{8,0},{10,2},{12,4},{14,6},{16,24},{18,... | collective-permute-start | bytes 36872 | tf_op jit(solution)/shard_map/ppermute | solution.py:160
  109.4 13.4 %collective-permute-start.3 = (f32[8,384]{1,0:T(8,128)S(1)}, f32[8,384]{1,0:T(8,128)S(1)}, u32[]{:S(2)}, u32[]{:S(2)}) collective-permute-start(f32[8,384]{1,0:T(8,128)S(1)} %add.14), channel_id=1, source_target_pairs={{0,16},{2,18},{4,20},{6,22},{8,24},{10,26},{12,28},{14,30},{16,0},... | collective-permute-start | bytes 36872 | tf_op jit(solution)/shard_map/ppermute | solution.py:160

commit v4 on v1

--- a/solution.py
+++ b/solution.py
@@ -1,4 +1,4 @@
-import functools
+import math
 
 import jax
 import jax.numpy as jnp
@@ -28,6 +28,14 @@
 BLOCKS = D // BLOCK
 STRIP = 3 * BLOCK
 STRIP_ROWS = D // N_PLANE
+DOUBLING = (
+    (("y",), 1, 8),
+    (("y",), 2, 16),
+    (("y",), 4, 32),
+    (("xh", "xl"), 3, 6),
+    (("xl",), 1, 2),
+    (("c",), 1, 1),
+)
 
 F32 = jnp.float32
 BF16 = jnp.bfloat16
@@ -37,9 +45,14 @@
     return lax.broadcasted_iota(jnp.int32, shape, dim)
 
 
-def call(body, outs, flops, moved, scratch=(), name=None):
+VMEM = pl.BlockSpec(memory_space=pltpu.VMEM)
+SMEM = pl.BlockSpec(memory_space=pltpu.SMEM)
+
+
+def call(body, outs, flops, moved, scratch=(), name=None, specs=None):
     return pl.pallas_call(
         body,
+        **({} if specs is None else dict(in_specs=specs)),
         out_shape=outs,
         scratch_shapes=scratch,
         name=name,
@@ -79,7 +92,16 @@
     return jnp.dot(left, right, precision=lax.Precision.HIGHEST, preferred_element_type=F32)
 
 
-def root_body(strip_ref, out_ref, full_ref):
+def root_body(me_ref, near_ref, far_ref, out_ref, strip_ref, full_ref):
+    half = N_PLANE // 2
+    for k in range(N_PLANE):
+        differs = 0
+        for bit, (_, _, mask) in enumerate(DOUBLING):
+            if k >> bit & 1:
+                differs ^= mask
+        source, at = (near_ref, k) if k < half else (far_ref, k - half)
+        to = pl.multiple_of((me_ref[0] ^ differs) * STRIP_ROWS, STRIP_ROWS)
+        strip_ref[pl.ds(to, STRIP_ROWS), :] = source[at * STRIP_ROWS:(at + 1) * STRIP_ROWS, :]
     for b in range(BLOCKS):
         for k in range(BLOCKS):
             c = (b + k) % BLOCKS
@@ -158,11 +180,15 @@
     strip = jnp.sum(parts.astype(F32), axis=0)
     layers = swap(jnp.broadcast_to(strip, (N_Z, STRIP_ROWS, STRIP)), "z")
     strip = jnp.sum(layers, axis=0)
-    whole = swap(jnp.broadcast_to(strip, (N_PLANE, STRIP_ROWS, STRIP)), PLANE).reshape(D, STRIP)
+    for axes, differs, _ in DOUBLING:
+        size = math.prod(SIZES[AXES.index(axis)] for axis in axes)
+        other = lax.ppermute(strip, axes, [(i, i ^ differs) for i in range(size)])
+        near, strip = strip, jnp.concatenate([strip, other], axis=0)
     whiten_b = call(
         root_body, jax.ShapeDtypeStruct((D, D), BF16), 36 * D * D * D, 2 << 20,
-        (pltpu.VMEM((D, D), F32),), name="root",
-    )(whole)
+        (pltpu.VMEM((D, STRIP), F32), pltpu.VMEM((D, D), F32)), name="root",
+        specs=(SMEM, VMEM, VMEM),
+    )(lax.axis_index(PLANE).reshape(1), near, other)
 
     best = call(
         best_body, jax.ShapeDtypeStruct((N_FINE, CAP), F32),

time: 176 us -> 148 us (0.84)
  waiting for transfers between devices: 65.2 us -> 34.4 us
  starting transfers between devices: 16.6 us -> 44 us
  blocking collectives: 80.6 us -> 55.3 us
    all_to_all x2, waiting for transfers between devices: 65.2 us -> 13.7 us  [swap(): return lax.all_to_all(value, axes, split_axis=0, concat_axis=0, tiled=True)]
    all_to_all x3 -> x2, blocking collectives: 80.6 us -> 55.3 us  [swap(): return lax.all_to_all(value, axes, split_axis=0, concat_axis=0, tiled=True)]
    ppermute x0 -> x6, starting transfers between devices: none -> 20.8 us  [per_device(): other = lax.ppermute(strip, axes, [(i, i ^ differs) for i in range(size)])]
    ppermute x0 -> x6, waiting for transfers between devices: none -> 20.7 us  [per_device(): other = lax.ppermute(strip, axes, [(i, i ^ differs) for i in range(size)])]
    all_to_all x2, starting transfers between devices: 16.6 us -> 23.2 us  [swap(): return lax.all_to_all(value, axes, split_axis=0, concat_axis=0, tiled=True)]
  transfers between devices with their start and end apart: 2 -> 8, of which waited for: 2 -> 8; matrix products, arithmetic and copies ran while one was open for 0% -> 0% of each run, Pallas kernels for 4% -> 5%
where the time goes in v4:
time: 148 us; the launch traced here: 147 us
  blocking collectives  55.3 us (37%)
  starting transfers between devices  44 us (30%)
  waiting for transfers between devices  34.4 us (23%)
  Pallas kernels  11.5 us (8%)
  local copies, waits for them, and re-layouts  1.8 us (1%)
    all_to_all x2, blocking collectives, swap(): return lax.all_to_all(value, axes, split_axis=0, concat_axis=0, tiled=True)  55.3 us
    all_to_all x2, starting transfers between devices, swap(): return lax.all_to_all(value, axes, split_axis=0, concat_axis=0, tiled=True)  23.2 us
    ppermute x6, starting transfers between devices, per_device(): other = lax.ppermute(strip, axes, [(i, i ^ differs) for i in range(size)])  20.8 us
    ppermute x6, waiting for transfers between devices, per_device(): other = lax.ppermute(strip, axes, [(i, i ^ differs) for i in range(size)])  20.7 us
    all_to_all x2, waiting for transfers between devices, swap(): return lax.all_to_all(value, axes, split_axis=0, concat_axis=0, tiled=True)  13.7 us
    pallas_call x1, Pallas kernels, per_device(): call(root_body, jax.ShapeDtypeStruct((D, D), BF16), 36 * D * D * D, 2 <<...  5.8 us
  transfers between devices with their start and end apart: 8, of which 8 were waited for; matrix products, arithmetic and copies ran while one was open for 0% of the time, Pallas kernels for 5%

profile of v4, /device:TPU:1, one launch (start us, length us, event | category | flops | bytes accessed | tf_op | source)
XLA Modules:
  0.0 147.3 jit_solution(1816275397465210599)
XLA Ops:
  0.0 0.0 copy-start.1
  0.0 1.0 copy-done.1
  1.0 0.5 gram.1
  1.5 32.6 %all_to_all.20 = bf16[64,8,384]{2,1,0:T(8,128)(2,1)S(1)} all-to-all(bf16[64,8,384]{2,1,0:T(8,128)(2,1)S(1)} %bitcast.11), channel_id=1, replica_groups=mesh['y'=8,'xh'=2,'xl'=2,'z'=16,'c'=2] {'y','xh','xl','c'}, dimensions={0} | all-to-all | bytes 786432 | tf_op jit(solution)/shard_map/all_to_all | solution.py:160
  34.1 0.0 copy-start.2
  34.1 0.1 convert_reduce_fusion
  34.2 0.7 broadcast_in_dim.3
  34.9 0.0 copy-start
  34.9 12.6 %all-to-all-start.2 = ((f32[16,8,384]{2,1,0:T(8,128)}), f32[16,8,384]{2,1,0:T(8,128)S(1)}, u32[]{:S(2)}, u32[]{:S(2)}) async-start(f32[16,8,384]{2,1,0:T(8,128)} %broadcast_in_dim.3), calls=%async_computation.2 | async-start | bytes 393216 | tf_op jit(solution)/shard_map/all_to_all | solution.py:160
  47.5 0.0 copy-done.2
  47.5 0.0 copy-done
  47.5 2.2 %pack.1 = (bf16[1024,512]{1,0:T(8,128)(2,1)}, s32[1,512]{1,0:T(1,128)S(1)}) custom-call(s32[1,512]{1,0:T(1,128)S(1)} %bitcast.14, bf16[512,512]{1,0:T(8,128)(2,1)S(1)} %copy-done.2), custom_call_target="tpu_custom_call" | custom-call | flops 536870912 | bytes 2097152 | tf_op jit(solution)/shard_map/pack/pallas_call | solution.py:170
  49.7 10.8 %all-to-all-done.2 = f32[16,8,384]{2,1,0:T(8,128)S(1)} async-done(((f32[16,8,384]{2,1,0:T(8,128)}), f32[16,8,384]{2,1,0:T(8,128)S(1)}, u32[]{:S(2)}, u32[]{:S(2)}) %all-to-all-start.2) | async-done | bytes 196640 | tf_op jit(solution)/shard_map/all_to_all | solution.py:160
  60.5 10.6 %all-to-all-start = ((bf16[64,16,512]{2,1,0:T(8,128)(2,1)}), bf16[64,16,512]{2,1,0:T(8,128)(2,1)S(1)}, u32[]{:S(2)}, u32[]{:S(2)}) async-start(bf16[64,16,512]{2,1,0:T(8,128)(2,1)} %bitcast.1), calls=%async_computation | async-start | bytes 2097152 | tf_op jit(solution)/shard_map/all_to_all | solution.py:160
  71.1 2.6 %collective-permute-start = (f32[8,384]{1,0:T(8,128)S(1)}, f32[8,384]{1,0:T(8,128)S(1)}, u32[]{:S(2)}, u32[]{:S(2)}) collective-permute-start(f32[8,384]{1,0:T(8,128)S(1)} %reduce_sum.19), channel_id=1, source_target_pairs={{0,128},{128,0},{256,384},{384,256},{512,640},{640,512},{768,896},... | collective-permute-start | bytes 36872 | tf_op jit(solution)/shard_map/ppermute | solution.py:185
  73.7 2.1 %collective-permute-done = f32[8,384]{1,0:T(8,128)S(1)} collective-permute-done((f32[8,384]{1,0:T(8,128)S(1)}, f32[8,384]{1,0:T(8,128)S(1)}, u32[]{:S(2)}, u32[]{:S(2)}) %collective-permute-start) | collective-permute-done | bytes 12320 | tf_op jit(solution)/shard_map/ppermute | solution.py:185
  75.9 2.5 %collective-permute-start.1 = (f32[16,384]{1,0:T(8,128)S(1)}, f32[16,384]{1,0:T(8,128)S(1)}, u32[]{:S(2)}, u32[]{:S(2)}) collective-permute-start(f32[16,384]{1,0:T(8,128)S(1)} %pad_maximum_fusion.2), channel_id=1, source_target_pairs={{0,256},{128,384},{256,0},{384,128},{512,768},{640,896},{768,512},... | collective-permute-start | bytes 73736 | tf_op jit(solution)/shard_map/ppermute | solution.py:185
  78.4 3.2 %collective-permute-done.1 = f32[16,384]{1,0:T(8,128)S(1)} collective-permute-done((f32[16,384]{1,0:T(8,128)S(1)}, f32[16,384]{1,0:T(8,128)S(1)}, u32[]{:S(2)}, u32[]{:S(2)}) %collective-permute-start.1) | collective-permute-done | bytes 24608 | tf_op jit(solution)/shard_map/ppermute | solution.py:185
  81.6 2.8 %collective-permute-start.2 = (f32[32,384]{1,0:T(8,128)S(1)}, f32[32,384]{1,0:T(8,128)S(1)}, u32[]{:S(2)}, u32[]{:S(2)}) collective-permute-start(f32[32,384]{1,0:T(8,128)S(1)} %pad_maximum_fusion.1), channel_id=1, source_target_pairs={{0,512},{128,640},{256,768},{384,896},{512,0},{640,128},{768,256},... | collective-permute-start | bytes 147464 | tf_op jit(solution)/shard_map/ppermute | solution.py:185
  84.5 5.9 %collective-permute-done.2 = f32[32,384]{1,0:T(8,128)S(1)} collective-permute-done((f32[32,384]{1,0:T(8,128)S(1)}, f32[32,384]{1,0:T(8,128)S(1)}, u32[]{:S(2)}, u32[]{:S(2)}) %collective-permute-start.2) | collective-permute-done | bytes 49184 | tf_op jit(solution)/shard_map/ppermute | solution.py:185
  90.4 3.7 %collective-permute-start.3 = (f32[64,384]{1,0:T(8,128)S(1)}, f32[64,384]{1,0:T(8,128)S(1)}, u32[]{:S(2)}, u32[]{:S(2)}) collective-permute-start(f32[64,384]{1,0:T(8,128)S(1)} %pad_maximum_fusion), channel_id=1, source_target_pairs={{0,96},{32,64},{64,32},{96,0},{1,97},{33,65},{65,33},{97,1},{2,98}... | collective-permute-start | bytes 294920 | tf_op jit(solution)/shard_map/ppermute | solution.py:185
  94.0 3.2 %collective-permute-done.3 = f32[64,384]{1,0:T(8,128)S(1)} collective-permute-done((f32[64,384]{1,0:T(8,128)S(1)}, f32[64,384]{1,0:T(8,128)S(1)}, u32[]{:S(2)}, u32[]{:S(2)}) %collective-permute-start.3) | collective-permute-done | bytes 98336 | tf_op jit(solution)/shard_map/ppermute | solution.py:185
  97.2 2.5 %collective-permute-start.4 = (f32[128,384]{1,0:T(8,128)S(1)}, f32[128,384]{1,0:T(8,128)S(1)}, u32[]{:S(2)}, u32[]{:S(2)}) collective-permute-start(f32[128,384]{1,0:T(8,128)S(1)} %get-tuple-element.9), channel_id=1, source_target_pairs={{0,32},{32,0},{1,33},{33,1},{2,34},{34,2},{3,35},{35,3},{4,36},{36... | collective-permute-start | bytes 589832 | tf_op jit(solution)/shard_map/ppermute | solution.py:185
  99.7 5.0 %collective-permute-done.4 = f32[128,384]{1,0:T(8,128)S(1)} collective-permute-done((f32[128,384]{1,0:T(8,128)S(1)}, f32[128,384]{1,0:T(8,128)S(1)}, u32[]{:S(2)}, u32[]{:S(2)}) %collective-permute-start.4) | collective-permute-done | bytes 196640 | tf_op jit(solution)/shard_map/ppermute | solution.py:185
  104.7 6.7 %collective-permute-start.5 = (f32[256,384]{1,0:T(8,128)S(1)}, f32[256,384]{1,0:T(8,128)S(1)}, u32[]{:S(2)}, u32[]{:S(2)}) collective-permute-start(f32[256,384]{1,0:T(8,128)S(1)} %constant_dynamic-update-slice_fusion.5.near_ref), channel_id=1, source_target_pairs={{0,1},{1,0},{2,3},{3,2},{4,5},{5,4},{6,7},{7,6},{8,9},{9,8},{10,11... | collective-permute-start | bytes 1179656 | tf_op jit(solution)/shard_map/ppermute | solution.py:185
  111.5 1.3 collective-permute-done.5.far_ref
  112.8 5.8 %root.1.whiten_ref = bf16[512,512]{1,0:T(8,128)(2,1)S(1)} custom-call(s32[1]{0:T(128)} %bitcast.3.me_ref, f32[256,384]{1,0:T(8,128)S(1)} %constant_dynamic-update-slice_fusion.5.near_ref, f32[256,384]{1,0:T(8,128)S(1)} %collective-permute-done.5.far_ref), custom_call_target="tpu_custom_call" | custom-call | flops 4831838208 | bytes 2097152 | tf_op jit(solution)/shard_map/root/pallas_call | solution.py:187
  118.6 2.8 %all-to-all-done = bf16[64,16,512]{2,1,0:T(8,128)(2,1)S(1)} async-done(((bf16[64,16,512]{2,1,0:T(8,128)(2,1)}), bf16[64,16,512]{2,1,0:T(8,128)(2,1)S(1)}, u32[]{:S(2)}, u32[]{:S(2)}) %all-to-all-start) | async-done | bytes 1048608 | tf_op jit(solution)/shard_map/all_to_all | solution.py:160
  121.5 2.2 %best.1 = f32[64,16]{1,0:T(8,128)S(1)} custom-call(bf16[1024,512]{1,0:T(8,128)(2,1)S(1)} %bitcast.10, bf16[512,512]{1,0:T(8,128)(2,1)S(1)} %root.1.whiten_ref), custom_call_target="tpu_custom_call" | custom-call | flops 1610612736 | bytes 2097152 | tf_op jit(solution)/shard_map/best/pallas_call | solution.py:193
  123.7 22.8 %all_to_all.21 = f32[64,1,16]{2,1,0:T(1,128)S(1)} all-to-all(f32[64,1,16]{2,1,0:T(1,128)S(1)} %bitcast.13), channel_id=1, replica_groups=mesh['y'=8,'xh'=2,'xl'=2,'z'=16,'c'=2] {'xl','z','c'}, dimensions={0} | all-to-all | bytes 8192 | tf_op jit(solution)/shard_map/all_to_all | solution.py:160
  146.5 0.8 pick.1
  (10 shorter events, 0.1 us)
Async XLA Ops:
  0.0 1.0 copy-start.1
  34.1 13.4 %copy-start.2 = (bf16[512,512]{1,0:T(8,128)(2,1)S(1)}, bf16[512,512]{1,0:T(8,128)(2,1)}, u32[]{:S(2)}) copy-start(bf16[512,512]{1,0:T(8,128)(2,1)} %rows_ref.3) | copy-start | bytes 1572868
  34.9 12.7 %copy-start = (s32[512,1]{0,1:T(1,128)S(1)}, s32[512,1]{0,1:T(1,128)}, u32[]{:S(2)}) copy-start(s32[512,1]{0,1:T(1,128)} %param.3) | copy-start | bytes 6148
  34.9 25.7 %all-to-all-start.2 = ((f32[16,8,384]{2,1,0:T(8,128)}), f32[16,8,384]{2,1,0:T(8,128)S(1)}, u32[]{:S(2)}, u32[]{:S(2)}) async-start(f32[16,8,384]{2,1,0:T(8,128)} %broadcast_in_dim.3), calls=%async_computation.2 | async-start | bytes 393216 | tf_op jit(solution)/shard_map/all_to_all | solution.py:160
  60.5 60.9 %all-to-all-start = ((bf16[64,16,512]{2,1,0:T(8,128)(2,1)}), bf16[64,16,512]{2,1,0:T(8,128)(2,1)S(1)}, u32[]{:S(2)}, u32[]{:S(2)}) async-start(bf16[64,16,512]{2,1,0:T(8,128)(2,1)} %bitcast.1), calls=%async_computation | async-start | bytes 2097152 | tf_op jit(solution)/shard_map/all_to_all | solution.py:160
  71.1 4.7 %collective-permute-start = (f32[8,384]{1,0:T(8,128)S(1)}, f32[8,384]{1,0:T(8,128)S(1)}, u32[]{:S(2)}, u32[]{:S(2)}) collective-permute-start(f32[8,384]{1,0:T(8,128)S(1)} %reduce_sum.19), channel_id=1, source_target_pairs={{0,128},{128,0},{256,384},{384,256},{512,640},{640,512},{768,896},... | collective-permute-start | bytes 36872 | tf_op jit(solution)/shard_map/ppermute | solution.py:185
  75.9 5.8 %collective-permute-start.1 = (f32[16,384]{1,0:T(8,128)S(1)}, f32[16,384]{1,0:T(8,128)S(1)}, u32[]{:S(2)}, u32[]{:S(2)}) collective-permute-start(f32[16,384]{1,0:T(8,128)S(1)} %pad_maximum_fusion.2), channel_id=1, source_target_pairs={{0,256},{128,384},{256,0},{384,128},{512,768},{640,896},{768,512},... | collective-permute-start | bytes 73736 | tf_op jit(solution)/shard_map/ppermute | solution.py:185
  81.6 8.7 %collective-permute-start.2 = (f32[32,384]{1,0:T(8,128)S(1)}, f32[32,384]{1,0:T(8,128)S(1)}, u32[]{:S(2)}, u32[]{:S(2)}) collective-permute-start(f32[32,384]{1,0:T(8,128)S(1)} %pad_maximum_fusion.1), channel_id=1, source_target_pairs={{0,512},{128,640},{256,768},{384,896},{512,0},{640,128},{768,256},... | collective-permute-start | bytes 147464 | tf_op jit(solution)/shard_map/ppermute | solution.py:185
  90.4 6.9 %collective-permute-start.3 = (f32[64,384]{1,0:T(8,128)S(1)}, f32[64,384]{1,0:T(8,128)S(1)}, u32[]{:S(2)}, u32[]{:S(2)}) collective-permute-start(f32[64,384]{1,0:T(8,128)S(1)} %pad_maximum_fusion), channel_id=1, source_target_pairs={{0,96},{32,64},{64,32},{96,0},{1,97},{33,65},{65,33},{97,1},{2,98}... | collective-permute-start | bytes 294920 | tf_op jit(solution)/shard_map/ppermute | solution.py:185
  97.2 7.5 %collective-permute-start.4 = (f32[128,384]{1,0:T(8,128)S(1)}, f32[128,384]{1,0:T(8,128)S(1)}, u32[]{:S(2)}, u32[]{:S(2)}) collective-permute-start(f32[128,384]{1,0:T(8,128)S(1)} %get-tuple-element.9), channel_id=1, source_target_pairs={{0,32},{32,0},{1,33},{33,1},{2,34},{34,2},{3,35},{35,3},{4,36},{36... | collective-permute-start | bytes 589832 | tf_op jit(solution)/shard_map/ppermute | solution.py:185
  104.7 8.1 %collective-permute-start.5 = (f32[256,384]{1,0:T(8,128)S(1)}, f32[256,384]{1,0:T(8,128)S(1)}, u32[]{:S(2)}, u32[]{:S(2)}) collective-permute-start(f32[256,384]{1,0:T(8,128)S(1)} %constant_dynamic-update-slice_fusion.5.near_ref), channel_id=1, source_target_pairs={{0,1},{1,0},{2,3},{3,2},{4,5},{5,4},{6,7},{7,6},{8,9},{9,8},{10,11... | collective-permute-start | bytes 1179656 | tf_op jit(solution)/shard_map/ppermute | solution.py:185

commit v5 on v4

--- a/solution.py
+++ b/solution.py
@@ -28,6 +28,7 @@
 BLOCKS = D // BLOCK
 STRIP = 3 * BLOCK
 STRIP_ROWS = D // N_PLANE
+SHRINK = 2.0 ** -12
 DOUBLING = (
     (("y",), 1, 8),
     (("y",), 2, 16),
@@ -177,9 +178,9 @@
     )(label, embeddings)
     received = swap(outgoing.reshape(N_FINE, CAP, D), FINE).reshape(SLOTS, D)
 
-    strip = jnp.sum(parts.astype(F32), axis=0)
+    strip = (jnp.sum(parts.astype(F32), axis=0) * SHRINK).astype(jnp.float16)
     layers = swap(jnp.broadcast_to(strip, (N_Z, STRIP_ROWS, STRIP)), "z")
-    strip = jnp.sum(layers, axis=0)
+    strip = jnp.sum(layers.astype(F32), axis=0) * (1.0 / SHRINK)
     for axes, differs, _ in DOUBLING:
         size = math.prod(SIZES[AXES.index(axis)] for axis in axes)
         other = lax.ppermute(strip, axes, [(i, i ^ differs) for i in range(size)])

time: 148 us -> 144 us (0.973)
  starting transfers between devices: 44 us -> 41.7 us
  waiting for transfers between devices: 34.4 us -> 32.5 us
    all_to_all x2, starting transfers between devices: 23.2 us -> 20.2 us  [swap(): return lax.all_to_all(value, axes, split_axis=0, concat_axis=0, tiled=True)]
  transfers between devices with their start and end apart: 8 -> 8, of which waited for: 8 -> 8; matrix products, arithmetic and copies ran while one was open for 0% -> 0% of each run, Pallas kernels for 5% -> 6%
where the time goes in v5:
time: 144 us; the launch traced here: 143 us
  blocking collectives  55.3 us (38%)
  starting transfers between devices  41.7 us (29%)
  waiting for transfers between devices  32.5 us (23%)
  Pallas kernels  11.5 us (8%)
  local copies, waits for them, and re-layouts  1.74 us (1%)
    all_to_all x2, blocking collectives, swap(): return lax.all_to_all(value, axes, split_axis=0, concat_axis=0, tiled=True)  55.3 us
    ppermute x6, starting transfers between devices, per_device(): other = lax.ppermute(strip, axes, [(i, i ^ differs) for i in range(size)])  21.5 us
    all_to_all x2, starting transfers between devices, swap(): return lax.all_to_all(value, axes, split_axis=0, concat_axis=0, tiled=True)  20.2 us
    ppermute x6, waiting for transfers between devices, per_device(): other = lax.ppermute(strip, axes, [(i, i ^ differs) for i in range(size)])  20 us
    all_to_all x2, waiting for transfers between devices, swap(): return lax.all_to_all(value, axes, split_axis=0, concat_axis=0, tiled=True)  12.5 us
    pallas_call x1, Pallas kernels, per_device(): call(root_body, jax.ShapeDtypeStruct((D, D), BF16), 36 * D * D * D, 2 <<...  5.8 us
  transfers between devices with their start and end apart: 8, of which 8 were waited for; matrix products, arithmetic and copies ran while one was open for 0% of the time, Pallas kernels for 6%

profile of v5, /device:TPU:1, one launch (start us, length us, event | category | flops | bytes accessed | tf_op | source)
XLA Modules:
  0.0 143.0 jit_solution(505562337958800941)
XLA Ops:
  0.0 0.0 copy-start.1
  0.0 1.0 copy-done.1
  1.0 0.5 gram.1
  1.5 32.6 %all_to_all.20 = bf16[64,8,384]{2,1,0:T(8,128)(2,1)S(1)} all-to-all(bf16[64,8,384]{2,1,0:T(8,128)(2,1)S(1)} %bitcast.11), channel_id=1, replica_groups=mesh['y'=8,'xh'=2,'xl'=2,'z'=16,'c'=2] {'y','xh','xl','c'}, dimensions={0} | all-to-all | bytes 786432 | tf_op jit(solution)/shard_map/all_to_all | solution.py:161
  34.1 0.0 copy-start.2
  34.1 0.1 convert_reduce_fusion
  34.2 0.6 broadcast_in_dim.3
  34.8 0.0 copy-start
  34.8 12.6 %all-to-all-start.2 = ((f16[16,8,384]{2,1,0:T(8,128)(2,1)}), f16[16,8,384]{2,1,0:T(8,128)(2,1)S(1)}, u32[]{:S(2)}, u32[]{:S(2)}) async-start(f16[16,8,384]{2,1,0:T(8,128)(2,1)} %broadcast_in_dim.3), calls=%async_computation.2 | async-start | bytes 196608 | tf_op jit(solution)/shard_map/all_to_all | solution.py:161
  47.5 0.0 copy-done.2
  47.5 0.0 copy-done
  47.5 2.2 %pack.1 = (bf16[1024,512]{1,0:T(8,128)(2,1)}, s32[1,512]{1,0:T(1,128)S(1)}) custom-call(s32[1,512]{1,0:T(1,128)S(1)} %bitcast.14, bf16[512,512]{1,0:T(8,128)(2,1)S(1)} %copy-done.2), custom_call_target="tpu_custom_call" | custom-call | flops 536870912 | bytes 2097152 | tf_op jit(solution)/shard_map/pack/pallas_call | solution.py:171
  49.7 9.7 %all-to-all-done.2 = f16[16,8,384]{2,1,0:T(8,128)(2,1)S(1)} async-done(((f16[16,8,384]{2,1,0:T(8,128)(2,1)}), f16[16,8,384]{2,1,0:T(8,128)(2,1)S(1)}, u32[]{:S(2)}, u32[]{:S(2)}) %all-to-all-start.2) | async-done | bytes 98336 | tf_op jit(solution)/shard_map/all_to_all | solution.py:161
  59.3 7.5 %all-to-all-start = ((bf16[64,16,512]{2,1,0:T(8,128)(2,1)}), bf16[64,16,512]{2,1,0:T(8,128)(2,1)S(1)}, u32[]{:S(2)}, u32[]{:S(2)}) async-start(bf16[64,16,512]{2,1,0:T(8,128)(2,1)} %bitcast.1), calls=%async_computation | async-start | bytes 2097152 | tf_op jit(solution)/shard_map/all_to_all | solution.py:161
  66.9 2.6 %collective-permute-start = (f32[8,384]{1,0:T(8,128)S(1)}, f32[8,384]{1,0:T(8,128)S(1)}, u32[]{:S(2)}, u32[]{:S(2)}) collective-permute-start(f32[8,384]{1,0:T(8,128)S(1)} %get-tuple-element.19), channel_id=1, source_target_pairs={{0,128},{128,0},{256,384},{384,256},{512,640},{640,512},{768,896},... | collective-permute-start | bytes 36872 | tf_op jit(solution)/shard_map/ppermute | solution.py:186
  69.5 2.1 %collective-permute-done = f32[8,384]{1,0:T(8,128)S(1)} collective-permute-done((f32[8,384]{1,0:T(8,128)S(1)}, f32[8,384]{1,0:T(8,128)S(1)}, u32[]{:S(2)}, u32[]{:S(2)}) %collective-permute-start) | collective-permute-done | bytes 12320 | tf_op jit(solution)/shard_map/ppermute | solution.py:186
  71.6 2.7 %collective-permute-start.1 = (f32[16,384]{1,0:T(8,128)S(1)}, f32[16,384]{1,0:T(8,128)S(1)}, u32[]{:S(2)}, u32[]{:S(2)}) collective-permute-start(f32[16,384]{1,0:T(8,128)S(1)} %pad_maximum_fusion.2), channel_id=1, source_target_pairs={{0,256},{128,384},{256,0},{384,128},{512,768},{640,896},{768,512},... | collective-permute-start | bytes 73736 | tf_op jit(solution)/shard_map/ppermute | solution.py:186
  74.3 3.0 %collective-permute-done.1 = f32[16,384]{1,0:T(8,128)S(1)} collective-permute-done((f32[16,384]{1,0:T(8,128)S(1)}, f32[16,384]{1,0:T(8,128)S(1)}, u32[]{:S(2)}, u32[]{:S(2)}) %collective-permute-start.1) | collective-permute-done | bytes 24608 | tf_op jit(solution)/shard_map/ppermute | solution.py:186
  77.4 3.0 %collective-permute-start.2 = (f32[32,384]{1,0:T(8,128)S(1)}, f32[32,384]{1,0:T(8,128)S(1)}, u32[]{:S(2)}, u32[]{:S(2)}) collective-permute-start(f32[32,384]{1,0:T(8,128)S(1)} %pad_maximum_fusion.1), channel_id=1, source_target_pairs={{0,512},{128,640},{256,768},{384,896},{512,0},{640,128},{768,256},... | collective-permute-start | bytes 147464 | tf_op jit(solution)/shard_map/ppermute | solution.py:186
  80.4 5.7 %collective-permute-done.2 = f32[32,384]{1,0:T(8,128)S(1)} collective-permute-done((f32[32,384]{1,0:T(8,128)S(1)}, f32[32,384]{1,0:T(8,128)S(1)}, u32[]{:S(2)}, u32[]{:S(2)}) %collective-permute-start.2) | collective-permute-done | bytes 49184 | tf_op jit(solution)/shard_map/ppermute | solution.py:186
  86.1 4.0 %collective-permute-start.3 = (f32[64,384]{1,0:T(8,128)S(1)}, f32[64,384]{1,0:T(8,128)S(1)}, u32[]{:S(2)}, u32[]{:S(2)}) collective-permute-start(f32[64,384]{1,0:T(8,128)S(1)} %pad_maximum_fusion), channel_id=1, source_target_pairs={{0,96},{32,64},{64,32},{96,0},{1,97},{33,65},{65,33},{97,1},{2,98}... | collective-permute-start | bytes 294920 | tf_op jit(solution)/shard_map/ppermute | solution.py:186
  90.2 2.8 %collective-permute-done.3 = f32[64,384]{1,0:T(8,128)S(1)} collective-permute-done((f32[64,384]{1,0:T(8,128)S(1)}, f32[64,384]{1,0:T(8,128)S(1)}, u32[]{:S(2)}, u32[]{:S(2)}) %collective-permute-start.3) | collective-permute-done | bytes 98336 | tf_op jit(solution)/shard_map/ppermute | solution.py:186
  93.0 2.5 %collective-permute-start.4 = (f32[128,384]{1,0:T(8,128)S(1)}, f32[128,384]{1,0:T(8,128)S(1)}, u32[]{:S(2)}, u32[]{:S(2)}) collective-permute-start(f32[128,384]{1,0:T(8,128)S(1)} %get-tuple-element.9), channel_id=1, source_target_pairs={{0,32},{32,0},{1,33},{33,1},{2,34},{34,2},{3,35},{35,3},{4,36},{36... | collective-permute-start | bytes 589832 | tf_op jit(solution)/shard_map/ppermute | solution.py:186
  95.5 5.0 %collective-permute-done.4 = f32[128,384]{1,0:T(8,128)S(1)} collective-permute-done((f32[128,384]{1,0:T(8,128)S(1)}, f32[128,384]{1,0:T(8,128)S(1)}, u32[]{:S(2)}, u32[]{:S(2)}) %collective-permute-start.4) | collective-permute-done | bytes 196640 | tf_op jit(solution)/shard_map/ppermute | solution.py:186
  100.5 6.7 %collective-permute-start.5 = (f32[256,384]{1,0:T(8,128)S(1)}, f32[256,384]{1,0:T(8,128)S(1)}, u32[]{:S(2)}, u32[]{:S(2)}) collective-permute-start(f32[256,384]{1,0:T(8,128)S(1)} %constant_dynamic-update-slice_fusion.5.near_ref), channel_id=1, source_target_pairs={{0,1},{1,0},{2,3},{3,2},{4,5},{5,4},{6,7},{7,6},{8,9},{9,8},{10,11... | collective-permute-start | bytes 1179656 | tf_op jit(solution)/shard_map/ppermute | solution.py:186
  107.2 1.3 collective-permute-done.5.far_ref
  108.6 5.8 %root.1.whiten_ref = bf16[512,512]{1,0:T(8,128)(2,1)S(1)} custom-call(s32[1]{0:T(128)} %bitcast.3.me_ref, f32[256,384]{1,0:T(8,128)S(1)} %constant_dynamic-update-slice_fusion.5.near_ref, f32[256,384]{1,0:T(8,128)S(1)} %collective-permute-done.5.far_ref), custom_call_target="tpu_custom_call" | custom-call | flops 4831838208 | bytes 2097152 | tf_op jit(solution)/shard_map/root/pallas_call | solution.py:188
  114.4 2.8 %all-to-all-done = bf16[64,16,512]{2,1,0:T(8,128)(2,1)S(1)} async-done(((bf16[64,16,512]{2,1,0:T(8,128)(2,1)}), bf16[64,16,512]{2,1,0:T(8,128)(2,1)S(1)}, u32[]{:S(2)}, u32[]{:S(2)}) %all-to-all-start) | async-done | bytes 1048608 | tf_op jit(solution)/shard_map/all_to_all | solution.py:161
  117.2 2.3 %best.1 = f32[64,16]{1,0:T(8,128)S(1)} custom-call(bf16[1024,512]{1,0:T(8,128)(2,1)S(1)} %bitcast.10, bf16[512,512]{1,0:T(8,128)(2,1)S(1)} %root.1.whiten_ref), custom_call_target="tpu_custom_call" | custom-call | flops 1610612736 | bytes 2097152 | tf_op jit(solution)/shard_map/best/pallas_call | solution.py:194
  119.5 22.7 %all_to_all.21 = f32[64,1,16]{2,1,0:T(1,128)S(1)} all-to-all(f32[64,1,16]{2,1,0:T(1,128)S(1)} %bitcast.13), channel_id=1, replica_groups=mesh['y'=8,'xh'=2,'xl'=2,'z'=16,'c'=2] {'xl','z','c'}, dimensions={0} | all-to-all | bytes 8192 | tf_op jit(solution)/shard_map/all_to_all | solution.py:161
  142.2 0.8 pick.1
  (11 shorter events, 0.1 us)
Async XLA Ops:
  0.0 1.0 copy-start.1
  34.1 13.4 %copy-start.2 = (bf16[512,512]{1,0:T(8,128)(2,1)S(1)}, bf16[512,512]{1,0:T(8,128)(2,1)}, u32[]{:S(2)}) copy-start(bf16[512,512]{1,0:T(8,128)(2,1)} %rows_ref.3) | copy-start | bytes 1572868
  34.8 12.7 %copy-start = (s32[512,1]{0,1:T(1,128)S(1)}, s32[512,1]{0,1:T(1,128)}, u32[]{:S(2)}) copy-start(s32[512,1]{0,1:T(1,128)} %param.3) | copy-start | bytes 6148
  34.8 24.5 %all-to-all-start.2 = ((f16[16,8,384]{2,1,0:T(8,128)(2,1)}), f16[16,8,384]{2,1,0:T(8,128)(2,1)S(1)}, u32[]{:S(2)}, u32[]{:S(2)}) async-start(f16[16,8,384]{2,1,0:T(8,128)(2,1)} %broadcast_in_dim.3), calls=%async_computation.2 | async-start | bytes 196608 | tf_op jit(solution)/shard_map/all_to_all | solution.py:161
  59.3 57.9 %all-to-all-start = ((bf16[64,16,512]{2,1,0:T(8,128)(2,1)}), bf16[64,16,512]{2,1,0:T(8,128)(2,1)S(1)}, u32[]{:S(2)}, u32[]{:S(2)}) async-start(bf16[64,16,512]{2,1,0:T(8,128)(2,1)} %bitcast.1), calls=%async_computation | async-start | bytes 2097152 | tf_op jit(solution)/shard_map/all_to_all | solution.py:161
  66.9 4.7 %collective-permute-start = (f32[8,384]{1,0:T(8,128)S(1)}, f32[8,384]{1,0:T(8,128)S(1)}, u32[]{:S(2)}, u32[]{:S(2)}) collective-permute-start(f32[8,384]{1,0:T(8,128)S(1)} %get-tuple-element.19), channel_id=1, source_target_pairs={{0,128},{128,0},{256,384},{384,256},{512,640},{640,512},{768,896},... | collective-permute-start | bytes 36872 | tf_op jit(solution)/shard_map/ppermute | solution.py:186
  71.6 5.8 %collective-permute-start.1 = (f32[16,384]{1,0:T(8,128)S(1)}, f32[16,384]{1,0:T(8,128)S(1)}, u32[]{:S(2)}, u32[]{:S(2)}) collective-permute-start(f32[16,384]{1,0:T(8,128)S(1)} %pad_maximum_fusion.2), channel_id=1, source_target_pairs={{0,256},{128,384},{256,0},{384,128},{512,768},{640,896},{768,512},... | collective-permute-start | bytes 73736 | tf_op jit(solution)/shard_map/ppermute | solution.py:186
  77.4 8.7 %collective-permute-start.2 = (f32[32,384]{1,0:T(8,128)S(1)}, f32[32,384]{1,0:T(8,128)S(1)}, u32[]{:S(2)}, u32[]{:S(2)}) collective-permute-start(f32[32,384]{1,0:T(8,128)S(1)} %pad_maximum_fusion.1), channel_id=1, source_target_pairs={{0,512},{128,640},{256,768},{384,896},{512,0},{640,128},{768,256},... | collective-permute-start | bytes 147464 | tf_op jit(solution)/shard_map/ppermute | solution.py:186
  86.1 6.9 %collective-permute-start.3 = (f32[64,384]{1,0:T(8,128)S(1)}, f32[64,384]{1,0:T(8,128)S(1)}, u32[]{:S(2)}, u32[]{:S(2)}) collective-permute-start(f32[64,384]{1,0:T(8,128)S(1)} %pad_maximum_fusion), channel_id=1, source_target_pairs={{0,96},{32,64},{64,32},{96,0},{1,97},{33,65},{65,33},{97,1},{2,98}... | collective-permute-start | bytes 294920 | tf_op jit(solution)/shard_map/ppermute | solution.py:186
  93.0 7.5 %collective-permute-start.4 = (f32[128,384]{1,0:T(8,128)S(1)}, f32[128,384]{1,0:T(8,128)S(1)}, u32[]{:S(2)}, u32[]{:S(2)}) collective-permute-start(f32[128,384]{1,0:T(8,128)S(1)} %get-tuple-element.9), channel_id=1, source_target_pairs={{0,32},{32,0},{1,33},{33,1},{2,34},{34,2},{3,35},{35,3},{4,36},{36... | collective-permute-start | bytes 589832 | tf_op jit(solution)/shard_map/ppermute | solution.py:186
  100.5 8.1 %collective-permute-start.5 = (f32[256,384]{1,0:T(8,128)S(1)}, f32[256,384]{1,0:T(8,128)S(1)}, u32[]{:S(2)}, u32[]{:S(2)}) collective-permute-start(f32[256,384]{1,0:T(8,128)S(1)} %constant_dynamic-update-slice_fusion.5.near_ref), channel_id=1, source_target_pairs={{0,1},{1,0},{2,3},{3,2},{4,5},{5,4},{6,7},{7,6},{8,9},{9,8},{10,11... | collective-permute-start | bytes 1179656 | tf_op jit(solution)/shard_map/ppermute | solution.py:186

commit v6 on v5

--- a/solution.py
+++ b/solution.py
@@ -14,7 +14,8 @@
 AXES = ("y", "xh", "xl", "z", "c")
 SIZES = (8, 2, 2, 16, 2)
 FINE = ("xl", "z", "c")
-PLANE = ("y", "xh", "xl", "c")
+FLAT = ("y", "xh", "xl")
+PLANE = ("c",) + FLAT
 
 D = 512
 ROW_DEV = 512
@@ -26,16 +27,19 @@
 SLOTS = N_FINE * CAP
 BLOCK = 128
 BLOCKS = D // BLOCK
+HALF = D // 2
+PARTS = 4
+
 STRIP = 3 * BLOCK
 STRIP_ROWS = D // N_PLANE
 SHRINK = 2.0 ** -12
 DOUBLING = (
-    (("y",), 1, 8),
-    (("y",), 2, 16),
-    (("y",), 4, 32),
-    (("xh", "xl"), 3, 6),
-    (("xl",), 1, 2),
-    (("c",), 1, 1),
+    (("y",), 1, 4),
+    (("y",), 2, 8),
+    (("y",), 4, 16),
+    (("xh", "xl"), 3, 3),
+    (("xl",), 1, 1),
+    (("c",), 1, 32),
 )
 
 F32 = jnp.float32
@@ -50,20 +54,31 @@
 SMEM = pl.BlockSpec(memory_space=pltpu.SMEM)
 
 
-def call(body, outs, flops, moved, scratch=(), name=None, specs=None):
+def call(body, outs, flops, moved, scratch=(), name=None, specs=None, room=48):
     return pl.pallas_call(
         body,
         **({} if specs is None else dict(in_specs=specs)),
         out_shape=outs,
         scratch_shapes=scratch,
         name=name,
-        compiler_params=pltpu.CompilerParams(vmem_limit_bytes=48 << 20),
+        compiler_params=pltpu.CompilerParams(vmem_limit_bytes=room << 20),
         cost_estimate=pl.CostEstimate(flops=flops, bytes_accessed=moved, transcendentals=0),
     )
 
 
-def gram_body(rows_ref, out_ref):
-    rows = rows_ref[...]
+def gram_body(rows_ref, out_ref, held_ref, sems):
+    part = ROW_DEV // PARTS
+    copies = [
+        pltpu.make_async_copy(
+            rows_ref.at[pl.ds(i * part, part), :], held_ref.at[pl.ds(i * part, part), :], sems.at[i]
+        )
+        for i in range(PARTS)
+    ]
+    for copy in copies:
+        copy.start()
+    for copy in copies:
+        copy.wait()
+    rows = held_ref[...]
     gram = lax.dot_general(rows, rows, (((0,), (0,)), ((), ())), preferred_element_type=F32)
     for b in range(BLOCKS):
         for k in range(3):
@@ -71,6 +86,13 @@
             out_ref[b * BLOCK:(b + 1) * BLOCK, k * BLOCK:(k + 1) * BLOCK] = gram[
                 b * BLOCK:(b + 1) * BLOCK, c * BLOCK:(c + 1) * BLOCK
             ].astype(out_ref.dtype)
+
+
+def halve_body(core_ref, both_ref, out_ref):
+    at = pl.multiple_of(core_ref[0] * HALF, HALF)
+    out_ref[...] = (
+        both_ref[pl.ds(at, HALF), :].astype(F32) + both_ref[pl.ds(at + D, HALF), :].astype(F32)
+    ).astype(BF16)
 
 
 def pack_body(label_ref, rows_ref, out_ref, slot_ref):
@@ -131,17 +153,20 @@
     unit = (whitened * lax.rsqrt(D * (meansq + EPS))).astype(BF16)
     bias = jnp.where(present[:, :1], 0.0, -4.0)
     tile = 256
-    best = jnp.full((1, SLOTS), -1.0, F32)
-    for b in range(SLOTS // tile):
-        lo = b * tile
-        similar = lax.dot_general(
-            unit[lo:lo + tile], unit, (((1,), (1,)), ((), ())), preferred_element_type=F32
-        )
-        similar = similar + bias[lo:lo + tile]
-        similar = jnp.where(
-            iota((tile, SLOTS), 0) + lo == iota((tile, SLOTS), 1), -1.0, similar
-        )
-        best = jnp.maximum(best, jnp.max(similar, axis=0, keepdims=True))
+    own = iota((tile, tile), 0) == iota((tile, tile), 1)
+    columns = []
+    for c in range(SLOTS // tile):
+        best = jnp.full((1, tile), -1.0, F32)
+        for b in range(SLOTS // tile):
+            similar = lax.dot_general(
+                unit[b * tile:(b + 1) * tile], unit[c * tile:(c + 1) * tile],
+                (((1,), (1,)), ((), ())), preferred_element_type=F32,
+            ) + bias[b * tile:(b + 1) * tile]
+            if b == c:
+                similar = jnp.where(own, -1.0, similar)
+            best = jnp.maximum(best, jnp.max(similar, axis=0, keepdims=True))
+        columns.append(best)
+    best = jnp.concatenate(columns, axis=1)
     spread = jnp.where(iota((N_FINE, SLOTS), 1) // CAP == iota((N_FINE, SLOTS), 0), best, 0.0)
     fold = (iota((SLOTS, CAP), 0) % CAP == iota((SLOTS, CAP), 1)).astype(F32)
     out_ref[...] = high(spread, fold)
@@ -164,9 +189,16 @@
 def per_device(embeddings, labels):
     label = labels.reshape(1, ROW_DEV)
     strips = call(
-        gram_body, jax.ShapeDtypeStruct((D, STRIP), BF16), 2 * ROW_DEV * D * D, 1 << 20, name="gram"
-    )(embeddings)
-    parts = swap(strips.reshape(N_PLANE, STRIP_ROWS, STRIP), PLANE)
+        gram_body, jax.ShapeDtypeStruct((D, STRIP), BF16), 2 * ROW_DEV * D * D, 1 << 20,
+        (pltpu.VMEM((ROW_DEV, D), BF16), pltpu.SemaphoreType.DMA((PARTS,))), name="gram",
+        specs=(pl.BlockSpec(memory_space=pltpu.HBM),),
+    )(pltpu.with_memory_space_constraint(embeddings, pltpu.HBM))
+    both = lax.all_gather(strips, "c", axis=0, tiled=True)
+    strips = call(
+        halve_body, jax.ShapeDtypeStruct((HALF, STRIP), BF16), D * STRIP, 1 << 20, name="halve",
+        specs=(SMEM, VMEM),
+    )(lax.axis_index("c").reshape(1), both)
+    parts = swap(strips.reshape(N_PLANE // 2, STRIP_ROWS, STRIP), FLAT)
 
     outgoing, slot = call(
         pack_body,

time: 144 us -> 141 us (0.979)
  blocking collectives: 55.3 us -> 52.5 us
    all_to_all x2, blocking collectives: 55.3 us -> 36.4 us  [swap(): return lax.all_to_all(value, axes, split_axis=0, concat_axis=0, tiled=True)]
    all_gather x0 -> x1, blocking collectives: none -> 16.2 us  [per_device(): both = lax.all_gather(strips, 'c', axis=0, tiled=True)]
where the time goes in v6:
time: 141 us; the launch traced here: 140 us
  blocking collectives  52.5 us (37%)
  starting transfers between devices  41.6 us (30%)
  waiting for transfers between devices  32.7 us (23%)
  Pallas kernels  12.6 us (9%)
    all_to_all x2, blocking collectives, swap(): return lax.all_to_all(value, axes, split_axis=0, concat_axis=0, tiled=True)  36.4 us
    ppermute x6, starting transfers between devices, per_device(): other = lax.ppermute(strip, axes, [(i, i ^ differs) for i in range(size)])  21.4 us
    ppermute x6, waiting for transfers between devices, per_device(): other = lax.ppermute(strip, axes, [(i, i ^ differs) for i in range(size)])  20.2 us
    all_to_all x2, starting transfers between devices, swap(): return lax.all_to_all(value, axes, split_axis=0, concat_axis=0, tiled=True)  20.2 us
    all_gather x1, blocking collectives, per_device(): both = lax.all_gather(strips, 'c', axis=0, tiled=True)  16.2 us
    all_to_all x2, waiting for transfers between devices, swap(): return lax.all_to_all(value, axes, split_axis=0, concat_axis=0, tiled=True)  12.5 us
    pallas_call x1, Pallas kernels, per_device(): call(root_body, jax.ShapeDtypeStruct((D, D), BF16), 36 * D * D * D, 2 <<...  5.8 us
  transfers between devices with their start and end apart: 8, of which 8 were waited for; matrix products, arithmetic and copies ran while one was open for 0% of the time, Pallas kernels for 6%

profile of v6, /device:TPU:1, one launch (start us, length us, event | category | flops | bytes accessed | tf_op | source)
XLA Modules:
  0.0 140.4 jit_solution(1208906121191029444)
XLA Ops:
  0.0 1.6 %gram.1 = bf16[512,384]{1,0:T(8,128)(2,1)S(1)} custom-call(bf16[512,512]{1,0:T(8,128)(2,1)} %rows_ref.3), custom_call_target="tpu_custom_call" | custom-call | flops 268435456 | bytes 1048576 | tf_op jit(solution)/shard_map/gram/pallas_call | solution.py:191
  1.6 16.2 %all_gather.3.both_ref = bf16[1024,384]{1,0:T(8,128)(2,1)S(1)} all-gather(bf16[512,384]{1,0:T(8,128)(2,1)S(1)} %gram.1), channel_id=1, replica_groups=mesh['y'=8,'xh'=2,'xl'=2,'z'=16,'c'=2] {'c'}, dimensions={0}, use_global_device_ids=true | all-gather | bytes 1179648 | tf_op jit(solution)/shard_map/all_gather | solution.py:196
  17.8 0.1 halve.1
  17.8 0.0 copy-start.1
  17.8 13.6 %all_to_all.20 = bf16[32,8,384]{2,1,0:T(8,128)(2,1)S(1)} all-to-all(bf16[32,8,384]{2,1,0:T(8,128)(2,1)S(1)} %bitcast.12), channel_id=1, replica_groups=mesh['y'=8,'xh'=2,'xl'=2,'z'=16,'c'=2] {'y','xh','xl'}, dimensions={0} | all-to-all | bytes 393216 | tf_op jit(solution)/shard_map/all_to_all | solution.py:186
  31.5 0.6 broadcast_in_dim.3
  32.1 0.0 copy-start
  32.1 12.6 %all-to-all-start.2 = ((f16[16,8,384]{2,1,0:T(8,128)(2,1)}), f16[16,8,384]{2,1,0:T(8,128)(2,1)S(1)}, u32[]{:S(2)}, u32[]{:S(2)}) async-start(f16[16,8,384]{2,1,0:T(8,128)(2,1)} %broadcast_in_dim.3), calls=%async_computation.2 | async-start | bytes 196608 | tf_op jit(solution)/shard_map/all_to_all | solution.py:186
  44.8 0.0 copy-done.1
  44.8 0.0 copy-done
  44.8 2.2 %pack.1 = (bf16[1024,512]{1,0:T(8,128)(2,1)}, s32[1,512]{1,0:T(1,128)S(1)}) custom-call(s32[1,512]{1,0:T(1,128)S(1)} %bitcast.15, bf16[512,512]{1,0:T(8,128)(2,1)S(1)} %copy-done.1), custom_call_target="tpu_custom_call" | custom-call | flops 536870912 | bytes 2097152 | tf_op jit(solution)/shard_map/pack/pallas_call | solution.py:203
  47.0 9.7 %all-to-all-done.2 = f16[16,8,384]{2,1,0:T(8,128)(2,1)S(1)} async-done(((f16[16,8,384]{2,1,0:T(8,128)(2,1)}), f16[16,8,384]{2,1,0:T(8,128)(2,1)S(1)}, u32[]{:S(2)}, u32[]{:S(2)}) %all-to-all-start.2) | async-done | bytes 98336 | tf_op jit(solution)/shard_map/all_to_all | solution.py:186
  56.6 7.5 %all-to-all-start = ((bf16[64,16,512]{2,1,0:T(8,128)(2,1)}), bf16[64,16,512]{2,1,0:T(8,128)(2,1)S(1)}, u32[]{:S(2)}, u32[]{:S(2)}) async-start(bf16[64,16,512]{2,1,0:T(8,128)(2,1)} %bitcast.1), calls=%async_computation | async-start | bytes 2097152 | tf_op jit(solution)/shard_map/all_to_all | solution.py:186
  64.2 2.7 %collective-permute-start = (f32[8,384]{1,0:T(8,128)S(1)}, f32[8,384]{1,0:T(8,128)S(1)}, u32[]{:S(2)}, u32[]{:S(2)}) collective-permute-start(f32[8,384]{1,0:T(8,128)S(1)} %get-tuple-element.19), channel_id=1, source_target_pairs={{0,128},{128,0},{256,384},{384,256},{512,640},{640,512},{768,896},... | collective-permute-start | bytes 36872 | tf_op jit(solution)/shard_map/ppermute | solution.py:218
  66.9 2.0 %collective-permute-done = f32[8,384]{1,0:T(8,128)S(1)} collective-permute-done((f32[8,384]{1,0:T(8,128)S(1)}, f32[8,384]{1,0:T(8,128)S(1)}, u32[]{:S(2)}, u32[]{:S(2)}) %collective-permute-start) | collective-permute-done | bytes 12320 | tf_op jit(solution)/shard_map/ppermute | solution.py:218
  68.9 2.9 %collective-permute-start.1 = (f32[16,384]{1,0:T(8,128)S(1)}, f32[16,384]{1,0:T(8,128)S(1)}, u32[]{:S(2)}, u32[]{:S(2)}) collective-permute-start(f32[16,384]{1,0:T(8,128)S(1)} %pad_maximum_fusion.2), channel_id=1, source_target_pairs={{0,256},{128,384},{256,0},{384,128},{512,768},{640,896},{768,512},... | collective-permute-start | bytes 73736 | tf_op jit(solution)/shard_map/ppermute | solution.py:218
  71.9 2.8 %collective-permute-done.1 = f32[16,384]{1,0:T(8,128)S(1)} collective-permute-done((f32[16,384]{1,0:T(8,128)S(1)}, f32[16,384]{1,0:T(8,128)S(1)}, u32[]{:S(2)}, u32[]{:S(2)}) %collective-permute-start.1) | collective-permute-done | bytes 24608 | tf_op jit(solution)/shard_map/ppermute | solution.py:218
  74.7 3.0 %collective-permute-start.2 = (f32[32,384]{1,0:T(8,128)S(1)}, f32[32,384]{1,0:T(8,128)S(1)}, u32[]{:S(2)}, u32[]{:S(2)}) collective-permute-start(f32[32,384]{1,0:T(8,128)S(1)} %pad_maximum_fusion.1), channel_id=1, source_target_pairs={{0,512},{128,640},{256,768},{384,896},{512,0},{640,128},{768,256},... | collective-permute-start | bytes 147464 | tf_op jit(solution)/shard_map/ppermute | solution.py:218
  77.7 6.0 %collective-permute-done.2 = f32[32,384]{1,0:T(8,128)S(1)} collective-permute-done((f32[32,384]{1,0:T(8,128)S(1)}, f32[32,384]{1,0:T(8,128)S(1)}, u32[]{:S(2)}, u32[]{:S(2)}) %collective-permute-start.2) | collective-permute-done | bytes 49184 | tf_op jit(solution)/shard_map/ppermute | solution.py:218
  83.7 4.0 %collective-permute-start.3 = (f32[64,384]{1,0:T(8,128)S(1)}, f32[64,384]{1,0:T(8,128)S(1)}, u32[]{:S(2)}, u32[]{:S(2)}) collective-permute-start(f32[64,384]{1,0:T(8,128)S(1)} %pad_maximum_fusion), channel_id=1, source_target_pairs={{0,96},{32,64},{64,32},{96,0},{1,97},{33,65},{65,33},{97,1},{2,98}... | collective-permute-start | bytes 294920 | tf_op jit(solution)/shard_map/ppermute | solution.py:218
  87.7 2.9 %collective-permute-done.3 = f32[64,384]{1,0:T(8,128)S(1)} collective-permute-done((f32[64,384]{1,0:T(8,128)S(1)}, f32[64,384]{1,0:T(8,128)S(1)}, u32[]{:S(2)}, u32[]{:S(2)}) %collective-permute-start.3) | collective-permute-done | bytes 98336 | tf_op jit(solution)/shard_map/ppermute | solution.py:218
  90.6 2.3 %collective-permute-start.4 = (f32[128,384]{1,0:T(8,128)S(1)}, f32[128,384]{1,0:T(8,128)S(1)}, u32[]{:S(2)}, u32[]{:S(2)}) collective-permute-start(f32[128,384]{1,0:T(8,128)S(1)} %get-tuple-element.9), channel_id=1, source_target_pairs={{0,32},{32,0},{1,33},{33,1},{2,34},{34,2},{3,35},{35,3},{4,36},{36... | collective-permute-start | bytes 589832 | tf_op jit(solution)/shard_map/ppermute | solution.py:218
  92.9 5.2 %collective-permute-done.4 = f32[128,384]{1,0:T(8,128)S(1)} collective-permute-done((f32[128,384]{1,0:T(8,128)S(1)}, f32[128,384]{1,0:T(8,128)S(1)}, u32[]{:S(2)}, u32[]{:S(2)}) %collective-permute-start.4) | collective-permute-done | bytes 196640 | tf_op jit(solution)/shard_map/ppermute | solution.py:218
  98.1 6.5 %collective-permute-start.5 = (f32[256,384]{1,0:T(8,128)S(1)}, f32[256,384]{1,0:T(8,128)S(1)}, u32[]{:S(2)}, u32[]{:S(2)}) collective-permute-start(f32[256,384]{1,0:T(8,128)S(1)} %constant_dynamic-update-slice_fusion.5.near_ref), channel_id=1, source_target_pairs={{0,1},{1,0},{2,3},{3,2},{4,5},{5,4},{6,7},{7,6},{8,9},{9,8},{10,11... | collective-permute-start | bytes 1179656 | tf_op jit(solution)/shard_map/ppermute | solution.py:218
  104.7 1.3 collective-permute-done.5.far_ref
  106.0 5.8 %root.1.whiten_ref = bf16[512,512]{1,0:T(8,128)(2,1)S(1)} custom-call(s32[1]{0:T(128)} %bitcast.3.me_ref, f32[256,384]{1,0:T(8,128)S(1)} %constant_dynamic-update-slice_fusion.5.near_ref, f32[256,384]{1,0:T(8,128)S(1)} %collective-permute-done.5.far_ref), custom_call_target="tpu_custom_call" | custom-call | flops 4831838208 | bytes 2097152 | tf_op jit(solution)/shard_map/root/pallas_call | solution.py:220
  111.8 2.8 %all-to-all-done = bf16[64,16,512]{2,1,0:T(8,128)(2,1)S(1)} async-done(((bf16[64,16,512]{2,1,0:T(8,128)(2,1)}), bf16[64,16,512]{2,1,0:T(8,128)(2,1)S(1)}, u32[]{:S(2)}, u32[]{:S(2)}) %all-to-all-start) | async-done | bytes 1048608 | tf_op jit(solution)/shard_map/all_to_all | solution.py:186
  114.6 2.2 %best.1 = f32[64,16]{1,0:T(8,128)S(1)} custom-call(bf16[1024,512]{1,0:T(8,128)(2,1)S(1)} %bitcast.11, bf16[512,512]{1,0:T(8,128)(2,1)S(1)} %root.1.whiten_ref), custom_call_target="tpu_custom_call" | custom-call | flops 1610612736 | bytes 2097152 | tf_op jit(solution)/shard_map/best/pallas_call | solution.py:226
  116.8 22.7 %all_to_all.21 = f32[64,1,16]{2,1,0:T(1,128)S(1)} all-to-all(f32[64,1,16]{2,1,0:T(1,128)S(1)} %bitcast.14), channel_id=1, replica_groups=mesh['y'=8,'xh'=2,'xl'=2,'z'=16,'c'=2] {'xl','z','c'}, dimensions={0} | all-to-all | bytes 8192 | tf_op jit(solution)/shard_map/all_to_all | solution.py:186
  139.6 0.8 pick.1
  (12 shorter events, 0.1 us)
Async XLA Ops:
  17.8 27.0 %copy-start.1 = (bf16[512,512]{1,0:T(8,128)(2,1)S(1)}, bf16[512,512]{1,0:T(8,128)(2,1)}, u32[]{:S(2)}) copy-start(bf16[512,512]{1,0:T(8,128)(2,1)} %rows_ref.3) | copy-start | bytes 1572868
  32.1 12.7 %copy-start = (s32[512,1]{0,1:T(1,128)S(1)}, s32[512,1]{0,1:T(1,128)}, u32[]{:S(2)}) copy-start(s32[512,1]{0,1:T(1,128)} %param.3) | copy-start | bytes 6148
  32.1 24.5 %all-to-all-start.2 = ((f16[16,8,384]{2,1,0:T(8,128)(2,1)}), f16[16,8,384]{2,1,0:T(8,128)(2,1)S(1)}, u32[]{:S(2)}, u32[]{:S(2)}) async-start(f16[16,8,384]{2,1,0:T(8,128)(2,1)} %broadcast_in_dim.3), calls=%async_computation.2 | async-start | bytes 196608 | tf_op jit(solution)/shard_map/all_to_all | solution.py:186
  56.6 58.0 %all-to-all-start = ((bf16[64,16,512]{2,1,0:T(8,128)(2,1)}), bf16[64,16,512]{2,1,0:T(8,128)(2,1)S(1)}, u32[]{:S(2)}, u32[]{:S(2)}) async-start(bf16[64,16,512]{2,1,0:T(8,128)(2,1)} %bitcast.1), calls=%async_computation | async-start | bytes 2097152 | tf_op jit(solution)/shard_map/all_to_all | solution.py:186
  64.2 4.7 %collective-permute-start = (f32[8,384]{1,0:T(8,128)S(1)}, f32[8,384]{1,0:T(8,128)S(1)}, u32[]{:S(2)}, u32[]{:S(2)}) collective-permute-start(f32[8,384]{1,0:T(8,128)S(1)} %get-tuple-element.19), channel_id=1, source_target_pairs={{0,128},{128,0},{256,384},{384,256},{512,640},{640,512},{768,896},... | collective-permute-start | bytes 36872 | tf_op jit(solution)/shard_map/ppermute | solution.py:218
  68.9 5.8 %collective-permute-start.1 = (f32[16,384]{1,0:T(8,128)S(1)}, f32[16,384]{1,0:T(8,128)S(1)}, u32[]{:S(2)}, u32[]{:S(2)}) collective-permute-start(f32[16,384]{1,0:T(8,128)S(1)} %pad_maximum_fusion.2), channel_id=1, source_target_pairs={{0,256},{128,384},{256,0},{384,128},{512,768},{640,896},{768,512},... | collective-permute-start | bytes 73736 | tf_op jit(solution)/shard_map/ppermute | solution.py:218
  74.7 9.0 %collective-permute-start.2 = (f32[32,384]{1,0:T(8,128)S(1)}, f32[32,384]{1,0:T(8,128)S(1)}, u32[]{:S(2)}, u32[]{:S(2)}) collective-permute-start(f32[32,384]{1,0:T(8,128)S(1)} %pad_maximum_fusion.1), channel_id=1, source_target_pairs={{0,512},{128,640},{256,768},{384,896},{512,0},{640,128},{768,256},... | collective-permute-start | bytes 147464 | tf_op jit(solution)/shard_map/ppermute | solution.py:218
  83.7 6.9 %collective-permute-start.3 = (f32[64,384]{1,0:T(8,128)S(1)}, f32[64,384]{1,0:T(8,128)S(1)}, u32[]{:S(2)}, u32[]{:S(2)}) collective-permute-start(f32[64,384]{1,0:T(8,128)S(1)} %pad_maximum_fusion), channel_id=1, source_target_pairs={{0,96},{32,64},{64,32},{96,0},{1,97},{33,65},{65,33},{97,1},{2,98}... | collective-permute-start | bytes 294920 | tf_op jit(solution)/shard_map/ppermute | solution.py:218
  90.6 7.5 %collective-permute-start.4 = (f32[128,384]{1,0:T(8,128)S(1)}, f32[128,384]{1,0:T(8,128)S(1)}, u32[]{:S(2)}, u32[]{:S(2)}) collective-permute-start(f32[128,384]{1,0:T(8,128)S(1)} %get-tuple-element.9), channel_id=1, source_target_pairs={{0,32},{32,0},{1,33},{33,1},{2,34},{34,2},{3,35},{35,3},{4,36},{36... | collective-permute-start | bytes 589832 | tf_op jit(solution)/shard_map/ppermute | solution.py:218
  98.1 7.8 %collective-permute-start.5 = (f32[256,384]{1,0:T(8,128)S(1)}, f32[256,384]{1,0:T(8,128)S(1)}, u32[]{:S(2)}, u32[]{:S(2)}) collective-permute-start(f32[256,384]{1,0:T(8,128)S(1)} %constant_dynamic-update-slice_fusion.5.near_ref), channel_id=1, source_target_pairs={{0,1},{1,0},{2,3},{3,2},{4,5},{5,4},{6,7},{7,6},{8,9},{9,8},{10,11... | collective-permute-start | bytes 1179656 | tf_op jit(solution)/shard_map/ppermute | solution.py:218

commit v7 on v6

--- a/solution.py
+++ b/solution.py
@@ -28,11 +28,12 @@
 BLOCK = 128
 BLOCKS = D // BLOCK
 HALF = D // 2
-PARTS = 4
+PARTS = 2
 
 STRIP = 3 * BLOCK
 STRIP_ROWS = D // N_PLANE
 SHRINK = 2.0 ** -12
+CHIP_SHRINK = 2.0 ** -7
 DOUBLING = (
     (("y",), 1, 4),
     (("y",), 2, 8),
@@ -44,6 +45,7 @@
 
 F32 = jnp.float32
 BF16 = jnp.bfloat16
+F16 = jnp.float16
 
 
 def iota(shape, dim):
@@ -76,23 +78,18 @@
     ]
     for copy in copies:
         copy.start()
-    for copy in copies:
+    gram = None
+    for i, copy in enumerate(copies):
         copy.wait()
-    rows = held_ref[...]
-    gram = lax.dot_general(rows, rows, (((0,), (0,)), ((), ())), preferred_element_type=F32)
+        rows = held_ref[i * part:(i + 1) * part, :]
+        term = lax.dot_general(rows, rows, (((0,), (0,)), ((), ())), preferred_element_type=F32)
+        gram = term if gram is None else gram + term
     for b in range(BLOCKS):
         for k in range(3):
             c = (b + k) % BLOCKS
             out_ref[b * BLOCK:(b + 1) * BLOCK, k * BLOCK:(k + 1) * BLOCK] = gram[
                 b * BLOCK:(b + 1) * BLOCK, c * BLOCK:(c + 1) * BLOCK
             ].astype(out_ref.dtype)
-
-
-def halve_body(core_ref, both_ref, out_ref):
-    at = pl.multiple_of(core_ref[0] * HALF, HALF)
-    out_ref[...] = (
-        both_ref[pl.ds(at, HALF), :].astype(F32) + both_ref[pl.ds(at + D, HALF), :].astype(F32)
-    ).astype(BF16)
 
 
 def pack_body(label_ref, rows_ref, out_ref, slot_ref):
@@ -167,9 +164,8 @@
             best = jnp.maximum(best, jnp.max(similar, axis=0, keepdims=True))
         columns.append(best)
     best = jnp.concatenate(columns, axis=1)
-    spread = jnp.where(iota((N_FINE, SLOTS), 1) // CAP == iota((N_FINE, SLOTS), 0), best, 0.0)
-    fold = (iota((SLOTS, CAP), 0) % CAP == iota((SLOTS, CAP), 1)).astype(F32)
-    out_ref[...] = high(spread, fold)
+    for source in range(N_FINE):
+        out_ref[source:source + 1, :] = best[:, source * CAP:(source + 1) * CAP]
 
 
 def pick_body(label_ref, slot_ref, best_ref, out_ref):
@@ -194,10 +190,14 @@
         specs=(pl.BlockSpec(memory_space=pltpu.HBM),),
     )(pltpu.with_memory_space_constraint(embeddings, pltpu.HBM))
     both = lax.all_gather(strips, "c", axis=0, tiled=True)
-    strips = call(
-        halve_body, jax.ShapeDtypeStruct((HALF, STRIP), BF16), D * STRIP, 1 << 20, name="halve",
-        specs=(SMEM, VMEM),
-    )(lax.axis_index("c").reshape(1), both)
+    at = lax.axis_index("c") * HALF
+    strips = sum(
+        lax.dynamic_slice(
+            both, (start, 0), (HALF, STRIP), allow_negative_indices=False
+        ).astype(F32)
+        for start in (at, at + D)
+    )
+    strips = (strips * CHIP_SHRINK).astype(F16)
     parts = swap(strips.reshape(N_PLANE // 2, STRIP_ROWS, STRIP), FLAT)
 
     outgoing, slot = call(
@@ -210,7 +210,7 @@
     )(label, embeddings)
     received = swap(outgoing.reshape(N_FINE, CAP, D), FINE).reshape(SLOTS, D)
 
-    strip = (jnp.sum(parts.astype(F32), axis=0) * SHRINK).astype(jnp.float16)
+    strip = (jnp.sum(parts.astype(F32), axis=0) * (SHRINK / CHIP_SHRINK)).astype(F16)
     layers = swap(jnp.broadcast_to(strip, (N_Z, STRIP_ROWS, STRIP)), "z")
     strip = jnp.sum(layers.astype(F32), axis=0) * (1.0 / SHRINK)
     for axes, differs, _ in DOUBLING:

time: 141 us -> 141 us (level)
  no operation moved by 1% of the time
where the time goes in v7:
time: 141 us; the launch traced here: 140 us
  blocking collectives  52.5 us (37%)
  starting transfers between devices  41.6 us (30%)
  waiting for transfers between devices  32.7 us (23%)
  Pallas kernels  12.3 us (9%)
    all_to_all x2, blocking collectives, swap(): return lax.all_to_all(value, axes, split_axis=0, concat_axis=0, tiled=True)  36.4 us
    ppermute x6, starting transfers between devices, per_device(): other = lax.ppermute(strip, axes, [(i, i ^ differs) for i in range(size)])  21.4 us
    ppermute x6, waiting for transfers between devices, per_device(): other = lax.ppermute(strip, axes, [(i, i ^ differs) for i in range(size)])  20.2 us
    all_to_all x2, starting transfers between devices, swap(): return lax.all_to_all(value, axes, split_axis=0, concat_axis=0, tiled=True)  20.2 us
    all_gather x1, blocking collectives, per_device(): both = lax.all_gather(strips, 'c', axis=0, tiled=True)  16.1 us
    all_to_all x2, waiting for transfers between devices, swap(): return lax.all_to_all(value, axes, split_axis=0, concat_axis=0, tiled=True)  12.5 us
    pallas_call x1, Pallas kernels, per_device(): call(root_body, jax.ShapeDtypeStruct((D, D), BF16), 36 * D * D * D, 2 <<...  5.8 us
  transfers between devices with their start and end apart: 8, of which 8 were waited for; matrix products, arithmetic and copies ran while one was open for 0% of the time, Pallas kernels for 6%

profile of v7, /device:TPU:1, one launch (start us, length us, event | category | flops | bytes accessed | tf_op | source)
XLA Modules:
  0.0 140.2 jit_solution(14240503497794955620)
XLA Ops:
  0.0 1.5 %gram.1 = bf16[512,384]{1,0:T(8,128)(2,1)S(1)} custom-call(bf16[512,512]{1,0:T(8,128)(2,1)} %rows_ref.3), custom_call_target="tpu_custom_call" | custom-call | flops 268435456 | bytes 1048576 | tf_op jit(solution)/shard_map/gram/pallas_call | solution.py:187
  1.5 16.1 %all_gather.3 = bf16[1024,384]{1,0:T(8,128)(2,1)S(1)} all-gather(bf16[512,384]{1,0:T(8,128)(2,1)S(1)} %gram.1), channel_id=1, replica_groups=mesh['y'=8,'xh'=2,'xl'=2,'z'=16,'c'=2] {'c'}, dimensions={0}, use_global_device_ids=true | all-gather | bytes 1179648 | tf_op jit(solution)/shard_map/all_gather | solution.py:192
  17.7 0.1 fusion
  17.8 0.0 copy-start.1
  17.8 13.6 %all_to_all.20 = f16[32,8,384]{2,1,0:T(8,128)(2,1)S(1)} all-to-all(f16[32,8,384]{2,1,0:T(8,128)(2,1)S(1)} %fusion), channel_id=1, replica_groups=mesh['y'=8,'xh'=2,'xl'=2,'z'=16,'c'=2] {'y','xh','xl'}, dimensions={0} | all-to-all | bytes 393216 | tf_op jit(solution)/shard_map/all_to_all | solution.py:182
  31.4 0.6 broadcast_in_dim.3
  32.1 0.0 copy-start
  32.1 12.6 %all-to-all-start.2 = ((f16[16,8,384]{2,1,0:T(8,128)(2,1)}), f16[16,8,384]{2,1,0:T(8,128)(2,1)S(1)}, u32[]{:S(2)}, u32[]{:S(2)}) async-start(f16[16,8,384]{2,1,0:T(8,128)(2,1)} %broadcast_in_dim.3), calls=%async_computation.2 | async-start | bytes 196608 | tf_op jit(solution)/shard_map/all_to_all | solution.py:182
  44.7 0.0 copy-done.1
  44.7 0.0 copy-done
  44.8 2.2 %pack.1 = (bf16[1024,512]{1,0:T(8,128)(2,1)}, s32[1,512]{1,0:T(1,128)S(1)}) custom-call(s32[1,512]{1,0:T(1,128)S(1)} %bitcast.14, bf16[512,512]{1,0:T(8,128)(2,1)S(1)} %copy-done.1), custom_call_target="tpu_custom_call" | custom-call | flops 536870912 | bytes 2097152 | tf_op jit(solution)/shard_map/pack/pallas_call | solution.py:203
  46.9 9.7 %all-to-all-done.2 = f16[16,8,384]{2,1,0:T(8,128)(2,1)S(1)} async-done(((f16[16,8,384]{2,1,0:T(8,128)(2,1)}), f16[16,8,384]{2,1,0:T(8,128)(2,1)S(1)}, u32[]{:S(2)}, u32[]{:S(2)}) %all-to-all-start.2) | async-done | bytes 98336 | tf_op jit(solution)/shard_map/all_to_all | solution.py:182
  56.6 7.5 %all-to-all-start = ((bf16[64,16,512]{2,1,0:T(8,128)(2,1)}), bf16[64,16,512]{2,1,0:T(8,128)(2,1)S(1)}, u32[]{:S(2)}, u32[]{:S(2)}) async-start(bf16[64,16,512]{2,1,0:T(8,128)(2,1)} %bitcast.1), calls=%async_computation | async-start | bytes 2097152 | tf_op jit(solution)/shard_map/all_to_all | solution.py:182
  64.2 2.7 %collective-permute-start = (f32[8,384]{1,0:T(8,128)S(1)}, f32[8,384]{1,0:T(8,128)S(1)}, u32[]{:S(2)}, u32[]{:S(2)}) collective-permute-start(f32[8,384]{1,0:T(8,128)S(1)} %get-tuple-element.19), channel_id=1, source_target_pairs={{0,128},{128,0},{256,384},{384,256},{512,640},{640,512},{768,896},... | collective-permute-start | bytes 36872 | tf_op jit(solution)/shard_map/ppermute | solution.py:218
  66.9 2.0 %collective-permute-done = f32[8,384]{1,0:T(8,128)S(1)} collective-permute-done((f32[8,384]{1,0:T(8,128)S(1)}, f32[8,384]{1,0:T(8,128)S(1)}, u32[]{:S(2)}, u32[]{:S(2)}) %collective-permute-start) | collective-permute-done | bytes 12320 | tf_op jit(solution)/shard_map/ppermute | solution.py:218
  68.9 2.9 %collective-permute-start.1 = (f32[16,384]{1,0:T(8,128)S(1)}, f32[16,384]{1,0:T(8,128)S(1)}, u32[]{:S(2)}, u32[]{:S(2)}) collective-permute-start(f32[16,384]{1,0:T(8,128)S(1)} %pad_maximum_fusion.2), channel_id=1, source_target_pairs={{0,256},{128,384},{256,0},{384,128},{512,768},{640,896},{768,512},... | collective-permute-start | bytes 73736 | tf_op jit(solution)/shard_map/ppermute | solution.py:218
  71.8 2.8 %collective-permute-done.1 = f32[16,384]{1,0:T(8,128)S(1)} collective-permute-done((f32[16,384]{1,0:T(8,128)S(1)}, f32[16,384]{1,0:T(8,128)S(1)}, u32[]{:S(2)}, u32[]{:S(2)}) %collective-permute-start.1) | collective-permute-done | bytes 24608 | tf_op jit(solution)/shard_map/ppermute | solution.py:218
  74.6 3.0 %collective-permute-start.2 = (f32[32,384]{1,0:T(8,128)S(1)}, f32[32,384]{1,0:T(8,128)S(1)}, u32[]{:S(2)}, u32[]{:S(2)}) collective-permute-start(f32[32,384]{1,0:T(8,128)S(1)} %pad_maximum_fusion.1), channel_id=1, source_target_pairs={{0,512},{128,640},{256,768},{384,896},{512,0},{640,128},{768,256},... | collective-permute-start | bytes 147464 | tf_op jit(solution)/shard_map/ppermute | solution.py:218
  77.7 6.0 %collective-permute-done.2 = f32[32,384]{1,0:T(8,128)S(1)} collective-permute-done((f32[32,384]{1,0:T(8,128)S(1)}, f32[32,384]{1,0:T(8,128)S(1)}, u32[]{:S(2)}, u32[]{:S(2)}) %collective-permute-start.2) | collective-permute-done | bytes 49184 | tf_op jit(solution)/shard_map/ppermute | solution.py:218
  83.7 4.0 %collective-permute-start.3 = (f32[64,384]{1,0:T(8,128)S(1)}, f32[64,384]{1,0:T(8,128)S(1)}, u32[]{:S(2)}, u32[]{:S(2)}) collective-permute-start(f32[64,384]{1,0:T(8,128)S(1)} %pad_maximum_fusion), channel_id=1, source_target_pairs={{0,96},{32,64},{64,32},{96,0},{1,97},{33,65},{65,33},{97,1},{2,98}... | collective-permute-start | bytes 294920 | tf_op jit(solution)/shard_map/ppermute | solution.py:218
  87.7 2.9 %collective-permute-done.3 = f32[64,384]{1,0:T(8,128)S(1)} collective-permute-done((f32[64,384]{1,0:T(8,128)S(1)}, f32[64,384]{1,0:T(8,128)S(1)}, u32[]{:S(2)}, u32[]{:S(2)}) %collective-permute-start.3) | collective-permute-done | bytes 98336 | tf_op jit(solution)/shard_map/ppermute | solution.py:218
  90.6 2.3 %collective-permute-start.4 = (f32[128,384]{1,0:T(8,128)S(1)}, f32[128,384]{1,0:T(8,128)S(1)}, u32[]{:S(2)}, u32[]{:S(2)}) collective-permute-start(f32[128,384]{1,0:T(8,128)S(1)} %get-tuple-element.9), channel_id=1, source_target_pairs={{0,32},{32,0},{1,33},{33,1},{2,34},{34,2},{3,35},{35,3},{4,36},{36... | collective-permute-start | bytes 589832 | tf_op jit(solution)/shard_map/ppermute | solution.py:218
  92.9 5.2 %collective-permute-done.4 = f32[128,384]{1,0:T(8,128)S(1)} collective-permute-done((f32[128,384]{1,0:T(8,128)S(1)}, f32[128,384]{1,0:T(8,128)S(1)}, u32[]{:S(2)}, u32[]{:S(2)}) %collective-permute-start.4) | collective-permute-done | bytes 196640 | tf_op jit(solution)/shard_map/ppermute | solution.py:218
  98.1 6.5 %collective-permute-start.5 = (f32[256,384]{1,0:T(8,128)S(1)}, f32[256,384]{1,0:T(8,128)S(1)}, u32[]{:S(2)}, u32[]{:S(2)}) collective-permute-start(f32[256,384]{1,0:T(8,128)S(1)} %constant_dynamic-update-slice_fusion.5.near_ref), channel_id=1, source_target_pairs={{0,1},{1,0},{2,3},{3,2},{4,5},{5,4},{6,7},{7,6},{8,9},{9,8},{10,11... | collective-permute-start | bytes 1179656 | tf_op jit(solution)/shard_map/ppermute | solution.py:218
  104.6 1.3 collective-permute-done.5.far_ref
  105.9 5.8 %root.1.whiten_ref = bf16[512,512]{1,0:T(8,128)(2,1)S(1)} custom-call(s32[1]{0:T(128)} %bitcast.3.me_ref, f32[256,384]{1,0:T(8,128)S(1)} %constant_dynamic-update-slice_fusion.5.near_ref, f32[256,384]{1,0:T(8,128)S(1)} %collective-permute-done.5.far_ref), custom_call_target="tpu_custom_call" | custom-call | flops 4831838208 | bytes 2097152 | tf_op jit(solution)/shard_map/root/pallas_call | solution.py:220
  111.7 2.8 %all-to-all-done = bf16[64,16,512]{2,1,0:T(8,128)(2,1)S(1)} async-done(((bf16[64,16,512]{2,1,0:T(8,128)(2,1)}), bf16[64,16,512]{2,1,0:T(8,128)(2,1)S(1)}, u32[]{:S(2)}, u32[]{:S(2)}) %all-to-all-start) | async-done | bytes 1048608 | tf_op jit(solution)/shard_map/all_to_all | solution.py:182
  114.6 2.0 %best.1 = f32[64,16]{1,0:T(8,128)S(1)} custom-call(bf16[1024,512]{1,0:T(8,128)(2,1)S(1)} %bitcast.11, bf16[512,512]{1,0:T(8,128)(2,1)S(1)} %root.1.whiten_ref), custom_call_target="tpu_custom_call" | custom-call | flops 1610612736 | bytes 2097152 | tf_op jit(solution)/shard_map/best/pallas_call | solution.py:226
  116.6 22.7 %all_to_all.21 = f32[64,1,16]{2,1,0:T(1,128)S(1)} all-to-all(f32[64,1,16]{2,1,0:T(1,128)S(1)} %bitcast.13), channel_id=1, replica_groups=mesh['y'=8,'xh'=2,'xl'=2,'z'=16,'c'=2] {'xl','z','c'}, dimensions={0} | all-to-all | bytes 8192 | tf_op jit(solution)/shard_map/all_to_all | solution.py:182
  139.3 0.8 pick.1
  (12 shorter events, 0.1 us)
Async XLA Ops:
  17.8 27.0 %copy-start.1 = (bf16[512,512]{1,0:T(8,128)(2,1)S(1)}, bf16[512,512]{1,0:T(8,128)(2,1)}, u32[]{:S(2)}) copy-start(bf16[512,512]{1,0:T(8,128)(2,1)} %rows_ref.3) | copy-start | bytes 1572868
  32.1 12.7 %copy-start = (s32[512,1]{0,1:T(1,128)S(1)}, s32[512,1]{0,1:T(1,128)}, u32[]{:S(2)}) copy-start(s32[512,1]{0,1:T(1,128)} %param.3) | copy-start | bytes 6148
  32.1 24.5 %all-to-all-start.2 = ((f16[16,8,384]{2,1,0:T(8,128)(2,1)}), f16[16,8,384]{2,1,0:T(8,128)(2,1)S(1)}, u32[]{:S(2)}, u32[]{:S(2)}) async-start(f16[16,8,384]{2,1,0:T(8,128)(2,1)} %broadcast_in_dim.3), calls=%async_computation.2 | async-start | bytes 196608 | tf_op jit(solution)/shard_map/all_to_all | solution.py:182
  56.6 58.0 %all-to-all-start = ((bf16[64,16,512]{2,1,0:T(8,128)(2,1)}), bf16[64,16,512]{2,1,0:T(8,128)(2,1)S(1)}, u32[]{:S(2)}, u32[]{:S(2)}) async-start(bf16[64,16,512]{2,1,0:T(8,128)(2,1)} %bitcast.1), calls=%async_computation | async-start | bytes 2097152 | tf_op jit(solution)/shard_map/all_to_all | solution.py:182
  64.2 4.7 %collective-permute-start = (f32[8,384]{1,0:T(8,128)S(1)}, f32[8,384]{1,0:T(8,128)S(1)}, u32[]{:S(2)}, u32[]{:S(2)}) collective-permute-start(f32[8,384]{1,0:T(8,128)S(1)} %get-tuple-element.19), channel_id=1, source_target_pairs={{0,128},{128,0},{256,384},{384,256},{512,640},{640,512},{768,896},... | collective-permute-start | bytes 36872 | tf_op jit(solution)/shard_map/ppermute | solution.py:218
  68.9 5.8 %collective-permute-start.1 = (f32[16,384]{1,0:T(8,128)S(1)}, f32[16,384]{1,0:T(8,128)S(1)}, u32[]{:S(2)}, u32[]{:S(2)}) collective-permute-start(f32[16,384]{1,0:T(8,128)S(1)} %pad_maximum_fusion.2), channel_id=1, source_target_pairs={{0,256},{128,384},{256,0},{384,128},{512,768},{640,896},{768,512},... | collective-permute-start | bytes 73736 | tf_op jit(solution)/shard_map/ppermute | solution.py:218
  74.6 9.0 %collective-permute-start.2 = (f32[32,384]{1,0:T(8,128)S(1)}, f32[32,384]{1,0:T(8,128)S(1)}, u32[]{:S(2)}, u32[]{:S(2)}) collective-permute-start(f32[32,384]{1,0:T(8,128)S(1)} %pad_maximum_fusion.1), channel_id=1, source_target_pairs={{0,512},{128,640},{256,768},{384,896},{512,0},{640,128},{768,256},... | collective-permute-start | bytes 147464 | tf_op jit(solution)/shard_map/ppermute | solution.py:218
  83.7 6.9 %collective-permute-start.3 = (f32[64,384]{1,0:T(8,128)S(1)}, f32[64,384]{1,0:T(8,128)S(1)}, u32[]{:S(2)}, u32[]{:S(2)}) collective-permute-start(f32[64,384]{1,0:T(8,128)S(1)} %pad_maximum_fusion), channel_id=1, source_target_pairs={{0,96},{32,64},{64,32},{96,0},{1,97},{33,65},{65,33},{97,1},{2,98}... | collective-permute-start | bytes 294920 | tf_op jit(solution)/shard_map/ppermute | solution.py:218
  90.6 7.5 %collective-permute-start.4 = (f32[128,384]{1,0:T(8,128)S(1)}, f32[128,384]{1,0:T(8,128)S(1)}, u32[]{:S(2)}, u32[]{:S(2)}) collective-permute-start(f32[128,384]{1,0:T(8,128)S(1)} %get-tuple-element.9), channel_id=1, source_target_pairs={{0,32},{32,0},{1,33},{33,1},{2,34},{34,2},{3,35},{35,3},{4,36},{36... | collective-permute-start | bytes 589832 | tf_op jit(solution)/shard_map/ppermute | solution.py:218
  98.1 7.8 %collective-permute-start.5 = (f32[256,384]{1,0:T(8,128)S(1)}, f32[256,384]{1,0:T(8,128)S(1)}, u32[]{:S(2)}, u32[]{:S(2)}) collective-permute-start(f32[256,384]{1,0:T(8,128)S(1)} %constant_dynamic-update-slice_fusion.5.near_ref), channel_id=1, source_target_pairs={{0,1},{1,0},{2,3},{3,2},{4,5},{5,4},{6,7},{7,6},{8,9},{9,8},{10,11... | collective-permute-start | bytes 1179656 | tf_op jit(solution)/shard_map/ppermute | solution.py:218

commit v8 on v7

--- a/solution.py
+++ b/solution.py
@@ -142,13 +142,11 @@
 
 
 def best_body(rows_ref, whiten_ref, out_ref):
-    rows = rows_ref[...].astype(F32)
-    present = rows == rows
-    clean = jnp.where(present, rows, 0.0).astype(BF16)
-    whitened = jnp.dot(clean, whiten_ref[...], preferred_element_type=F32)
+    present = rows_ref[:, :BLOCK].astype(F32)[:, :1]
+    present = present == present
+    whitened = jnp.dot(rows_ref[...], whiten_ref[...], preferred_element_type=F32)
     meansq = jnp.mean(whitened * whitened, axis=-1, keepdims=True)
     unit = (whitened * lax.rsqrt(D * (meansq + EPS))).astype(BF16)
-    bias = jnp.where(present[:, :1], 0.0, -4.0)
     tile = 256
     own = iota((tile, tile), 0) == iota((tile, tile), 1)
     columns = []
@@ -158,12 +156,15 @@
             similar = lax.dot_general(
                 unit[b * tile:(b + 1) * tile], unit[c * tile:(c + 1) * tile],
                 (((1,), (1,)), ((), ())), preferred_element_type=F32,
-            ) + bias[b * tile:(b + 1) * tile]
+            )
+            keep = present[b * tile:(b + 1) * tile]
             if b == c:
-                similar = jnp.where(own, -1.0, similar)
+                keep = keep & jnp.logical_not(own)
+            similar = jnp.where(keep, similar, -1.0)
             best = jnp.maximum(best, jnp.max(similar, axis=0, keepdims=True))
         columns.append(best)
     best = jnp.concatenate(columns, axis=1)
+    best = jnp.where(best == best, best, -1.0)
     for source in range(N_FINE):
         out_ref[source:source + 1, :] = best[:, source * CAP:(source + 1) * CAP]
 
@@ -208,6 +209,7 @@
         ),
         2 * SLOTS * ROW_DEV * D, 2 << 20, name="pack",
     )(label, embeddings)
+    parts, outgoing = lax.optimization_barrier((parts, outgoing))
     received = swap(outgoing.reshape(N_FINE, CAP, D), FINE).reshape(SLOTS, D)
 
     strip = (jnp.sum(parts.astype(F32), axis=0) * (SHRINK / CHIP_SHRINK)).astype(F16)

time: 141 us -> 141 us (level)
  blocking collectives: 52.5 us -> 62.4 us
  starting transfers between devices: 41.6 us -> 32.9 us
    all_to_all x2, blocking collectives: 36.4 us -> 46.2 us  [swap(): return lax.all_to_all(value, axes, split_axis=0, concat_axis=0, tiled=True)]
    all_to_all x2, starting transfers between devices: 20.2 us -> 11.5 us  [swap(): return lax.all_to_all(value, axes, split_axis=0, concat_axis=0, tiled=True)]
where the time goes in v8:
time: 141 us; the launch traced here: 140 us
  blocking collectives  62.4 us (44%)
  starting transfers between devices  32.9 us (23%)
  waiting for transfers between devices  31.3 us (22%)
  Pallas kernels  12.3 us (9%)
    all_to_all x2, blocking collectives, swap(): return lax.all_to_all(value, axes, split_axis=0, concat_axis=0, tiled=True)  46.2 us
    ppermute x6, starting transfers between devices, per_device(): other = lax.ppermute(strip, axes, [(i, i ^ differs) for i in range(size)])  21.4 us
    ppermute x6, waiting for transfers between devices, per_device(): other = lax.ppermute(strip, axes, [(i, i ^ differs) for i in range(size)])  20.2 us
    all_gather x1, blocking collectives, per_device(): both = lax.all_gather(strips, 'c', axis=0, tiled=True)  16.1 us
    all_to_all x2, starting transfers between devices, swap(): return lax.all_to_all(value, axes, split_axis=0, concat_axis=0, tiled=True)  11.5 us
    all_to_all x2, waiting for transfers between devices, swap(): return lax.all_to_all(value, axes, split_axis=0, concat_axis=0, tiled=True)  11.1 us
    pallas_call x1, Pallas kernels, per_device(): call(root_body, jax.ShapeDtypeStruct((D, D), BF16), 36 * D * D * D, 2 <<...  5.8 us
  transfers between devices with their start and end apart: 8, of which 8 were waited for; matrix products, arithmetic and copies ran while one was open for 0% of the time, Pallas kernels for 6%

profile of v8, /device:TPU:1, one launch (start us, length us, event | category | flops | bytes accessed | tf_op | source)
XLA Modules:
  0.0 140.1 jit_solution(4075669209835567758)
XLA Ops:
  0.0 1.5 %gram.1 = bf16[512,384]{1,0:T(8,128)(2,1)S(1)} custom-call(bf16[512,512]{1,0:T(8,128)(2,1)} %rows_ref.3), custom_call_target="tpu_custom_call" | custom-call | flops 268435456 | bytes 1048576 | tf_op jit(solution)/shard_map/gram/pallas_call | solution.py:188
  1.5 16.1 %all_gather.3 = bf16[1024,384]{1,0:T(8,128)(2,1)S(1)} all-gather(bf16[512,384]{1,0:T(8,128)(2,1)S(1)} %gram.1), channel_id=1, replica_groups=mesh['y'=8,'xh'=2,'xl'=2,'z'=16,'c'=2] {'c'}, dimensions={0}, use_global_device_ids=true | all-gather | bytes 1179648 | tf_op jit(solution)/shard_map/all_gather | solution.py:193
  17.7 0.0 copy-start.1
  17.7 0.8 fusion
  18.4 0.0 copy-start
  18.4 4.0 %all-to-all-start = ((f16[32,8,384]{2,1,0:T(8,128)(2,1)}), f16[32,8,384]{2,1,0:T(8,128)(2,1)S(1)}, u32[]{:S(2)}, u32[]{:S(2)}) async-start(f16[32,8,384]{2,1,0:T(8,128)(2,1)} %fusion), calls=%async_computation | async-start | bytes 393216 | tf_op jit(solution)/shard_map/all_to_all | solution.py:183
  22.4 0.0 copy-done.1
  22.4 0.0 copy-done
  22.5 2.2 %pack.1 = (bf16[1024,512]{1,0:T(8,128)(2,1)}, s32[1,512]{1,0:T(1,128)S(1)}) custom-call(s32[1,512]{1,0:T(1,128)S(1)} %bitcast.14, bf16[512,512]{1,0:T(8,128)(2,1)S(1)} %copy-done.1), custom_call_target="tpu_custom_call" | custom-call | flops 536870912 | bytes 2097152 | tf_op jit(solution)/shard_map/pack/pallas_call | solution.py:204
  24.6 8.3 %all-to-all-done = f16[32,8,384]{2,1,0:T(8,128)(2,1)S(1)} async-done(((f16[32,8,384]{2,1,0:T(8,128)(2,1)}), f16[32,8,384]{2,1,0:T(8,128)(2,1)S(1)}, u32[]{:S(2)}, u32[]{:S(2)}) %all-to-all-start) | async-done | bytes 196640 | tf_op jit(solution)/shard_map/all_to_all | solution.py:183
  33.0 23.5 %all_to_all.20 = f16[16,8,384]{2,1,0:T(8,128)(2,1)S(1)} all-to-all(f16[16,8,384]{2,1,0:T(8,128)(2,1)S(1)} %broadcast_in_dim.3), channel_id=1, replica_groups=mesh['y'=8,'xh'=2,'xl'=2,'z'=16,'c'=2] {'z'}, dimensions={0} | all-to-all | bytes 196608 | tf_op jit(solution)/shard_map/all_to_all | solution.py:183
  56.5 7.5 %all-to-all-start.1 = ((bf16[64,16,512]{2,1,0:T(8,128)(2,1)}), bf16[64,16,512]{2,1,0:T(8,128)(2,1)S(1)}, u32[]{:S(2)}, u32[]{:S(2)}) async-start(bf16[64,16,512]{2,1,0:T(8,128)(2,1)} %bitcast.2), calls=%async_computation.1 | async-start | bytes 2097152 | tf_op jit(solution)/shard_map/all_to_all | solution.py:183
  64.1 2.7 %collective-permute-start = (f32[8,384]{1,0:T(8,128)S(1)}, f32[8,384]{1,0:T(8,128)S(1)}, u32[]{:S(2)}, u32[]{:S(2)}) collective-permute-start(f32[8,384]{1,0:T(8,128)S(1)} %get-tuple-element.23), channel_id=1, source_target_pairs={{0,128},{128,0},{256,384},{384,256},{512,640},{640,512},{768,896},... | collective-permute-start | bytes 36872 | tf_op jit(solution)/shard_map/ppermute | solution.py:220
  66.8 2.0 %collective-permute-done = f32[8,384]{1,0:T(8,128)S(1)} collective-permute-done((f32[8,384]{1,0:T(8,128)S(1)}, f32[8,384]{1,0:T(8,128)S(1)}, u32[]{:S(2)}, u32[]{:S(2)}) %collective-permute-start) | collective-permute-done | bytes 12320 | tf_op jit(solution)/shard_map/ppermute | solution.py:220
  68.8 2.9 %collective-permute-start.1 = (f32[16,384]{1,0:T(8,128)S(1)}, f32[16,384]{1,0:T(8,128)S(1)}, u32[]{:S(2)}, u32[]{:S(2)}) collective-permute-start(f32[16,384]{1,0:T(8,128)S(1)} %pad_maximum_fusion.2), channel_id=1, source_target_pairs={{0,256},{128,384},{256,0},{384,128},{512,768},{640,896},{768,512},... | collective-permute-start | bytes 73736 | tf_op jit(solution)/shard_map/ppermute | solution.py:220
  71.7 2.8 %collective-permute-done.1 = f32[16,384]{1,0:T(8,128)S(1)} collective-permute-done((f32[16,384]{1,0:T(8,128)S(1)}, f32[16,384]{1,0:T(8,128)S(1)}, u32[]{:S(2)}, u32[]{:S(2)}) %collective-permute-start.1) | collective-permute-done | bytes 24608 | tf_op jit(solution)/shard_map/ppermute | solution.py:220
  74.6 3.0 %collective-permute-start.2 = (f32[32,384]{1,0:T(8,128)S(1)}, f32[32,384]{1,0:T(8,128)S(1)}, u32[]{:S(2)}, u32[]{:S(2)}) collective-permute-start(f32[32,384]{1,0:T(8,128)S(1)} %pad_maximum_fusion.1), channel_id=1, source_target_pairs={{0,512},{128,640},{256,768},{384,896},{512,0},{640,128},{768,256},... | collective-permute-start | bytes 147464 | tf_op jit(solution)/shard_map/ppermute | solution.py:220
  77.6 6.0 %collective-permute-done.2 = f32[32,384]{1,0:T(8,128)S(1)} collective-permute-done((f32[32,384]{1,0:T(8,128)S(1)}, f32[32,384]{1,0:T(8,128)S(1)}, u32[]{:S(2)}, u32[]{:S(2)}) %collective-permute-start.2) | collective-permute-done | bytes 49184 | tf_op jit(solution)/shard_map/ppermute | solution.py:220
  83.6 4.0 %collective-permute-start.3 = (f32[64,384]{1,0:T(8,128)S(1)}, f32[64,384]{1,0:T(8,128)S(1)}, u32[]{:S(2)}, u32[]{:S(2)}) collective-permute-start(f32[64,384]{1,0:T(8,128)S(1)} %pad_maximum_fusion), channel_id=1, source_target_pairs={{0,96},{32,64},{64,32},{96,0},{1,97},{33,65},{65,33},{97,1},{2,98}... | collective-permute-start | bytes 294920 | tf_op jit(solution)/shard_map/ppermute | solution.py:220
  87.6 2.9 %collective-permute-done.3 = f32[64,384]{1,0:T(8,128)S(1)} collective-permute-done((f32[64,384]{1,0:T(8,128)S(1)}, f32[64,384]{1,0:T(8,128)S(1)}, u32[]{:S(2)}, u32[]{:S(2)}) %collective-permute-start.3) | collective-permute-done | bytes 98336 | tf_op jit(solution)/shard_map/ppermute | solution.py:220
  90.5 2.3 %collective-permute-start.4 = (f32[128,384]{1,0:T(8,128)S(1)}, f32[128,384]{1,0:T(8,128)S(1)}, u32[]{:S(2)}, u32[]{:S(2)}) collective-permute-start(f32[128,384]{1,0:T(8,128)S(1)} %get-tuple-element.13), channel_id=1, source_target_pairs={{0,32},{32,0},{1,33},{33,1},{2,34},{34,2},{3,35},{35,3},{4,36},{36... | collective-permute-start | bytes 589832 | tf_op jit(solution)/shard_map/ppermute | solution.py:220
  92.8 5.2 %collective-permute-done.4 = f32[128,384]{1,0:T(8,128)S(1)} collective-permute-done((f32[128,384]{1,0:T(8,128)S(1)}, f32[128,384]{1,0:T(8,128)S(1)}, u32[]{:S(2)}, u32[]{:S(2)}) %collective-permute-start.4) | collective-permute-done | bytes 196640 | tf_op jit(solution)/shard_map/ppermute | solution.py:220
  98.0 6.5 %collective-permute-start.5 = (f32[256,384]{1,0:T(8,128)S(1)}, f32[256,384]{1,0:T(8,128)S(1)}, u32[]{:S(2)}, u32[]{:S(2)}) collective-permute-start(f32[256,384]{1,0:T(8,128)S(1)} %constant_dynamic-update-slice_fusion.5.near_ref), channel_id=1, source_target_pairs={{0,1},{1,0},{2,3},{3,2},{4,5},{5,4},{6,7},{7,6},{8,9},{9,8},{10,11... | collective-permute-start | bytes 1179656 | tf_op jit(solution)/shard_map/ppermute | solution.py:220
  104.5 1.3 collective-permute-done.5.far_ref
  105.9 5.8 %root.1.whiten_ref = bf16[512,512]{1,0:T(8,128)(2,1)S(1)} custom-call(s32[1]{0:T(128)} %bitcast.4.me_ref, f32[256,384]{1,0:T(8,128)S(1)} %constant_dynamic-update-slice_fusion.5.near_ref, f32[256,384]{1,0:T(8,128)S(1)} %collective-permute-done.5.far_ref), custom_call_target="tpu_custom_call" | custom-call | flops 4831838208 | bytes 2097152 | tf_op jit(solution)/shard_map/root/pallas_call | solution.py:222
  111.7 2.8 %all-to-all-done.1 = bf16[64,16,512]{2,1,0:T(8,128)(2,1)S(1)} async-done(((bf16[64,16,512]{2,1,0:T(8,128)(2,1)}), bf16[64,16,512]{2,1,0:T(8,128)(2,1)S(1)}, u32[]{:S(2)}, u32[]{:S(2)}) %all-to-all-start.1) | async-done | bytes 1048608 | tf_op jit(solution)/shard_map/all_to_all | solution.py:183
  114.5 2.0 %best.1 = f32[64,16]{1,0:T(8,128)S(1)} custom-call(bf16[1024,512]{1,0:T(8,128)(2,1)S(1)} %bitcast.11, bf16[512,512]{1,0:T(8,128)(2,1)S(1)} %root.1.whiten_ref), custom_call_target="tpu_custom_call" | custom-call | flops 1610612736 | bytes 2097152 | tf_op jit(solution)/shard_map/best/pallas_call | solution.py:228
  116.5 22.7 %all_to_all.21 = f32[64,1,16]{2,1,0:T(1,128)S(1)} all-to-all(f32[64,1,16]{2,1,0:T(1,128)S(1)} %bitcast.13), channel_id=1, replica_groups=mesh['y'=8,'xh'=2,'xl'=2,'z'=16,'c'=2] {'xl','z','c'}, dimensions={0} | all-to-all | bytes 8192 | tf_op jit(solution)/shard_map/all_to_all | solution.py:183
  139.2 0.8 pick.1
  (13 shorter events, 0.2 us)
Async XLA Ops:
  17.7 4.8 %copy-start.1 = (bf16[512,512]{1,0:T(8,128)(2,1)S(1)}, bf16[512,512]{1,0:T(8,128)(2,1)}, u32[]{:S(2)}) copy-start(bf16[512,512]{1,0:T(8,128)(2,1)} %rows_ref.3) | copy-start | bytes 1572868
  18.4 4.0 %copy-start = (s32[512,1]{0,1:T(1,128)S(1)}, s32[512,1]{0,1:T(1,128)}, u32[]{:S(2)}) copy-start(s32[512,1]{0,1:T(1,128)} %param.3) | copy-start | bytes 6148
  18.4 14.5 %all-to-all-start = ((f16[32,8,384]{2,1,0:T(8,128)(2,1)}), f16[32,8,384]{2,1,0:T(8,128)(2,1)S(1)}, u32[]{:S(2)}, u32[]{:S(2)}) async-start(f16[32,8,384]{2,1,0:T(8,128)(2,1)} %fusion), calls=%async_computation | async-start | bytes 393216 | tf_op jit(solution)/shard_map/all_to_all | solution.py:183
  56.5 58.0 %all-to-all-start.1 = ((bf16[64,16,512]{2,1,0:T(8,128)(2,1)}), bf16[64,16,512]{2,1,0:T(8,128)(2,1)S(1)}, u32[]{:S(2)}, u32[]{:S(2)}) async-start(bf16[64,16,512]{2,1,0:T(8,128)(2,1)} %bitcast.2), calls=%async_computation.1 | async-start | bytes 2097152 | tf_op jit(solution)/shard_map/all_to_all | solution.py:183
  64.1 4.7 %collective-permute-start = (f32[8,384]{1,0:T(8,128)S(1)}, f32[8,384]{1,0:T(8,128)S(1)}, u32[]{:S(2)}, u32[]{:S(2)}) collective-permute-start(f32[8,384]{1,0:T(8,128)S(1)} %get-tuple-element.23), channel_id=1, source_target_pairs={{0,128},{128,0},{256,384},{384,256},{512,640},{640,512},{768,896},... | collective-permute-start | bytes 36872 | tf_op jit(solution)/shard_map/ppermute | solution.py:220
  68.8 5.8 %collective-permute-start.1 = (f32[16,384]{1,0:T(8,128)S(1)}, f32[16,384]{1,0:T(8,128)S(1)}, u32[]{:S(2)}, u32[]{:S(2)}) collective-permute-start(f32[16,384]{1,0:T(8,128)S(1)} %pad_maximum_fusion.2), channel_id=1, source_target_pairs={{0,256},{128,384},{256,0},{384,128},{512,768},{640,896},{768,512},... | collective-permute-start | bytes 73736 | tf_op jit(solution)/shard_map/ppermute | solution.py:220
  74.6 9.0 %collective-permute-start.2 = (f32[32,384]{1,0:T(8,128)S(1)}, f32[32,384]{1,0:T(8,128)S(1)}, u32[]{:S(2)}, u32[]{:S(2)}) collective-permute-start(f32[32,384]{1,0:T(8,128)S(1)} %pad_maximum_fusion.1), channel_id=1, source_target_pairs={{0,512},{128,640},{256,768},{384,896},{512,0},{640,128},{768,256},... | collective-permute-start | bytes 147464 | tf_op jit(solution)/shard_map/ppermute | solution.py:220
  83.6 6.9 %collective-permute-start.3 = (f32[64,384]{1,0:T(8,128)S(1)}, f32[64,384]{1,0:T(8,128)S(1)}, u32[]{:S(2)}, u32[]{:S(2)}) collective-permute-start(f32[64,384]{1,0:T(8,128)S(1)} %pad_maximum_fusion), channel_id=1, source_target_pairs={{0,96},{32,64},{64,32},{96,0},{1,97},{33,65},{65,33},{97,1},{2,98}... | collective-permute-start | bytes 294920 | tf_op jit(solution)/shard_map/ppermute | solution.py:220
  90.5 7.5 %collective-permute-start.4 = (f32[128,384]{1,0:T(8,128)S(1)}, f32[128,384]{1,0:T(8,128)S(1)}, u32[]{:S(2)}, u32[]{:S(2)}) collective-permute-start(f32[128,384]{1,0:T(8,128)S(1)} %get-tuple-element.13), channel_id=1, source_target_pairs={{0,32},{32,0},{1,33},{33,1},{2,34},{34,2},{3,35},{35,3},{4,36},{36... | collective-permute-start | bytes 589832 | tf_op jit(solution)/shard_map/ppermute | solution.py:220
  98.0 7.8 %collective-permute-start.5 = (f32[256,384]{1,0:T(8,128)S(1)}, f32[256,384]{1,0:T(8,128)S(1)}, u32[]{:S(2)}, u32[]{:S(2)}) collective-permute-start(f32[256,384]{1,0:T(8,128)S(1)} %constant_dynamic-update-slice_fusion.5.near_ref), channel_id=1, source_target_pairs={{0,1},{1,0},{2,3},{3,2},{4,5},{5,4},{6,7},{7,6},{8,9},{9,8},{10,11... | collective-permute-start | bytes 1179656 | tf_op jit(solution)/shard_map/ppermute | solution.py:220

commit v9 on v7

--- a/solution.py
+++ b/solution.py
@@ -35,12 +35,11 @@
 SHRINK = 2.0 ** -12
 CHIP_SHRINK = 2.0 ** -7
 DOUBLING = (
+    (("y",), 4, 16),
+    (("y",), 2, 8),
     (("y",), 1, 4),
-    (("y",), 2, 8),
-    (("y",), 4, 16),
     (("xh", "xl"), 3, 3),
     (("xl",), 1, 1),
-    (("c",), 1, 32),
 )
 
 F32 = jnp.float32
@@ -108,20 +107,28 @@
         out_ref[:, k * BLOCK:(k + 1) * BLOCK] = jnp.where(filled, part, jnp.nan).astype(BF16)
 
 
-def high(left, right):
-    return jnp.dot(left, right, precision=lax.Precision.HIGHEST, preferred_element_type=F32)
-
-
-def root_body(me_ref, near_ref, far_ref, out_ref, strip_ref, full_ref):
+def parts_of(value):
+    upper = value.astype(BF16)
+    return upper, (value - upper.astype(F32)).astype(BF16)
+
+
+def product(left, right):
+    def dot(a, b):
+        return jnp.dot(a, b, preferred_element_type=F32)
+
+    return dot(left[0], right[0]) + (dot(left[0], right[1]) + dot(left[1], right[0]))
+
+
+def root_body(me_ref, both_ref, out_ref, strip_ref, full_ref):
     half = N_PLANE // 2
     for k in range(N_PLANE):
         differs = 0
         for bit, (_, _, mask) in enumerate(DOUBLING):
             if k >> bit & 1:
                 differs ^= mask
-        source, at = (near_ref, k) if k < half else (far_ref, k - half)
-        to = pl.multiple_of((me_ref[0] ^ differs) * STRIP_ROWS, STRIP_ROWS)
-        strip_ref[pl.ds(to, STRIP_ROWS), :] = source[at * STRIP_ROWS:(at + 1) * STRIP_ROWS, :]
+        to = (me_ref[0] ^ differs) + k // half * half
+        to = pl.multiple_of(to * STRIP_ROWS, STRIP_ROWS)
+        strip_ref[pl.ds(to, STRIP_ROWS), :] = both_ref[k * STRIP_ROWS:(k + 1) * STRIP_ROWS, :]
     for b in range(BLOCKS):
         for k in range(BLOCKS):
             c = (b + k) % BLOCKS
@@ -135,9 +142,10 @@
     norm_scale = jnp.max(jnp.sum(jnp.abs(second), axis=0, keepdims=True), axis=1, keepdims=True)
     root_est = second / norm_scale
     inverse_est = 0.5 * (3.0 * identity - root_est)
-    root_est = high(root_est, inverse_est)
-    newton_step = 0.5 * (3.0 * identity - high(inverse_est, root_est))
-    inverse_est = high(newton_step, inverse_est)
+    first = parts_of(inverse_est)
+    root_est = product(parts_of(root_est), first)
+    newton_step = 0.5 * (3.0 * identity - product(first, parts_of(root_est)))
+    inverse_est = product(parts_of(newton_step), first)
     out_ref[...] = (inverse_est / jnp.sqrt(norm_scale)).astype(BF16)
 
 
@@ -216,12 +224,13 @@
     for axes, differs, _ in DOUBLING:
         size = math.prod(SIZES[AXES.index(axis)] for axis in axes)
         other = lax.ppermute(strip, axes, [(i, i ^ differs) for i in range(size)])
-        near, strip = strip, jnp.concatenate([strip, other], axis=0)
+        strip = jnp.concatenate([strip, other], axis=0)
+    both = lax.all_gather(strip, "c", axis=0, tiled=True)
     whiten_b = call(
-        root_body, jax.ShapeDtypeStruct((D, D), BF16), 36 * D * D * D, 2 << 20,
+        root_body, jax.ShapeDtypeStruct((D, D), BF16), 18 * D * D * D, 2 << 20,
         (pltpu.VMEM((D, STRIP), F32), pltpu.VMEM((D, D), F32)), name="root",
-        specs=(SMEM, VMEM, VMEM),
-    )(lax.axis_index(PLANE).reshape(1), near, other)
+        specs=(SMEM, VMEM),
+    )(lax.axis_index(FLAT).reshape(1), both)
 
     best = call(
         best_body, jax.ShapeDtypeStruct((N_FINE, CAP), F32),

time: 141 us -> 141 us (level)
  blocking collectives: 52.5 us -> 59.1 us
  starting transfers between devices: 41.6 us -> 35.1 us
  Pallas kernels: 12.3 us -> 9.74 us
  waiting for transfers between devices: 32.7 us -> 35.2 us
    all_gather x0 -> x1, blocking collectives: none -> 6.6 us  [per_device(): both = lax.all_gather(strip, 'c', axis=0, tiled=True)]
    ppermute x6 -> x5, starting transfers between devices: 21.4 us -> 14.9 us  [per_device(): other = lax.ppermute(strip, axes, [(i, i ^ differs) for i in range(size)])]
    all_to_all x2, waiting for transfers between devices: 12.5 us -> 16.3 us  [swap(): return lax.all_to_all(value, axes, split_axis=0, concat_axis=0, tiled=True)]
    pallas_call x1, Pallas kernels: 5.8 us -> 3.22 us  [per_device(): call(root_body, jax.ShapeDtypeStruct((D, D), BF16), 18 * D * D * D, 2 <<...]
    ppermute x6 -> x5, waiting for transfers between devices: 20.2 us -> 18.9 us  [per_device(): other = lax.ppermute(strip, axes, [(i, i ^ differs) for i in range(size)])]
  transfers between devices with their start and end apart: 8 -> 7, of which waited for: 8 -> 7; matrix products, arithmetic and copies ran while one was open for 0% -> 0% of each run, Pallas kernels for 6% -> 4%
where the time goes in v9:
time: 141 us; the launch traced here: 140 us
  blocking collectives  59.1 us (42%)
  waiting for transfers between devices  35.2 us (25%)
  starting transfers between devices  35.1 us (25%)
  Pallas kernels  9.74 us (7%)
    all_to_all x2, blocking collectives, swap(): return lax.all_to_all(value, axes, split_axis=0, concat_axis=0, tiled=True)  36.3 us
    all_to_all x2, starting transfers between devices, swap(): return lax.all_to_all(value, axes, split_axis=0, concat_axis=0, tiled=True)  20.2 us
    ppermute x5, waiting for transfers between devices, per_device(): other = lax.ppermute(strip, axes, [(i, i ^ differs) for i in range(size)])  18.9 us
    all_to_all x2, waiting for transfers between devices, swap(): return lax.all_to_all(value, axes, split_axis=0, concat_axis=0, tiled=True)  16.3 us
    all_gather x1, blocking collectives, per_device(): both = lax.all_gather(strips, 'c', axis=0, tiled=True)  16.1 us
    ppermute x5, starting transfers between devices, per_device(): other = lax.ppermute(strip, axes, [(i, i ^ differs) for i in range(size)])  14.9 us
    all_gather x1, blocking collectives, per_device(): both = lax.all_gather(strip, 'c', axis=0, tiled=True)  6.6 us
    pallas_call x1, Pallas kernels, per_device(): call(root_body, jax.ShapeDtypeStruct((D, D), BF16), 18 * D * D * D, 2 <<...  3.22 us
  transfers between devices with their start and end apart: 7, of which 7 were waited for; matrix products, arithmetic and copies ran while one was open for 0% of the time, Pallas kernels for 4%

profile of v9, /device:TPU:1, one launch (start us, length us, event | category | flops | bytes accessed | tf_op | source)
XLA Modules:
  0.0 140.1 jit_solution(13403257468276181118)
XLA Ops:
  0.0 1.5 %gram.1 = bf16[512,384]{1,0:T(8,128)(2,1)S(1)} custom-call(bf16[512,512]{1,0:T(8,128)(2,1)} %rows_ref.3), custom_call_target="tpu_custom_call" | custom-call | flops 268435456 | bytes 1048576 | tf_op jit(solution)/shard_map/gram/pallas_call | solution.py:195
  1.5 16.1 %all_gather.6 = bf16[1024,384]{1,0:T(8,128)(2,1)S(1)} all-gather(bf16[512,384]{1,0:T(8,128)(2,1)S(1)} %gram.1), channel_id=1, replica_groups=mesh['y'=8,'xh'=2,'xl'=2,'z'=16,'c'=2] {'c'}, dimensions={0}, use_global_device_ids=true | all-gather | bytes 1179648 | tf_op jit(solution)/shard_map/all_gather | solution.py:200
  17.7 0.1 fusion
  17.8 0.0 copy-start.1
  17.8 13.6 %all_to_all.20 = f16[32,8,384]{2,1,0:T(8,128)(2,1)S(1)} all-to-all(f16[32,8,384]{2,1,0:T(8,128)(2,1)S(1)} %fusion), channel_id=1, replica_groups=mesh['y'=8,'xh'=2,'xl'=2,'z'=16,'c'=2] {'y','xh','xl'}, dimensions={0} | all-to-all | bytes 393216 | tf_op jit(solution)/shard_map/all_to_all | solution.py:190
  31.4 0.6 broadcast_in_dim.3
  32.1 0.0 copy-start
  32.1 12.6 %all-to-all-start.2 = ((f16[16,8,384]{2,1,0:T(8,128)(2,1)}), f16[16,8,384]{2,1,0:T(8,128)(2,1)S(1)}, u32[]{:S(2)}, u32[]{:S(2)}) async-start(f16[16,8,384]{2,1,0:T(8,128)(2,1)} %broadcast_in_dim.3), calls=%async_computation.2 | async-start | bytes 196608 | tf_op jit(solution)/shard_map/all_to_all | solution.py:190
  44.7 0.0 copy-done.1
  44.7 0.0 copy-done
  44.8 2.2 %pack.1 = (bf16[1024,512]{1,0:T(8,128)(2,1)}, s32[1,512]{1,0:T(1,128)S(1)}) custom-call(s32[1,512]{1,0:T(1,128)S(1)} %bitcast.14, bf16[512,512]{1,0:T(8,128)(2,1)S(1)} %copy-done.1), custom_call_target="tpu_custom_call" | custom-call | flops 536870912 | bytes 2097152 | tf_op jit(solution)/shard_map/pack/pallas_call | solution.py:211
  46.9 9.7 %all-to-all-done.2 = f16[16,8,384]{2,1,0:T(8,128)(2,1)S(1)} async-done(((f16[16,8,384]{2,1,0:T(8,128)(2,1)}), f16[16,8,384]{2,1,0:T(8,128)(2,1)S(1)}, u32[]{:S(2)}, u32[]{:S(2)}) %all-to-all-start.2) | async-done | bytes 98336 | tf_op jit(solution)/shard_map/all_to_all | solution.py:190
  56.6 7.5 %all-to-all-start = ((bf16[64,16,512]{2,1,0:T(8,128)(2,1)}), bf16[64,16,512]{2,1,0:T(8,128)(2,1)S(1)}, u32[]{:S(2)}, u32[]{:S(2)}) async-start(bf16[64,16,512]{2,1,0:T(8,128)(2,1)} %bitcast.1), calls=%async_computation | async-start | bytes 2097152 | tf_op jit(solution)/shard_map/all_to_all | solution.py:190
  64.2 3.0 %collective-permute-start = (f32[8,384]{1,0:T(8,128)S(1)}, f32[8,384]{1,0:T(8,128)S(1)}, u32[]{:S(2)}, u32[]{:S(2)}) collective-permute-start(f32[8,384]{1,0:T(8,128)S(1)} %get-tuple-element.19), channel_id=1, source_target_pairs={{0,512},{128,640},{256,768},{384,896},{512,0},{640,128},{768,256},... | collective-permute-start | bytes 36872 | tf_op jit(solution)/shard_map/ppermute | solution.py:226
  67.2 5.6 %collective-permute-done = f32[8,384]{1,0:T(8,128)S(1)} collective-permute-done((f32[8,384]{1,0:T(8,128)S(1)}, f32[8,384]{1,0:T(8,128)S(1)}, u32[]{:S(2)}, u32[]{:S(2)}) %collective-permute-start) | collective-permute-done | bytes 12320 | tf_op jit(solution)/shard_map/ppermute | solution.py:226
  72.8 2.9 %collective-permute-start.1 = (f32[16,384]{1,0:T(8,128)S(1)}, f32[16,384]{1,0:T(8,128)S(1)}, u32[]{:S(2)}, u32[]{:S(2)}) collective-permute-start(f32[16,384]{1,0:T(8,128)S(1)} %pad_maximum_fusion.2), channel_id=1, source_target_pairs={{0,256},{128,384},{256,0},{384,128},{512,768},{640,896},{768,512},... | collective-permute-start | bytes 73736 | tf_op jit(solution)/shard_map/ppermute | solution.py:226
  75.7 2.8 %collective-permute-done.1 = f32[16,384]{1,0:T(8,128)S(1)} collective-permute-done((f32[16,384]{1,0:T(8,128)S(1)}, f32[16,384]{1,0:T(8,128)S(1)}, u32[]{:S(2)}, u32[]{:S(2)}) %collective-permute-start.1) | collective-permute-done | bytes 24608 | tf_op jit(solution)/shard_map/ppermute | solution.py:226
  78.6 2.7 %collective-permute-start.2 = (f32[32,384]{1,0:T(8,128)S(1)}, f32[32,384]{1,0:T(8,128)S(1)}, u32[]{:S(2)}, u32[]{:S(2)}) collective-permute-start(f32[32,384]{1,0:T(8,128)S(1)} %pad_maximum_fusion.1), channel_id=1, source_target_pairs={{0,128},{128,0},{256,384},{384,256},{512,640},{640,512},{768,896},... | collective-permute-start | bytes 147464 | tf_op jit(solution)/shard_map/ppermute | solution.py:226
  81.3 2.4 %collective-permute-done.2 = f32[32,384]{1,0:T(8,128)S(1)} collective-permute-done((f32[32,384]{1,0:T(8,128)S(1)}, f32[32,384]{1,0:T(8,128)S(1)}, u32[]{:S(2)}, u32[]{:S(2)}) %collective-permute-start.2) | collective-permute-done | bytes 49184 | tf_op jit(solution)/shard_map/ppermute | solution.py:226
  83.7 4.0 %collective-permute-start.3 = (f32[64,384]{1,0:T(8,128)S(1)}, f32[64,384]{1,0:T(8,128)S(1)}, u32[]{:S(2)}, u32[]{:S(2)}) collective-permute-start(f32[64,384]{1,0:T(8,128)S(1)} %pad_maximum_fusion), channel_id=1, source_target_pairs={{0,96},{32,64},{64,32},{96,0},{1,97},{33,65},{65,33},{97,1},{2,98}... | collective-permute-start | bytes 294920 | tf_op jit(solution)/shard_map/ppermute | solution.py:226
  87.7 2.9 %collective-permute-done.3 = f32[64,384]{1,0:T(8,128)S(1)} collective-permute-done((f32[64,384]{1,0:T(8,128)S(1)}, f32[64,384]{1,0:T(8,128)S(1)}, u32[]{:S(2)}, u32[]{:S(2)}) %collective-permute-start.3) | collective-permute-done | bytes 98336 | tf_op jit(solution)/shard_map/ppermute | solution.py:226
  90.6 2.3 %collective-permute-start.4 = (f32[128,384]{1,0:T(8,128)S(1)}, f32[128,384]{1,0:T(8,128)S(1)}, u32[]{:S(2)}, u32[]{:S(2)}) collective-permute-start(f32[128,384]{1,0:T(8,128)S(1)} %get-tuple-element.9), channel_id=1, source_target_pairs={{0,32},{32,0},{1,33},{33,1},{2,34},{34,2},{3,35},{35,3},{4,36},{36... | collective-permute-start | bytes 589832 | tf_op jit(solution)/shard_map/ppermute | solution.py:226
  92.9 5.2 %collective-permute-done.4 = f32[128,384]{1,0:T(8,128)S(1)} collective-permute-done((f32[128,384]{1,0:T(8,128)S(1)}, f32[128,384]{1,0:T(8,128)S(1)}, u32[]{:S(2)}, u32[]{:S(2)}) %collective-permute-start.4) | collective-permute-done | bytes 196640 | tf_op jit(solution)/shard_map/ppermute | solution.py:226
  98.1 6.6 %all_gather.7.both_ref = f32[512,384]{1,0:T(8,128)S(1)} all-gather(f32[256,384]{1,0:T(8,128)S(1)} %constant_dynamic-update-slice_fusion.5), channel_id=1, replica_groups=mesh['y'=8,'xh'=2,'xl'=2,'z'=16,'c'=2] {'c'}, dimensions={0}, use_global_device_ids=true | all-gather | bytes 1179648 | tf_op jit(solution)/shard_map/all_gather | solution.py:228
  104.7 3.2 %root.1.whiten_ref = bf16[512,512]{1,0:T(8,128)(2,1)S(1)} custom-call(s32[1]{0:T(128)} %bitcast.3.me_ref, f32[512,384]{1,0:T(8,128)S(1)} %all_gather.7.both_ref), custom_call_target="tpu_custom_call" | custom-call | flops 2415919104 | bytes 2097152 | tf_op jit(solution)/shard_map/root/pallas_call | solution.py:229
  107.9 6.7 %all-to-all-done = bf16[64,16,512]{2,1,0:T(8,128)(2,1)S(1)} async-done(((bf16[64,16,512]{2,1,0:T(8,128)(2,1)}), bf16[64,16,512]{2,1,0:T(8,128)(2,1)S(1)}, u32[]{:S(2)}, u32[]{:S(2)}) %all-to-all-start) | async-done | bytes 1048608 | tf_op jit(solution)/shard_map/all_to_all | solution.py:190
  114.6 2.0 %best.1 = f32[64,16]{1,0:T(8,128)S(1)} custom-call(bf16[1024,512]{1,0:T(8,128)(2,1)S(1)} %bitcast.11, bf16[512,512]{1,0:T(8,128)(2,1)S(1)} %root.1.whiten_ref), custom_call_target="tpu_custom_call" | custom-call | flops 1610612736 | bytes 2097152 | tf_op jit(solution)/shard_map/best/pallas_call | solution.py:235
  116.6 22.7 %all_to_all.21 = f32[64,1,16]{2,1,0:T(1,128)S(1)} all-to-all(f32[64,1,16]{2,1,0:T(1,128)S(1)} %bitcast.13), channel_id=1, replica_groups=mesh['y'=8,'xh'=2,'xl'=2,'z'=16,'c'=2] {'xl','z','c'}, dimensions={0} | all-to-all | bytes 8192 | tf_op jit(solution)/shard_map/all_to_all | solution.py:190
  139.3 0.8 pick.1
  (12 shorter events, 0.1 us)
Async XLA Ops:
  17.8 27.0 %copy-start.1 = (bf16[512,512]{1,0:T(8,128)(2,1)S(1)}, bf16[512,512]{1,0:T(8,128)(2,1)}, u32[]{:S(2)}) copy-start(bf16[512,512]{1,0:T(8,128)(2,1)} %rows_ref.3) | copy-start | bytes 1572868
  32.1 12.7 %copy-start = (s32[512,1]{0,1:T(1,128)S(1)}, s32[512,1]{0,1:T(1,128)}, u32[]{:S(2)}) copy-start(s32[512,1]{0,1:T(1,128)} %param.3) | copy-start | bytes 6148
  32.1 24.5 %all-to-all-start.2 = ((f16[16,8,384]{2,1,0:T(8,128)(2,1)}), f16[16,8,384]{2,1,0:T(8,128)(2,1)S(1)}, u32[]{:S(2)}, u32[]{:S(2)}) async-start(f16[16,8,384]{2,1,0:T(8,128)(2,1)} %broadcast_in_dim.3), calls=%async_computation.2 | async-start | bytes 196608 | tf_op jit(solution)/shard_map/all_to_all | solution.py:190
  56.6 58.0 %all-to-all-start = ((bf16[64,16,512]{2,1,0:T(8,128)(2,1)}), bf16[64,16,512]{2,1,0:T(8,128)(2,1)S(1)}, u32[]{:S(2)}, u32[]{:S(2)}) async-start(bf16[64,16,512]{2,1,0:T(8,128)(2,1)} %bitcast.1), calls=%async_computation | async-start | bytes 2097152 | tf_op jit(solution)/shard_map/all_to_all | solution.py:190
  64.2 8.6 %collective-permute-start = (f32[8,384]{1,0:T(8,128)S(1)}, f32[8,384]{1,0:T(8,128)S(1)}, u32[]{:S(2)}, u32[]{:S(2)}) collective-permute-start(f32[8,384]{1,0:T(8,128)S(1)} %get-tuple-element.19), channel_id=1, source_target_pairs={{0,512},{128,640},{256,768},{384,896},{512,0},{640,128},{768,256},... | collective-permute-start | bytes 36872 | tf_op jit(solution)/shard_map/ppermute | solution.py:226
  72.8 5.8 %collective-permute-start.1 = (f32[16,384]{1,0:T(8,128)S(1)}, f32[16,384]{1,0:T(8,128)S(1)}, u32[]{:S(2)}, u32[]{:S(2)}) collective-permute-start(f32[16,384]{1,0:T(8,128)S(1)} %pad_maximum_fusion.2), channel_id=1, source_target_pairs={{0,256},{128,384},{256,0},{384,128},{512,768},{640,896},{768,512},... | collective-permute-start | bytes 73736 | tf_op jit(solution)/shard_map/ppermute | solution.py:226
  78.6 5.1 %collective-permute-start.2 = (f32[32,384]{1,0:T(8,128)S(1)}, f32[32,384]{1,0:T(8,128)S(1)}, u32[]{:S(2)}, u32[]{:S(2)}) collective-permute-start(f32[32,384]{1,0:T(8,128)S(1)} %pad_maximum_fusion.1), channel_id=1, source_target_pairs={{0,128},{128,0},{256,384},{384,256},{512,640},{640,512},{768,896},... | collective-permute-start | bytes 147464 | tf_op jit(solution)/shard_map/ppermute | solution.py:226
  83.7 6.9 %collective-permute-start.3 = (f32[64,384]{1,0:T(8,128)S(1)}, f32[64,384]{1,0:T(8,128)S(1)}, u32[]{:S(2)}, u32[]{:S(2)}) collective-permute-start(f32[64,384]{1,0:T(8,128)S(1)} %pad_maximum_fusion), channel_id=1, source_target_pairs={{0,96},{32,64},{64,32},{96,0},{1,97},{33,65},{65,33},{97,1},{2,98}... | collective-permute-start | bytes 294920 | tf_op jit(solution)/shard_map/ppermute | solution.py:226
  90.6 7.5 %collective-permute-start.4 = (f32[128,384]{1,0:T(8,128)S(1)}, f32[128,384]{1,0:T(8,128)S(1)}, u32[]{:S(2)}, u32[]{:S(2)}) collective-permute-start(f32[128,384]{1,0:T(8,128)S(1)} %get-tuple-element.9), channel_id=1, source_target_pairs={{0,32},{32,0},{1,33},{33,1},{2,34},{34,2},{3,35},{35,3},{4,36},{36... | collective-permute-start | bytes 589832 | tf_op jit(solution)/shard_map/ppermute | solution.py:226
